TPU v7x, 128 devices: a whole 4x4x4 slice. The times are simulated.
128 devices in a mesh: frame: 8 (over x_hi, z), pos: 16 (over y, x_lo, core).
Axes of the slice: x: 4 (x_hi: 2, x_lo: 2; x = x_hi * 2 + x_lo), y: 4, z: 4, core: 2. Of those that a mesh axis runs over, the one named last changes fastest.
Arguments:
- latents: bfloat16 [256, 1024, 256], P('frame', 'pos'), as said below
- gain_one: float32 [256], replicated, may hold values from 0.5 to 1.5
- query_one: bfloat16 [256, 256], replicated, as said below
- key_one: bfloat16 [256, 256], replicated, as said below
- value_one: bfloat16 [256, 256], replicated, may hold values from -0.375 to 0.375
- out_one: bfloat16 [256, 256], replicated, may hold values from -0.75 to 0.75
- gain_two: float32 [256], replicated, may hold values from 0.5 to 1.5
- query_two: bfloat16 [256, 256], replicated, as said below
- key_two: bfloat16 [256, 256], replicated, as said below
- value_two: bfloat16 [256, 256], replicated, may hold values from -0.375 to 0.375
- out_two: bfloat16 [256, 256], replicated, may hold values from -0.75 to 0.75
Outputs:
- decoded: bfloat16 [256, 1024, 256], P('frame', 'pos')
Inputs may be any that keep to these rules, and one draw needn't show every extreme that they name: `latents`: latent features of the video. `query_one`: A projection of the spatial block. `key_one`: A projection of the spatial block. `query_two`: A projection of the temporal block. `key_two`: A projection of the temporal block.
All inputs are finite; a program needn't handle non-finite values.
Results may differ from a plain program's by a relative error of at most 0.015.
The roundings to bfloat16 on the way count: a program that leaves them out, or rounds other values in their place, can miss the bound.
Values may be sent and summed in bfloat16 or wider, within the bound.
A program may use at most 320 MiB of HBM per device.

v0:
```python
import jax
import jax.numpy as jnp
from jax import lax
from jax.sharding import PartitionSpec as P

HEADS = 4


def broadcast(value, axis, source):
    kept = jnp.where(lax.axis_index(axis) == source, value, 0).astype(value.dtype)
    return lax.psum(kept, axis)


def normed(values, gain):
    wide = values.astype(jnp.float32)
    factor = lax.rsqrt(jnp.mean(wide * wide, axis=-1, keepdims=True) + 1e-06)
    return (wide * factor * gain).astype(jnp.bfloat16)


def project(values, weight):
    flat = values.reshape(-1, values.shape[-1])
    result = jnp.dot(flat, weight, preferred_element_type=jnp.float32).astype(jnp.bfloat16)
    return result.reshape(values.shape[:-1] + (weight.shape[1],))


def heads_of(values):
    return values.reshape(values.shape[:-1] + (HEADS, values.shape[-1] // HEADS))


def soft_step(carry, query, keys, vals, score_form, value_form):
    highest, totals, summed = carry
    scale = query.shape[-1] ** (-0.5)
    scores = jnp.einsum(score_form, query, keys, preferred_element_type=jnp.float32) * scale
    new_high = jnp.maximum(highest, jnp.max(scores, axis=-1))
    keep = jnp.exp(highest - new_high)
    weights = jnp.exp(scores - new_high[..., None])
    totals = totals * keep + jnp.sum(weights, axis=-1)
    summed = summed * keep[..., None] + jnp.einsum(
        value_form, weights.astype(jnp.bfloat16), vals, preferred_element_type=jnp.float32
    )
    return (new_high, totals, summed)


def empty_carry(lead, depth):
    return (
        jnp.full(lead, -1e30, jnp.float32),
        jnp.zeros(lead, jnp.float32),
        jnp.zeros(lead + (depth,), jnp.float32),
    )


def shards(
    latents,
    gain_one,
    query_one,
    key_one,
    value_one,
    out_one,
    gain_two,
    query_two,
    key_two,
    value_two,
    out_two,
):
    frames, places, width = latents.shape
    depth = width // HEADS
    normed_one = normed(latents, gain_one)
    q_one = heads_of(project(normed_one, query_one))
    k_one = project(normed_one, key_one)
    v_one = project(normed_one, value_one)
    first_keys, first_vals = (k_one[0], v_one[0])
    first_keys, first_vals = (broadcast(first_keys, "frame", 0), broadcast(first_vals, "frame", 0))
    first_keys, first_vals = (
        lax.all_gather(first_keys, "pos", axis=0, tiled=True),
        lax.all_gather(first_vals, "pos", axis=0, tiled=True),
    )
    carry = empty_carry((frames, HEADS, places), depth)
    carry = soft_step(
        carry, q_one, heads_of(first_keys), heads_of(first_vals), "fphd,khd->fhpk", "fhpk,khd->fhpd"
    )
    pieces = (
        lax.all_gather(k_one, "pos", axis=1, tiled=True),
        lax.all_gather(v_one, "pos", axis=1, tiled=True),
    )
    carry = soft_step(
        carry, q_one, heads_of(pieces[0]), heads_of(pieces[1]), "fphd,fkhd->fhpk", "fhpk,fkhd->fhpd"
    )
    attended_one = (
        (carry[2] / carry[1][..., None])
        .transpose(0, 2, 1, 3)
        .reshape(frames, places, width)
        .astype(jnp.bfloat16)
    )
    mixed_one = jnp.dot(
        attended_one.reshape(-1, width), out_one, preferred_element_type=jnp.float32
    ).reshape(frames, places, width)
    middle = (latents.astype(jnp.float32) + mixed_one).astype(jnp.bfloat16)
    normed_two = normed(middle, gain_two)
    q_two = heads_of(project(normed_two, query_two))
    carry_two = empty_carry((places, HEADS, frames), depth)
    k_two = project(normed_two, key_two)
    v_two = project(normed_two, value_two)
    pieces = (
        lax.all_gather(k_two, "frame", axis=0, tiled=True),
        lax.all_gather(v_two, "frame", axis=0, tiled=True),
    )
    carry_two = soft_step(
        carry_two,
        q_two,
        heads_of(pieces[0]),
        heads_of(pieces[1]),
        "fphd,kphd->phfk",
        "phfk,kphd->phfd",
    )
    attended_two = (
        (carry_two[2] / carry_two[1][..., None])
        .transpose(2, 0, 1, 3)
        .reshape(frames, places, width)
        .astype(jnp.bfloat16)
    )
    mixed_two = jnp.dot(
        attended_two.reshape(-1, width), out_two, preferred_element_type=jnp.float32
    ).reshape(frames, places, width)
    return (middle.astype(jnp.float32) + mixed_two).astype(jnp.bfloat16)


def solution(mesh):
    return jax.shard_map(
        shards,
        mesh=mesh,
        in_specs=(P("frame", "pos", None), P(), P(), P(), P(), P(), P(), P(), P(), P(), P()),
        out_specs=P("frame", "pos", None),
        check_vma=False,
    )
```

profile of v0, /device:TPU:1, one launch (start us, length us, event | category | flops | bytes accessed | tf_op | source)
XLA Modules:
  0.0 649.6 jit_solution(16036912624553404310)
XLA Ops:
  7.4 1.6 fusion.27
  9.0 1.6 fusion.29
  14.6 1.6 copy.78
  17.6 1.9 copy.71
  19.5 174.5 %all-reduce.3.cloned.1.call-done = (bf16[64,256]{1,0:T(8,128)(2,1)}, bf16[64,256]{1,0:T(8,128)(2,1)}) async-done(((bf16[64,256]{1,0:T(8,128)(2,1)}, bf16[64,256]{1,0:T(8,128)(2,1)}), (bf16[64,256]{1,0:T(8,128)(2,1)}, bf16[64,256]{1,0:T(8,128)(2,1)})) %all-reduce.3.cloned.1.call-update) | async-done | bytes 65552 | tf_op jit(solution)/shard_map/psum | solution.py:11
  194.0 30.8 %all_gather.18 = bf16[1024,256]{1,0:T(8,128)(2,1)S(1)} all-gather(bf16[64,256]{1,0:T(8,128)(2,1)} %get-tuple-element.6), channel_id=1, replica_groups=mesh['frame'=8,'pos'=16] {'pos'}, dimensions={0}, use_global_device_ids=true | all-gather | bytes 557056 | tf_op jit(solution)/shard_map/all_gather | solution.py:74
  225.0 20.4 %all_gather.19 = bf16[1024,256]{1,0:T(8,128)(2,1)} all-gather(bf16[64,256]{1,0:T(8,128)(2,1)} %get-tuple-element.5), channel_id=1, replica_groups=mesh['frame'=8,'pos'=16] {'pos'}, dimensions={0}, use_global_device_ids=true | all-gather | bytes 557056 | tf_op jit(solution)/shard_map/all_gather | solution.py:75
  246.6 14.7 %fusion.50 = f32[4,1024,2048]{1,2,0} fusion(bf16[4,64,2048]{1,2,0:T(8,128)(2,1)} %bitcast.115, bf16[1024,4,64]{0,2,1:T(8,128)(2,1)S(1)} %bitcast.122), kind=kOutput, calls=%fused_computation.75 | convolution fusion | flops 1073741824 | bytes 35127296
  261.3 12.1 %bitcast_reduce_fusion = f32[32,4,64]{2,0,1:T(8,128)S(1)} fusion(f32[4,1024,32,64]{1,3,2,0:T(8,128)} %bitcast.103), kind=kLoop, calls=%fused_computation.1 | loop fusion | flops 16769024 | bytes 33587200 | tf_op jit(solution)/shard_map/reduce_max | solution.py:34
  273.5 22.5 %copy.73 = bf16[32,1024,256]{1,2,0:T(8,128)(2,1)} copy(bf16[32,1024,256]{2,1,0:T(8,128)(2,1)} %all-gather.5.cloned.1.call-done) | data formatting | bytes 33554432 | tf_op jit(solution)/shard_map/all_gather | solution.py:82
  296.1 16.5 %multiply_reduce_fusion = (f32[32,4,64]{2,1,0:T(4,128)S(1)}, f32[32,4,64,1024]{3,2,1,0:T(8,128)}) fusion(bf16[32,1024,4,64]{1,3,2,0:T(8,128)(2,1)} %bitcast.106, bf16[32,64,4,64]{3,2,1,0:T(4,128)(2,1)S(1)} %reshape_reshape.6), kind=kOutput, calls=%fused_computation.4 | convolution fusion | flops 1090510848 | bytes 51412992 | tf_op jit(solution)/shard_map/fphd,fkhd->fhpk/dot_general | solution.py:33
  312.6 14.8 %fusion.3 = f32[32,4,64]{2,0,1:T(8,128)S(1)} fusion(f32[4,1024,32,64]{1,3,2,0:T(8,128)} %bitcast.104, f32[32,4,64]{2,0,1:T(8,128)S(1)} %get-tuple-element.15), kind=kLoop, calls=%fused_computation.7 | loop fusion | flops 25157632 | bytes 33619968 | tf_op jit(solution)/shard_map/reduce_sum | solution.py:37
  327.4 5.3 copy-done.1
  332.7 9.8 %fusion.1 = (f32[32,4,64]{2,1,0:T(4,128)S(1)}, bf16[32,4,64,1024]{3,2,1,0:T(8,128)(2,1)}) fusion(f32[32,4,64,1024]{3,2,1,0:T(8,128)S(1)} %copy-done.1, f32[32,4,64]{2,1,0:T(4,128)S(1)} %copy.77), kind=kLoop, calls=%fused_computation.5 | loop fusion | flops 33546240 | bytes 50397184 | tf_op jit(solution)/shard_map/reduce_sum | solution.py:37
  342.6 16.1 %fusion.5 = f32[4,64,32,64]{3,1,2,0:T(8,128)} fusion(bf16[1024,4,64,1]{0,2,3,1:T(8,128)(2,1)S(1)} %bitcast.121, f32[4,1024,32,64]{1,3,2,0:T(8,128)} %bitcast.105, f32[32,4,64]{2,0,1:T(8,128)S(1)} %get-tuple-element.15), kind=kOutput, calls=%fused_computation.9 | convolution fusion | flops 1098907648 | bytes 36208640 | tf_op jit(solution)/shard_map/fhpk,khd->fhpd/dot_general | solution.py:38
  358.7 23.2 %copy.79 = bf16[32,1024,256]{1,2,0:T(8,128)(2,1)} copy(bf16[32,1024,256]{2,0,1:T(8,128)(2,1)} %all-gather.7.cloned.1.call-done) | data formatting | bytes 33554432 | tf_op jit(solution)/shard_map/all_gather | solution.py:83
  382.0 15.0 %fusion.19 = bf16[32,64,4,64]{1,3,0,2:T(8,128)(2,1)} fusion(f32[4,64,32,64]{3,1,2,0:T(8,128)} %fusion.5, bf16[32,1024,4,64]{1,3,2,0:T(8,128)(2,1)} %bitcast.108, bf16[32,4,64,1024]{3,2,1,0:T(8,128)(2,1)} %get-tuple-element.10, f32[32,64,4]{1,0,2:T(8,128)S(1)} %get-tuple-element.7, f32[32,64,4]{1,0,2:T(8,128)S(1)} %get-tuple-element.8, ...), kind=kOutput, calls=%fused_computation.25 | convolution fusion | flops 1076363264 | bytes 36798464 | tf_op jit(solution)/shard_map/fhpk,fkhd->fhpd/dot_general | solution.py:38
  397.0 3.1 copy.84
  400.1 2.2 convert_element_type.74
  402.3 1.8 fusion.31
  405.4 1.4 convolution_convert_fusion.1
  406.9 1.5 convolution_convert_fusion
  409.8 99.1 %all-gather.9.cloned.1.call-done = bf16[256,64,256]{2,1,0:T(8,128)(2,1)} async-done(((bf16[32,64,256]{2,1,0:T(8,128)(2,1)}), bf16[256,64,256]{2,1,0:T(8,128)(2,1)}) %all-gather.9.cloned.1.call-update) | async-done | bytes 8388624 | tf_op jit(solution)/shard_map/all_gather | solution.py:104
  508.8 13.0 %copy.85 = bf16[256,64,256]{0,2,1:T(8,128)(2,1)} copy(bf16[256,64,256]{2,1,0:T(8,128)(2,1)} %all-gather.9.cloned.1.call-done) | data formatting | bytes 16777216 | tf_op jit(solution)/shard_map/all_gather | solution.py:104
  521.8 5.7 multiply_reduce_fusion.1
  527.6 3.1 copy-done.2
  530.7 2.8 fusion.12
  533.6 82.9 %all-gather.11.cloned.1.call-done = bf16[256,64,256]{2,1,0:T(8,128)(2,1)} async-done(((bf16[32,64,256]{2,1,0:T(8,128)(2,1)}), bf16[256,64,256]{2,1,0:T(8,128)(2,1)}) %all-gather.11.cloned.1.call-update) | async-done | bytes 8388624 | tf_op jit(solution)/shard_map/all_gather | solution.py:105
  616.5 12.9 %copy.87 = bf16[256,64,256]{0,2,1:T(8,128)(2,1)} copy(bf16[256,64,256]{2,1,0:T(8,128)(2,1)} %all-gather.11.cloned.1.call-done) | data formatting | bytes 16777216 | tf_op jit(solution)/shard_map/all_gather | solution.py:105
  629.4 8.0 %fusion.17 = bf16[32,64,4,64]{3,0,2,1:T(8,128)(2,1)S(1)} fusion(f32[32,64,4]{0,2,1:T(4,128)S(1)} %bitcast_add_fusion.3, f32[32,64,4]{0,2,1:T(4,128)S(1)} %get-tuple-element.11, bf16[256,64,4,64]{0,3,2,1:T(8,128)(2,1)} %bitcast.116, f32[64,4,32,256]{3,2,1,0:T(8,128)} %copy-done.2, f32[64,4,32]{2,1,0:T(4,128)S(1)} %get-tuple-element.12), kind=kOutput, calls=%fused_computation.22 | convolution fusion | flops 276299776 | bytes 17924096 | tf_op jit(solution)/shard_map/phfk,kphd->phfd/dot_general | solution.py:38
  638.5 1.4 convert_element_type.83
  639.9 2.6 fusion.34
  (52 shorter events, 10.9 us)
Async XLA Ops:
  7.4 394.9 %copy-start = (bf16[256,256]{1,0:T(8,128)(2,1)S(1)}, bf16[256,256]{1,0:T(8,128)(2,1)}, u32[]{:S(2)}) copy-start(bf16[256,256]{1,0:T(8,128)(2,1)} %param.16) | copy-start | bytes 393220
  7.4 8.9 %copy-start.6 = (bf16[256,256]{1,0:T(8,128)(2,1)S(1)}, bf16[256,256]{1,0:T(8,128)(2,1)}, u32[]{:S(2)}) copy-start(bf16[256,256]{1,0:T(8,128)(2,1)} %param.13) | copy-start | bytes 393220
  7.4 186.6 %all-reduce.3.cloned.1.call-start = ((), (), s32[]{:S(2)}) async-start(), calls=%async_computation.4 | async-start | bytes 131072 | tf_op jit(solution)/shard_map/psum | solution.py:11
  13.3 1.0 copy-start.3
  14.0 259.5 %all-gather.5.cloned.1.call-start = ((), (), s32[]{:S(2)}) async-start(), calls=%async_computation | async-start | bytes 17825792 | tf_op jit(solution)/shard_map/all_gather | solution.py:82
  14.6 344.1 %all-gather.7.cloned.1.call-start = ((), (), s32[]{:S(2)}) async-start(), calls=%async_computation.1 | async-start | bytes 17825792 | tf_op jit(solution)/shard_map/all_gather | solution.py:83
  16.2 492.6 %all-gather.9.cloned.1.call-start = ((), (), s32[]{:S(2)}) async-start(), calls=%async_computation.2 | async-start | bytes 9437184 | tf_op jit(solution)/shard_map/all_gather | solution.py:104
  312.6 20.2 %copy-start.1 = (f32[32,4,64,1024]{3,2,1,0:T(8,128)S(1)}, f32[32,4,64,1024]{3,2,1,0:T(8,128)}, u32[]{:S(2)}) copy-start(f32[32,4,64,1024]{3,2,1,0:T(8,128)} %get-tuple-element.17) | copy-start | bytes 100663296
  382.0 20.3 %copy-start.5 = (bf16[32,64,256]{2,1,0:T(8,128)(2,1)S(1)}, bf16[32,64,256]{2,1,0:T(8,128)(2,1)}, u32[]{:S(2)}) copy-start(bf16[32,64,256]{2,1,0:T(8,128)(2,1)} %param.11) | copy-start | bytes 3145732
  397.0 8.1 %copy-start.11 = (f32[256]{0:T(256)S(1)}, f32[256]{0:T(256)}, u32[]{:S(2)}) copy-start(f32[256]{0:T(256)} %param.17) | copy-start | bytes 3076
  397.0 8.4 %copy-start.7 = (bf16[256,256]{1,0:T(8,128)(2,1)S(1)}, bf16[256,256]{1,0:T(8,128)(2,1)}, u32[]{:S(2)}) copy-start(bf16[256,256]{1,0:T(8,128)(2,1)} %param.19) | copy-start | bytes 393220
  397.0 9.9 %copy-start.8 = (bf16[256,256]{1,0:T(8,128)(2,1)S(1)}, bf16[256,256]{1,0:T(8,128)(2,1)}, u32[]{:S(2)}) copy-start(bf16[256,256]{1,0:T(8,128)(2,1)} %param.20) | copy-start | bytes 393220
  402.3 6.2 copy-start.9
  404.1 1.0 copy-start.4
  406.9 209.7 %all-gather.11.cloned.1.call-start = ((), (), s32[]{:S(2)}) async-start(), calls=%async_computation.3 | async-start | bytes 9437184 | tf_op jit(solution)/shard_map/all_gather | solution.py:105
  527.5 3.2 copy-start.2
  629.4 10.5 %copy-start.10 = (bf16[256,256]{1,0:T(8,128)(2,1)S(1)}, bf16[256,256]{1,0:T(8,128)(2,1)}, u32[]{:S(2)}) copy-start(bf16[256,256]{1,0:T(8,128)(2,1)} %param.21) | copy-start | bytes 393220
Sparse Core Ops, SparseCore 0:
  14.1 179.8 all-reduce.2
  407.0 101.8 all-gather.8
  511.5 105.0 all-gather.10
Sparse Core Ops, SparseCore 1:
  16.2 95.5 all-gather.4
  113.5 94.1 all-gather.6
where the time goes:
time: 652 us; the launch traced here: 650 us
  waiting for transfers between devices  357 us (55%)
  local copies, waits for them, and re-layouts  95.6 us (15%)
  matrix products  86.9 us (13%)
  blocking collectives  51.2 us (8%)
  other arithmetic  44 us (7%)
  between operations  14.9 us (2%)
    psum x1, waiting for transfers between devices, broadcast(): return lax.psum(kept, axis)  175 us
    all_gather x1, waiting for transfers between devices, shards(): lax.all_gather(k_two, 'frame', axis=0, tiled=True)  99.1 us
    all_gather x1, waiting for transfers between devices, shards(): lax.all_gather(v_two, 'frame', axis=0, tiled=True)  82.9 us
    dot_general x3, matrix products, soft_step(): jnp.einsum(value_form, weights.astype(jnp.bfloat16), vals, preferred_elem...  39.1 us
    all_gather x1, blocking collectives, shards(): lax.all_gather(first_keys, 'pos', axis=0, tiled=True)  30.8 us
    reduce_sum x3, other arithmetic, soft_step(): totals = totals * keep + jnp.sum(weights, axis=-1)  27.4 us
    all_gather x1, local copies, waits for them, and re-layouts, shards(): lax.all_gather(v_one, 'pos', axis=1, tiled=True)  23.2 us
    all_gather x1, local copies, waits for them, and re-layouts, shards(): lax.all_gather(k_one, 'pos', axis=1, tiled=True)  22.5 us
  transfers between devices with their start and end apart: 5, of which 3 were waited for; matrix products, arithmetic and copies ran while one was open for 21% of the time, Pallas kernels for 0%

commit v1 on v0

v1 whole, which is shorter than its diff:
```python
import jax
import jax.numpy as jnp
from jax import lax
from jax.sharding import PartitionSpec as P

HEADS = 4


def normed(values, gain):
    wide = values.astype(jnp.float32)
    factor = lax.rsqrt(jnp.mean(wide * wide, axis=-1, keepdims=True) + 1e-06)
    return (wide * factor * gain).astype(jnp.bfloat16)


def project(values, weight):
    flat = values.reshape(-1, values.shape[-1])
    result = jnp.dot(flat, weight, preferred_element_type=jnp.float32).astype(jnp.bfloat16)
    return result.reshape(values.shape[:-1] + (weight.shape[1],))


def heads_of(values):
    return values.reshape(values.shape[:-1] + (HEADS, values.shape[-1] // HEADS))


def softmax_attend(query, keys, vals, score_form, value_form, total_form):
    scale = query.shape[-1] ** (-0.5)
    scores = jnp.einsum(score_form, query, keys, preferred_element_type=jnp.float32) * scale
    weights = jnp.exp(scores - jnp.max(scores, axis=-1, keepdims=True))
    totals = jnp.sum(weights, axis=-1)
    summed = jnp.einsum(
        value_form, weights.astype(jnp.bfloat16), vals, preferred_element_type=jnp.float32
    )
    return summed / jnp.einsum(total_form, totals)[..., None]


def shards(
    latents,
    gain_one,
    query_one,
    key_one,
    value_one,
    out_one,
    gain_two,
    query_two,
    key_two,
    value_two,
    out_two,
):
    frames, places, width = latents.shape
    n_pos = lax.axis_size("pos")
    n_frame = lax.axis_size("frame")
    per = frames // n_pos
    first = jnp.where(lax.axis_index("frame") == 0, latents[0], 0).astype(latents.dtype)
    first = lax.psum(first, "frame")
    sent = jnp.concatenate(
        [
            latents.reshape(n_pos, per, places, width),
            jnp.broadcast_to(first[None, None], (n_pos, 1, places, width)),
        ],
        axis=1,
    )
    got = lax.all_to_all(sent, "pos", 0, 0, tiled=True)
    xs = got[:, :per].transpose(1, 0, 2, 3).reshape(per, n_pos * places, width)
    x0 = got[:, per].reshape(n_pos * places, width)

    n_one = normed(xs, gain_one)
    q_one = heads_of(project(n_one, query_one))
    k_one = heads_of(project(n_one, key_one))
    v_one = heads_of(project(n_one, value_one))
    n_zero = normed(x0, gain_one)
    k_zero = heads_of(project(n_zero, key_one))
    v_zero = heads_of(project(n_zero, value_one))
    keys = jnp.concatenate([k_one, jnp.broadcast_to(k_zero[None], k_one.shape)], axis=1)
    vals = jnp.concatenate([v_one, jnp.broadcast_to(v_zero[None], v_one.shape)], axis=1)
    attended_one = softmax_attend(
        q_one, keys, vals, "fphd,fkhd->fhpk", "fhpk,fkhd->fphd", "fhp->fph"
    ).reshape(xs.shape).astype(jnp.bfloat16)
    mixed_one = jnp.dot(
        attended_one.reshape(-1, width), out_one, preferred_element_type=jnp.float32
    ).reshape(xs.shape)
    middle = (xs.astype(jnp.float32) + mixed_one).astype(jnp.bfloat16)

    all_places = n_pos * places
    run = all_places // (n_pos * n_frame)
    sent = (
        middle.reshape(per, n_pos, n_frame, run, width)
        .transpose(2, 1, 0, 3, 4)
        .reshape(n_frame * n_pos, per, run, width)
    )
    got = lax.all_to_all(sent, ("frame", "pos"), 0, 0, tiled=True)
    mid_t = got.reshape(n_frame * n_pos * per, run, width)

    n_two = normed(mid_t, gain_two)
    q_two = heads_of(project(n_two, query_two))
    k_two = heads_of(project(n_two, key_two))
    v_two = heads_of(project(n_two, value_two))
    attended_two = softmax_attend(
        q_two, k_two, v_two, "fphd,kphd->phfk", "phfk,kphd->fphd", "phf->fph"
    ).reshape(mid_t.shape).astype(jnp.bfloat16)
    mixed_two = jnp.dot(
        attended_two.reshape(-1, width), out_two, preferred_element_type=jnp.float32
    ).reshape(mid_t.shape)
    decoded = (mid_t.astype(jnp.float32) + mixed_two).astype(jnp.bfloat16)

    sent = decoded.reshape(n_frame, frames, run, width)
    got = lax.all_to_all(sent, "frame", 0, 0, tiled=True)
    return got.transpose(1, 0, 2, 3).reshape(frames, places, width)


def solution(mesh):
    return jax.shard_map(
        shards,
        mesh=mesh,
        in_specs=(P("frame", "pos", None), P(), P(), P(), P(), P(), P(), P(), P(), P(), P()),
        out_specs=P("frame", "pos", None),
        check_vma=False,
    )
```

time: 652 us -> 244 us (0.37)
  waiting for transfers between devices: 357 us -> 0 us
  local copies, waits for them, and re-layouts: 95.6 us -> 34.1 us
  blocking collectives: 51.2 us -> 111 us
  matrix products: 86.9 us -> 66.5 us
  between operations: 14.9 us -> 0.27 us
  other arithmetic: 44 us -> 29.8 us
    all_gather x4 -> x0, waiting for transfers between devices: 182 us -> none  [the longest x1 99.1 us: shards(): lax.all_gather(k_two, 'frame', axis=0, tiled=True)]
    psum x1 -> x0, waiting for transfers between devices: 175 us -> none  [broadcast(): return lax.psum(kept, axis)]
    all_to_all x0 -> x3, blocking collectives: none -> 74.6 us  [the longest x1 33.2 us: shards(): got = lax.all_to_all(sent, 'pos', 0, 0, tiled=True)]
    all_gather x6 -> x0, local copies, waits for them, and re-layouts: 73.1 us -> none  [the longest x1 23.2 us: shards(): lax.all_gather(v_one, 'pos', axis=1, tiled=True)]
    all_gather x2 -> x0, blocking collectives: 51.2 us -> none  [the longest x1 30.8 us: shards(): lax.all_gather(first_keys, 'pos', axis=0, tiled=True)]
    psum x0 -> x1, blocking collectives: none -> 36.7 us  [shards(): first = lax.psum(first, 'frame')]
    another operation x3 -> x8, local copies, waits for them, and re-layouts: 3.6 us -> 27.4 us  [heads_of(): values.reshape(values.shape[:-1] + (HEADS, values.shape[-1] // HEADS))]
    unnamed x1 -> x0, matrix products: 14.7 us -> none
  transfers between devices with their start and end apart: 5 -> 0, of which waited for: 3 -> 0; matrix products, arithmetic and copies ran while one was open for 21% -> 0% of each run, Pallas kernels for 0% -> 0%
where the time goes in v1:
time: 244 us; the launch traced here: 242 us
  blocking collectives  111 us (45%)
  matrix products  66.5 us (27%)
  local copies, waits for them, and re-layouts  34.1 us (14%)
  other arithmetic  29.8 us (12%)
    psum x1, blocking collectives, shards(): first = lax.psum(first, 'frame')  36.7 us
    all_to_all x1, blocking collectives, shards(): got = lax.all_to_all(sent, 'pos', 0, 0, tiled=True)  33.2 us
    dot_general x2, matrix products, softmax_attend(): jnp.einsum(score_form, query, keys, preferred_element_type=jnp.float32)  28.3 us
    another operation x8, local copies, waits for them, and re-layouts, heads_of(): values.reshape(values.shape[:-1] + (HEADS, values.shape[-1] // HEADS))  27.4 us
    dot_general x2, matrix products, softmax_attend(): jnp.einsum(value_form, weights.astype(jnp.bfloat16), vals, preferred_elem...  26.9 us
    all_to_all x1, blocking collectives, shards(): got = lax.all_to_all(sent, ('frame', 'pos'), 0, 0, tiled=True)  23.2 us
    reduce_sum x2, other arithmetic, softmax_attend(): totals = jnp.sum(weights, axis=-1)  22.8 us
    all_to_all x1, blocking collectives, shards(): got = lax.all_to_all(sent, 'frame', 0, 0, tiled=True)  18.2 us

profile of v1, /device:TPU:1, one launch (start us, length us, event | category | flops | bytes accessed | tf_op | source)
XLA Modules:
  0.0 242.0 jit_solution(5843305531094082782)
XLA Ops:
  0.8 36.7 %psum.7 = bf16[64,256]{1,0:T(8,128)(2,1)S(1)} all-reduce(bf16[64,256]{1,0:T(8,128)(2,1)S(1)} %select_bitcast_fusion), channel_id=1, replica_groups=mesh['frame'=8,'pos'=16] {'frame'}, use_global_device_ids=true, to_apply=%region_0.1 | all-reduce | flops 16384 | bytes 65536 | tf_op jit(solution)/shard_map/psum | solution.py:54
  37.5 1.4 pad_maximum_fusion
  38.9 33.2 %all_to_all.15 = bf16[16,3,64,256]{3,2,1,0:T(8,128)(2,1)S(1)} all-to-all(bf16[16,3,64,256]{3,2,1,0:T(8,128)(2,1)S(1)} %pad_maximum_fusion), channel_id=1, replica_groups=mesh['frame'=8,'pos'=16] {'pos'}, dimensions={0} | all-to-all | bytes 3145728 | tf_op jit(solution)/shard_map/all_to_all | solution.py:62
  73.3 1.5 copy_convert_fusion
  75.2 1.4 convolution_convert_fusion.3
  76.6 1.2 slice_convert_fusion
  78.0 1.1 convolution_convert_fusion.6
  79.1 1.4 convolution_convert_fusion.5
  80.5 1.1 convolution_convert_fusion.7
  81.7 4.5 %reshape.135 = bf16[2,1024,4,64]{3,2,1,0:T(4,128)(2,1)} reshape(bf16[2048,256]{1,0:T(8,128)(2,1)} %convolution_convert_fusion.3) | data formatting | bytes 2097152 | tf_op jit(solution)/shard_map/reshape;reshape | solution.py:22
  86.1 4.1 %copy.61 = bf16[2,1024,4,64]{1,3,2,0:T(8,128)(2,1)} copy(bf16[2,1024,4,64]{3,2,1,0:T(4,128)(2,1)} %reshape.135) | data formatting | bytes 2097152 | tf_op jit(solution)/shard_map/reshape;reshape | solution.py:22
  90.2 1.4 convolution_convert_fusion.4
  91.6 4.5 %reshape.134 = bf16[2,1024,4,64]{3,2,1,0:T(4,128)(2,1)} reshape(bf16[2048,256]{1,0:T(8,128)(2,1)} %convolution_convert_fusion.4) | data formatting | bytes 2097152 | tf_op jit(solution)/shard_map/reshape;reshape | solution.py:22
  96.1 1.9 reshape.133
  98.0 4.2 %copy.58 = bf16[2,1024,4,64]{1,3,2,0:T(8,128)(2,1)} copy(bf16[2,1024,4,64]{3,2,1,0:T(4,128)(2,1)} %reshape.133) | data formatting | bytes 2097152 | tf_op jit(solution)/shard_map/reshape;reshape | solution.py:22
  102.2 1.2 broadcast_in_dim.19
  103.3 24.7 %multiply_reduce_fusion = (f32[2,4,1024]{2,1,0:T(4,128)S(1)}, f32[2,4,1024,2048]{3,2,1,0:T(8,128)}) fusion(bf16[2,1024,4,64]{1,3,2,0:T(8,128)(2,1)S(1)} %broadcast_in_dim.19, bf16[2,1024,4,64]{1,3,2,0:T(8,128)(2,1)S(1)} %copy-done.3, bf16[2,1024,4,64]{3,2,1,0:T(4,128)(2,1)} %reshape.134), kind=kOutput, calls=%fused_computation.1 | convolution fusion | flops 2185224192 | bytes 70287360 | tf_op jit(solution)/shard_map/fphd,fkhd->fhpk/dot_general | solution.py:27
  128.1 21.2 %fusion = f32[2,4,1024]{2,1,0:T(4,128)S(1)} fusion(f32[2,4,1024,2048]{3,2,1,0:T(8,128)} %get-tuple-element.6, f32[2,4,1024]{2,1,0:T(4,128)S(1)} %get-tuple-element.5), kind=kLoop, calls=%fused_computation.2 | loop fusion | flops 50323456 | bytes 67174400 | tf_op jit(solution)/shard_map/reduce_sum | solution.py:29
  149.3 2.2 broadcast_in_dim.17
  151.6 24.9 %fusion.24 = bf16[2,1024,4,64]{1,3,2,0:T(8,128)(2,1)} fusion(f32[2,4,1024,2048]{3,2,1,0:T(8,128)} %get-tuple-element.6, f32[2,4,1024]{2,1,0:T(4,128)S(1)} %get-tuple-element.5, bf16[2,1024,4,64]{1,3,2,0:T(8,128)(2,1)} %broadcast_in_dim.17, bf16[2,1024,4,64]{1,3,2,0:T(8,128)(2,1)S(1)} %copy-done.4, f32[2,1024,4]{1,2,0:T(4,128)S(1)} %bitcast.88), kind=kOutput, calls=%fused_computation.38 | convolution fusion | flops 2203058176 | bytes 70320128 | tf_op jit(solution)/shard_map/fhpk,fkhd->fphd/dot_general | solution.py:30
  176.5 1.7 fusion.19
  178.3 23.2 %all_to_all.16 = bf16[128,2,8,256]{3,2,1,0:T(8,128)(2,1)S(1)} all-to-all(bf16[128,2,8,256]{3,2,1,0:T(8,128)(2,1)S(1)} %bitcast.80), channel_id=1, replica_groups=mesh['frame'=8,'pos'=16] {'frame','pos'}, dimensions={0} | all-to-all | bytes 2097152 | tf_op jit(solution)/shard_map/all_to_all | solution.py:90
  203.1 1.8 reshape_reshape.22
  205.4 1.9 reshape_reshape.23
  207.3 1.4 convolution_convert_fusion.2
  208.7 4.6 %reshape_reshape.21 = bf16[256,8,4,64]{3,2,1,0:T(4,128)(2,1)} reshape(bf16[2048,256]{1,0:T(8,128)(2,1)} %convolution_convert_fusion.2) | data formatting | bytes 2097152 | tf_op jit(solution)/shard_map/reshape;reshape | solution.py:22
  213.2 3.6 %multiply_reduce_fusion.1 = (f32[8,4,256]{2,1,0:T(4,128)S(1)}, f32[8,4,256,256]{2,3,1,0:T(8,128)S(1)}) fusion(bf16[256,8,4,64]{3,2,1,0:T(4,128)(2,1)} %reshape_reshape.23, bf16[256,8,4,64]{3,2,1,0:T(4,128)(2,1)S(1)} %copy-done.2), kind=kOutput, calls=%fused_computation.6 | convolution fusion | flops 272621568 | bytes 10518528 | tf_op jit(solution)/shard_map/fphd,kphd->phfk/dot_general | solution.py:27
  216.8 1.5 fusion.4
  218.4 1.9 fusion.20
  221.3 0.9 fusion.23
  222.2 18.2 %all_to_all.17 = bf16[8,32,8,256]{3,1,2,0:T(8,128)(2,1)S(1)} all-to-all(bf16[8,32,8,256]{3,1,2,0:T(8,128)(2,1)S(1)} %copy.71), channel_id=1, replica_groups=mesh['frame'=8,'pos'=16] {'frame'}, dimensions={0} | all-to-all | bytes 2097152 | tf_op jit(solution)/shard_map/all_to_all | solution.py:106
  240.4 1.6 copy.72
  (51 shorter events, 5.7 us)
Async XLA Ops:
  0.0 75.2 %copy-start = (bf16[256,256]{1,0:T(8,128)(2,1)S(1)}, bf16[256,256]{1,0:T(8,128)(2,1)}, u32[]{:S(2)}) copy-start(bf16[256,256]{1,0:T(8,128)(2,1)} %param.14) | copy-start | bytes 393220
  72.1 1.2 copy-start.1
  72.5 2.3 copy-start.14
  76.6 2.5 %copy-start.7 = (bf16[256,256]{1,0:T(8,128)(2,1)S(1)}, bf16[256,256]{1,0:T(8,128)(2,1)}, u32[]{:S(2)}) copy-start(bf16[256,256]{1,0:T(8,128)(2,1)} %param.15) | copy-start | bytes 393220
  86.1 4.1 %copy-start.8 = (bf16[256,256]{1,0:T(8,128)(2,1)S(1)}, bf16[256,256]{1,0:T(8,128)(2,1)}, u32[]{:S(2)}) copy-start(bf16[256,256]{1,0:T(8,128)(2,1)} %param.13) | copy-start | bytes 393220
  91.6 4.5 %copy-start.5 = (bf16[2048,256]{1,0:T(8,128)(2,1)S(1)}, bf16[2048,256]{1,0:T(8,128)(2,1)}, u32[]{:S(2)}) copy-start(bf16[2048,256]{1,0:T(8,128)(2,1)} %convolution_convert_fusion.5) | copy-start | bytes 3145732
  98.0 5.3 %copy-start.3 = (bf16[2,1024,4,64]{1,3,2,0:T(8,128)(2,1)S(1)}, bf16[2,1024,4,64]{1,3,2,0:T(8,128)(2,1)}, u32[]{:S(2)}) copy-start(bf16[2,1024,4,64]{1,3,2,0:T(8,128)(2,1)} %copy.61) | copy-start | bytes 3145732
  149.3 2.2 copy-start.4
  151.6 24.9 %copy-start.9 = (bf16[256,256]{1,0:T(8,128)(2,1)S(1)}, bf16[256,256]{1,0:T(8,128)(2,1)}, u32[]{:S(2)}) copy-start(bf16[256,256]{1,0:T(8,128)(2,1)} %param.16) | copy-start | bytes 393220
  178.3 24.0 %copy-start.15 = (f32[256]{0:T(256)S(1)}, f32[256]{0:T(256)}, u32[]{:S(2)}) copy-start(f32[256]{0:T(256)} %param.17) | copy-start | bytes 3076
  201.5 1.1 copy-start.10
  203.1 1.8 copy-start.11
  205.4 1.9 copy-start.12
  208.7 4.6 %copy-start.2 = (bf16[256,8,4,64]{3,2,1,0:T(4,128)(2,1)S(1)}, bf16[256,8,4,64]{3,2,1,0:T(4,128)(2,1)}, u32[]{:S(2)}) copy-start(bf16[256,8,4,64]{3,2,1,0:T(4,128)(2,1)} %reshape_reshape.22) | copy-start | bytes 3145732
  216.8 1.6 copy-start.6
  220.3 0.9 copy-start.13

commit v2 on v1

--- a/solution.py
+++ b/solution.py
@@ -1,9 +1,144 @@
 import jax
 import jax.numpy as jnp
 from jax import lax
+from jax.experimental import pallas as pl
+from jax.experimental.pallas import tpu as pltpu
 from jax.sharding import PartitionSpec as P
 
 HEADS = 4
+
+MESH = pl.DeviceIdType.MESH
+
+
+def exchange(x, names, sizes, cid):
+    n = x.shape[0]
+
+    def where(peer):
+        if len(names) == 1:
+            return {names[0]: peer}
+        return {names[0]: peer // sizes[1], names[1]: peer % sizes[1]}
+
+    def kernel(x_ref, o_ref, send_sem, recv_sem):
+        me = lax.axis_index(names[0])
+        if len(names) == 2:
+            me = me * sizes[1] + lax.axis_index(names[1])
+        barrier = pltpu.get_barrier_semaphore()
+        for k in range(1, n):
+            pl.semaphore_signal(barrier, inc=1, device_id=where((me + k) % n), device_id_type=MESH)
+        pl.semaphore_wait(barrier, n - 1)
+        copies = []
+        for k in range(1, n):
+            peer = (me + k) % n
+            copy = pltpu.make_async_remote_copy(
+                src_ref=x_ref.at[peer],
+                dst_ref=o_ref.at[me],
+                send_sem=send_sem.at[k],
+                recv_sem=recv_sem.at[k],
+                device_id=where(peer),
+                device_id_type=MESH,
+            )
+            copy.start()
+            copies.append(copy)
+        o_ref[me] = x_ref[me]
+        for copy in copies:
+            copy.wait()
+
+    return pl.pallas_call(
+        kernel,
+        out_shape=jax.ShapeDtypeStruct(x.shape, x.dtype),
+        in_specs=[pl.BlockSpec(memory_space=pltpu.VMEM)],
+        out_specs=pl.BlockSpec(memory_space=pltpu.VMEM),
+        scratch_shapes=[pltpu.SemaphoreType.DMA((n,)), pltpu.SemaphoreType.DMA((n,))],
+        compiler_params=pltpu.CompilerParams(collective_id=cid, has_side_effects=True),
+    )(x)
+
+
+def spatial_exchange(x, n_pos, n_frame, cid):
+    _, per, places, width = x.shape
+
+    def kernel(x_ref, o_ref, z_ref, send_sem, recv_sem, fsend_sem, frecv_sem, zsend_sem, zrecv_sem, local_sem):
+        fi = lax.axis_index("frame")
+        pi = lax.axis_index("pos")
+        barrier = pltpu.get_barrier_semaphore()
+        for k in range(1, n_pos):
+            pl.semaphore_signal(barrier, inc=1, device_id={"pos": (pi + k) % n_pos}, device_id_type=MESH)
+        for g in range(1, n_frame):
+            pl.semaphore_signal(barrier, inc=1, device_id={"frame": (fi + g) % n_frame}, device_id_type=MESH)
+        pl.semaphore_wait(barrier, n_pos - 1 + n_frame - 1)
+        copies = []
+        for k in range(1, n_pos):
+            peer = (pi + k) % n_pos
+            copy = pltpu.make_async_remote_copy(
+                src_ref=x_ref.at[peer],
+                dst_ref=o_ref.at[pi],
+                send_sem=send_sem.at[k],
+                recv_sem=recv_sem.at[k],
+                device_id={"pos": peer},
+                device_id_type=MESH,
+            )
+            copy.start()
+            copies.append(copy)
+        o_ref[pi] = x_ref[pi]
+
+        def spread(g):
+            return pltpu.make_async_remote_copy(
+                src_ref=x_ref.at[0, 0],
+                dst_ref=z_ref.at[pi],
+                send_sem=fsend_sem.at[g],
+                recv_sem=frecv_sem,
+                device_id={"frame": g},
+                device_id_type=MESH,
+            )
+
+        @pl.when(fi == 0)
+        def _():
+            local = pltpu.make_async_copy(x_ref.at[0, 0], z_ref.at[pi], local_sem)
+            local.start()
+            sends = [spread(g) for g in range(1, n_frame)]
+            for send in sends:
+                send.start()
+            local.wait()
+            for send in sends:
+                send.wait_send()
+
+        @pl.when(fi != 0)
+        def _():
+            spread(1).wait_recv()
+
+        for k in range(1, n_pos):
+            peer = (pi + k) % n_pos
+            copy = pltpu.make_async_remote_copy(
+                src_ref=z_ref.at[pi],
+                dst_ref=z_ref.at[pi],
+                send_sem=zsend_sem.at[k],
+                recv_sem=zrecv_sem.at[k],
+                device_id={"pos": peer},
+                device_id_type=MESH,
+            )
+            copy.start()
+            copies.append(copy)
+        for copy in copies:
+            copy.wait()
+
+    return pl.pallas_call(
+        kernel,
+        out_shape=(
+            jax.ShapeDtypeStruct(x.shape, x.dtype),
+            jax.ShapeDtypeStruct((n_pos, places, width), x.dtype),
+        ),
+        in_specs=[pl.BlockSpec(memory_space=pltpu.VMEM)],
+        out_specs=(pl.BlockSpec(memory_space=pltpu.VMEM), pl.BlockSpec(memory_space=pltpu.VMEM)),
+        scratch_shapes=[
+            pltpu.SemaphoreType.DMA((n_pos,)),
+            pltpu.SemaphoreType.DMA((n_pos,)),
+            pltpu.SemaphoreType.DMA((n_frame,)),
+            pltpu.SemaphoreType.DMA,
+            pltpu.SemaphoreType.DMA((n_pos,)),
+            pltpu.SemaphoreType.DMA((n_pos,)),
+            pltpu.SemaphoreType.DMA,
+        ],
+        compiler_params=pltpu.CompilerParams(collective_id=cid, has_side_effects=True),
+    )(x)
 
 
 def normed(values, gain):
@@ -50,18 +185,9 @@
     n_pos = lax.axis_size("pos")
     n_frame = lax.axis_size("frame")
     per = frames // n_pos
-    first = jnp.where(lax.axis_index("frame") == 0, latents[0], 0).astype(latents.dtype)
-    first = lax.psum(first, "frame")
-    sent = jnp.concatenate(
-        [
-            latents.reshape(n_pos, per, places, width),
-            jnp.broadcast_to(first[None, None], (n_pos, 1, places, width)),
-        ],
-        axis=1,
-    )
-    got = lax.all_to_all(sent, "pos", 0, 0, tiled=True)
-    xs = got[:, :per].transpose(1, 0, 2, 3).reshape(per, n_pos * places, width)
-    x0 = got[:, per].reshape(n_pos * places, width)
+    got, zero = spatial_exchange(latents.reshape(n_pos, per, places, width), n_pos, n_frame, 1)
+    xs = got.transpose(1, 0, 2, 3).reshape(per, n_pos * places, width)
+    x0 = zero.reshape(n_pos * places, width)
 
     n_one = normed(xs, gain_one)
     q_one = heads_of(project(n_one, query_one))
@@ -87,7 +213,7 @@
         .transpose(2, 1, 0, 3, 4)
         .reshape(n_frame * n_pos, per, run, width)
     )
-    got = lax.all_to_all(sent, ("frame", "pos"), 0, 0, tiled=True)
+    got = exchange(sent, ("frame", "pos"), (n_frame, n_pos), 2)
     mid_t = got.reshape(n_frame * n_pos * per, run, width)
 
     n_two = normed(mid_t, gain_two)
@@ -103,7 +229,7 @@
     decoded = (mid_t.astype(jnp.float32) + mixed_two).astype(jnp.bfloat16)
 
     sent = decoded.reshape(n_frame, frames, run, width)
-    got = lax.all_to_all(sent, "frame", 0, 0, tiled=True)
+    got = exchange(sent, ("frame",), (n_frame,), 3)
     return got.transpose(1, 0, 2, 3).reshape(frames, places, width)
 
 

time: 244 us -> 215 us (0.88)
  blocking collectives: 111 us -> 0 us
  Pallas kernels: 0 us -> 77.1 us
  local copies, waits for them, and re-layouts: 34.1 us -> 37.7 us
    pallas_call x0 -> x3, Pallas kernels: none -> 77.1 us  [the longest x2 44 us: exchange(): pl.pallas_call(kernel, out_shape=jax.ShapeDtypeStruct(x.shape, x.dtype),...]
    all_to_all x3 -> x0, blocking collectives: 74.6 us -> none  [the longest x1 33.2 us: shards(): got = lax.all_to_all(sent, 'pos', 0, 0, tiled=True)]
    psum x1 -> x0, blocking collectives: 36.7 us -> none  [shards(): first = lax.psum(first, 'frame')]
    dot_general x2, matrix products: 26.9 us -> 30.7 us  [softmax_attend(): jnp.einsum(value_form, weights.astype(jnp.bfloat16), vals, preferred_elem...]
    unnamed x32 -> x36, local copies, waits for them, and re-layouts: 1.27 us -> 4 us
    dot_general x8, matrix products: 8.76 us -> 6.23 us  [project(): jnp.dot(flat, weight, preferred_element_type=jnp.float32)]
where the time goes in v2:
time: 215 us; the launch traced here: 212 us
  Pallas kernels  77.1 us (36%)
  matrix products  66.8 us (31%)
  local copies, waits for them, and re-layouts  37.7 us (18%)
  other arithmetic  30.1 us (14%)
    pallas_call x2, Pallas kernels, exchange(): pl.pallas_call(kernel, out_shape=jax.ShapeDtypeStruct(x.shape, x.dtype),...  44 us
    pallas_call x1, Pallas kernels, spatial_exchange(): pl.pallas_call(kernel, out_shape=(jax.ShapeDtypeStruct(x.shape, x.dtype),...  33.1 us
    dot_general x2, matrix products, softmax_attend(): jnp.einsum(value_form, weights.astype(jnp.bfloat16), vals, preferred_elem...  30.7 us
    dot_general x2, matrix products, softmax_attend(): jnp.einsum(score_form, query, keys, preferred_element_type=jnp.float32)  27.3 us
    another operation x8, local copies, waits for them, and re-layouts, heads_of(): values.reshape(values.shape[:-1] + (HEADS, values.shape[-1] // HEADS))  27 us
    reduce_sum x2, other arithmetic, softmax_attend(): totals = jnp.sum(weights, axis=-1)  22.9 us
    dot_general x8, matrix products, project(): jnp.dot(flat, weight, preferred_element_type=jnp.float32)  6.23 us

profile of v2, /device:TPU:1, one launch (start us, length us, event | category | flops | bytes accessed | tf_op | source)
XLA Modules:
  0.0 212.0 jit_solution(16435082451330508682)
XLA Ops:
  0.0 33.1 %shard_map.109 = (bf16[16,2,64,256]{3,2,1,0:T(8,128)(2,1)}, bf16[16,64,256]{2,1,0:T(8,128)(2,1)}) custom-call(bf16[16,2,64,256]{3,2,1,0:T(8,128)(2,1)} %bitcast.84), custom_call_target="tpu_custom_call" | custom-call | tf_op jit(solution)/shard_map/pallas_call | solution.py:123
  33.1 1.5 convert_bitcast_fusion
  34.7 1.1 copy-done.8
  36.6 1.4 convolution_convert_fusion.3
  38.0 4.4 %reshape.128 = bf16[2,1024,4,64]{3,2,1,0:T(4,128)(2,1)} reshape(bf16[2048,256]{1,0:T(8,128)(2,1)} %convolution_convert_fusion.3) | data formatting | bytes 2097152 | tf_op jit(solution)/shard_map/reshape;reshape | solution.py:157
  42.5 4.1 %copy.49 = bf16[2,1024,4,64]{1,3,2,0:T(8,128)(2,1)} copy(bf16[2,1024,4,64]{3,2,1,0:T(4,128)(2,1)} %reshape.128) | data formatting | bytes 2097152 | tf_op jit(solution)/shard_map/reshape;reshape | solution.py:157
  46.5 1.4 convolution_convert_fusion.4
  48.0 4.4 %reshape.127 = bf16[2,1024,4,64]{3,2,1,0:T(4,128)(2,1)} reshape(bf16[2048,256]{1,0:T(8,128)(2,1)} %convolution_convert_fusion.4) | data formatting | bytes 2097152 | tf_op jit(solution)/shard_map/reshape;reshape | solution.py:157
  52.4 1.3 multiply_reduce_fusion.3
  53.7 1.4 fusion.36
  55.8 23.1 %multiply_reduce_fusion = (f32[2,4,1024]{2,1,0:T(4,128)S(1)}, f32[2,4,1024,2048]{3,2,1,0:T(8,128)}) fusion(bf16[2,1024,4,64]{1,3,2,0:T(8,128)(2,1)S(1)} %broadcast_in_dim.11, bf16[2,1024,4,64]{1,3,2,0:T(8,128)(2,1)S(1)} %copy-done.6, bf16[2,1024,4,64]{3,2,1,0:T(4,128)(2,1)S(1)} %copy-done.3), kind=kOutput, calls=%fused_computation.1 | convolution fusion | flops 2185224192 | bytes 70287360 | tf_op jit(solution)/shard_map/fphd,fkhd->fhpk/dot_general | solution.py:162
  78.9 21.3 %fusion = f32[2,4,1024]{2,1,0:T(4,128)S(1)} fusion(f32[2,4,1024,2048]{3,2,1,0:T(8,128)} %get-tuple-element.10, f32[2,4,1024]{2,1,0:T(4,128)S(1)} %get-tuple-element.9), kind=kLoop, calls=%fused_computation.2 | loop fusion | flops 50323456 | bytes 67174400 | tf_op jit(solution)/shard_map/reduce_sum | solution.py:164
  100.1 1.4 convolution_convert_fusion.5
  101.6 4.4 %reshape.126 = bf16[2,1024,4,64]{3,2,1,0:T(4,128)(2,1)} reshape(bf16[2048,256]{1,0:T(8,128)(2,1)} %convolution_convert_fusion.5) | data formatting | bytes 2097152 | tf_op jit(solution)/shard_map/reshape;reshape | solution.py:157
  106.0 4.1 %copy.46 = bf16[2,1024,4,64]{1,3,2,0:T(8,128)(2,1)} copy(bf16[2,1024,4,64]{3,2,1,0:T(4,128)(2,1)} %reshape.126) | data formatting | bytes 2097152 | tf_op jit(solution)/shard_map/reshape;reshape | solution.py:157
  110.5 1.1 broadcast_in_dim.9
  112.1 24.8 %fusion.21 = bf16[2,1024,4,64]{1,3,2,0:T(8,128)(2,1)} fusion(f32[2,4,1024,2048]{3,2,1,0:T(8,128)} %get-tuple-element.10, f32[2,4,1024]{2,1,0:T(4,128)S(1)} %get-tuple-element.9, bf16[2,1024,4,64]{1,3,2,0:T(8,128)(2,1)} %broadcast_in_dim.9, bf16[2,1024,4,64]{1,3,2,0:T(8,128)(2,1)S(1)} %copy-done.7, f32[2,1024,4]{1,2,0:T(4,128)S(1)} %bitcast.86), kind=kOutput, calls=%fused_computation.34 | convolution fusion | flops 2203058176 | bytes 70320128 | tf_op jit(solution)/shard_map/fhpk,fkhd->fphd/dot_general | solution.py:165
  136.9 1.7 fusion.25
  138.6 1.1 copy.52
  139.7 26.7 %shard_map.110 = bf16[128,2,8,256]{3,2,1,0:T(8,128)(2,1)} custom-call(bf16[128,2,8,256]{3,2,1,0:T(8,128)(2,1)} %bitcast.79), custom_call_target="tpu_custom_call" | custom-call | tf_op jit(solution)/shard_map/pallas_call | solution.py:46
  166.3 1.7 multiply_reduce_fusion.2
  169.2 1.8 reshape_reshape.22
  171.5 1.9 reshape_reshape.23
  173.3 4.2 %multiply_reduce_fusion.1 = (f32[8,4,256]{2,1,0:T(4,128)S(1)}, f32[8,4,256,256]{2,3,1,0:T(8,128)S(1)}) fusion(bf16[256,8,4,64]{3,2,1,0:T(4,128)(2,1)} %reshape_reshape.23, bf16[256,8,4,64]{3,2,1,0:T(4,128)(2,1)} %reshape_reshape.22), kind=kOutput, calls=%fused_computation.6 | convolution fusion | flops 272621568 | bytes 10518528 | tf_op jit(solution)/shard_map/fphd,kphd->phfk/dot_general | solution.py:162
  177.6 1.6 fusion.4
  179.1 1.6 copy-done.1
  181.2 1.8 reshape_reshape.21
  183.0 5.9 %fusion.18 = bf16[256,8,4,64]{0,3,2,1:T(8,128)(2,1)S(1)} fusion(f32[256,8,4]{0,2,1:T(4,128)S(1)} %bitcast.87, f32[8,4,256,256]{2,3,1,0:T(8,128)} %copy-done.1, f32[8,4,256]{2,1,0:T(4,128)S(1)} %get-tuple-element.11, bf16[256,8,4,64]{3,2,1,0:T(4,128)(2,1)} %reshape_reshape.21), kind=kOutput, calls=%fused_computation.29 | convolution fusion | flops 275775488 | bytes 10551296 | tf_op jit(solution)/shard_map/phfk,kphd->fphd/dot_general | solution.py:165
  189.9 0.9 fusion.26
  190.8 1.6 copy.59
  192.3 17.4 %shard_map.111 = bf16[8,32,8,256]{3,2,1,0:T(8,128)(2,1)} custom-call(bf16[8,32,8,256]{3,2,1,0:T(8,128)(2,1)} %bitcast.80), custom_call_target="tpu_custom_call" | custom-call | tf_op jit(solution)/shard_map/pallas_call | solution.py:46
  209.7 2.3 %copy_bitcast_fusion = bf16[32,64,256]{2,1,0:T(8,128)(2,1)} fusion(bf16[8,32,8,256]{3,2,1,0:T(8,128)(2,1)} %shard_map.111), kind=kLoop, calls=%fused_computation.53 | loop fusion | bytes 2097152 | tf_op jit(solution)/shard_map/reshape | solution.py:233
  (52 shorter events, 5.3 us)
Async XLA Ops:
  0.0 36.6 %copy-start = (bf16[256,256]{1,0:T(8,128)(2,1)S(1)}, bf16[256,256]{1,0:T(8,128)(2,1)}, u32[]{:S(2)}) copy-start(bf16[256,256]{1,0:T(8,128)(2,1)} %param.14) | copy-start | bytes 393220
  34.5 1.2 copy-start.8
  34.6 1.7 copy-start.16
  42.5 4.1 %copy-start.10 = (bf16[256,256]{1,0:T(8,128)(2,1)S(1)}, bf16[256,256]{1,0:T(8,128)(2,1)}, u32[]{:S(2)}) copy-start(bf16[256,256]{1,0:T(8,128)(2,1)} %param.13) | copy-start | bytes 393220
  53.7 1.9 copy-start.3
  53.7 2.0 copy-start.6
  55.2 23.7 %copy-start.4 = (bf16[1024,256]{1,0:T(8,128)(2,1)}, bf16[1024,256]{1,0:T(8,128)(2,1)S(1)}, u32[]{:S(2)}) copy-start(bf16[1024,256]{1,0:T(8,128)(2,1)S(1)} %fusion.36) | copy-start | bytes 1572868
  78.8 21.3 %copy-start.9 = (bf16[256,256]{1,0:T(8,128)(2,1)S(1)}, bf16[256,256]{1,0:T(8,128)(2,1)}, u32[]{:S(2)}) copy-start(bf16[256,256]{1,0:T(8,128)(2,1)} %param.15) | copy-start | bytes 393220
  106.0 4.1 %copy-start.5 = (bf16[1024,256]{1,0:T(8,128)(2,1)S(1)}, bf16[1024,256]{1,0:T(8,128)(2,1)}, u32[]{:S(2)}) copy-start(bf16[1024,256]{1,0:T(8,128)(2,1)} %copy-done.4) | copy-start | bytes 1572868
  110.5 1.6 copy-start.7
  112.1 24.8 %copy-start.11 = (bf16[256,256]{1,0:T(8,128)(2,1)S(1)}, bf16[256,256]{1,0:T(8,128)(2,1)}, u32[]{:S(2)}) copy-start(bf16[256,256]{1,0:T(8,128)(2,1)} %param.16) | copy-start | bytes 393220
  139.7 28.7 %copy-start.17 = (f32[256]{0:T(256)S(1)}, f32[256]{0:T(256)}, u32[]{:S(2)}) copy-start(f32[256]{0:T(256)} %param.17) | copy-start | bytes 3076
  166.3 2.1 copy-start.2
  166.3 2.4 %copy-start.12 = (bf16[256,256]{1,0:T(8,128)(2,1)S(1)}, bf16[256,256]{1,0:T(8,128)(2,1)}, u32[]{:S(2)}) copy-start(bf16[256,256]{1,0:T(8,128)(2,1)} %param.18) | copy-start | bytes 393220
  169.2 1.8 copy-start.13
  177.5 3.2 %copy-start.1 = (f32[8,4,256,256]{2,3,1,0:T(8,128)}, f32[8,4,256,256]{2,3,1,0:T(8,128)S(1)}, u32[]{:S(2)}) copy-start(f32[8,4,256,256]{2,3,1,0:T(8,128)S(1)} %get-tuple-element.12) | copy-start | bytes 25165828
  177.5 3.2 %copy-start.14 = (bf16[256,256]{1,0:T(8,128)(2,1)S(1)}, bf16[256,256]{1,0:T(8,128)(2,1)}, u32[]{:S(2)}) copy-start(bf16[256,256]{1,0:T(8,128)(2,1)} %param.20) | copy-start | bytes 393220
  189.0 0.9 copy-start.15

commit v3 on v2

--- a/solution.py
+++ b/solution.py
@@ -139,6 +139,57 @@
         ],
         compiler_params=pltpu.CompilerParams(collective_id=cid, has_side_effects=True),
     )(x)
+
+
+def spatial_attend(x, q, kt, vt, k0t, v0t, out_w, rows):
+    frames, places, width = x.shape
+    depth = width // HEADS
+    scale = depth ** (-0.5)
+
+    def kernel(x_ref, q_ref, kt_ref, vt_ref, k0t_ref, v0t_ref, w_ref, o_ref):
+        acc = x_ref[0].astype(jnp.float32)
+        for h in range(HEADS):
+            part = pl.ds(h * depth, depth)
+            qh = q_ref[0, :, part]
+            own = jnp.dot(qh, kt_ref[0, part, :], preferred_element_type=jnp.float32) * scale
+            first = jnp.dot(qh, k0t_ref[part, :], preferred_element_type=jnp.float32) * scale
+            high = jnp.maximum(jnp.max(own, axis=-1, keepdims=True), jnp.max(first, axis=-1, keepdims=True))
+            own = jnp.exp(own - high)
+            first = jnp.exp(first - high)
+            totals = jnp.sum(own, axis=-1, keepdims=True) + jnp.sum(first, axis=-1, keepdims=True)
+            contract = (((1,), (1,)), ((), ()))
+            summed = lax.dot_general(
+                own.astype(jnp.bfloat16), vt_ref[0, part, :], contract, preferred_element_type=jnp.float32
+            ) + lax.dot_general(
+                first.astype(jnp.bfloat16), v0t_ref[part, :], contract, preferred_element_type=jnp.float32
+            )
+            attended = (summed / totals).astype(jnp.bfloat16)
+            acc = acc + jnp.dot(attended, w_ref[part, :], preferred_element_type=jnp.float32)
+        o_ref[0] = acc.astype(o_ref.dtype)
+
+    tile = lambda f, t: (f, t, 0)
+    whole = lambda f, t: (f, 0, 0)
+    fixed = lambda f, t: (0, 0)
+    return pl.pallas_call(
+        kernel,
+        out_shape=jax.ShapeDtypeStruct(x.shape, x.dtype),
+        grid=(frames, places // rows),
+        in_specs=[
+            pl.BlockSpec((1, rows, width), tile),
+            pl.BlockSpec((1, rows, width), tile),
+            pl.BlockSpec((1, width, places), whole),
+            pl.BlockSpec((1, width, places), whole),
+            pl.BlockSpec((width, places), fixed),
+            pl.BlockSpec((width, places), fixed),
+            pl.BlockSpec((width, width), fixed),
+        ],
+        out_specs=pl.BlockSpec((1, rows, width), tile),
+    )(x, q, kt, vt, k0t, v0t, out_w)
+
+
+def transposed(values, weight):
+    result = jnp.einsum("...rc,cd->...dr", values, weight, preferred_element_type=jnp.float32)
+    return result.astype(jnp.bfloat16)
 
 
 def normed(values, gain):
@@ -190,21 +241,18 @@
     x0 = zero.reshape(n_pos * places, width)
 
     n_one = normed(xs, gain_one)
-    q_one = heads_of(project(n_one, query_one))
-    k_one = heads_of(project(n_one, key_one))
-    v_one = heads_of(project(n_one, value_one))
+    q_one = project(n_one, query_one)
     n_zero = normed(x0, gain_one)
-    k_zero = heads_of(project(n_zero, key_one))
-    v_zero = heads_of(project(n_zero, value_one))
-    keys = jnp.concatenate([k_one, jnp.broadcast_to(k_zero[None], k_one.shape)], axis=1)
-    vals = jnp.concatenate([v_one, jnp.broadcast_to(v_zero[None], v_one.shape)], axis=1)
-    attended_one = softmax_attend(
-        q_one, keys, vals, "fphd,fkhd->fhpk", "fhpk,fkhd->fphd", "fhp->fph"
-    ).reshape(xs.shape).astype(jnp.bfloat16)
-    mixed_one = jnp.dot(
-        attended_one.reshape(-1, width), out_one, preferred_element_type=jnp.float32
-    ).reshape(xs.shape)
-    middle = (xs.astype(jnp.float32) + mixed_one).astype(jnp.bfloat16)
+    middle = spatial_attend(
+        xs,
+        q_one,
+        transposed(n_one, key_one),
+        transposed(n_one, value_one),
+        transposed(n_zero, key_one),
+        transposed(n_zero, value_one),
+        out_one,
+        min(256, n_pos * places),
+    )
 
     all_places = n_pos * places
     run = all_places // (n_pos * n_frame)

time: 215 us -> 166 us (0.77)
  matrix products: 66.8 us -> 19.3 us
  Pallas kernels: 77.1 us -> 121 us
  other arithmetic: 30.1 us -> 5.4 us
  local copies, waits for them, and re-layouts: 37.7 us -> 16.7 us
    pallas_call x0 -> x1, Pallas kernels: none -> 44.6 us  [spatial_attend(): pl.pallas_call(kernel, out_shape=jax.ShapeDtypeStruct(x.shape, x.dtype),...]
    dot_general x2 -> x1, matrix products: 30.7 us -> 5.93 us  [softmax_attend(): jnp.einsum(value_form, weights.astype(jnp.bfloat16), vals, preferred_elem...]
    dot_general x2 -> x1, matrix products: 27.3 us -> 4.2 us  [softmax_attend(): jnp.einsum(score_form, query, keys, preferred_element_type=jnp.float32)]
    another operation x8 -> x3, local copies, waits for them, and re-layouts: 27 us -> 5.49 us  [heads_of(): values.reshape(values.shape[:-1] + (HEADS, values.shape[-1] // HEADS))]
    reduce_sum x2 -> x1, other arithmetic: 22.9 us -> 1.59 us  [softmax_attend(): totals = jnp.sum(weights, axis=-1)]
    dot_general x1 -> x4, matrix products: 1.71 us -> 5.61 us  [transposed(): jnp.einsum('...rc,cd->...dr', values, weight, preferred_element_type=jnp....]
    dot_general x8 -> x4, matrix products: 6.23 us -> 2.7 us  [project(): jnp.dot(flat, weight, preferred_element_type=jnp.float32)]
where the time goes in v3:
time: 166 us; the launch traced here: 163 us
  Pallas kernels  121 us (73%)
  matrix products  19.3 us (12%)
  local copies, waits for them, and re-layouts  16.7 us (10%)
  other arithmetic  5.4 us (3%)
    pallas_call x1, Pallas kernels, spatial_attend(): pl.pallas_call(kernel, out_shape=jax.ShapeDtypeStruct(x.shape, x.dtype),...  44.6 us
    pallas_call x2, Pallas kernels, exchange(): pl.pallas_call(kernel, out_shape=jax.ShapeDtypeStruct(x.shape, x.dtype),...  43.8 us
    pallas_call x1, Pallas kernels, spatial_exchange(): pl.pallas_call(kernel, out_shape=(jax.ShapeDtypeStruct(x.shape, x.dtype),...  33.1 us
    dot_general x1, matrix products, softmax_attend(): jnp.einsum(value_form, weights.astype(jnp.bfloat16), vals, preferred_elem...  5.93 us
    dot_general x4, matrix products, transposed(): jnp.einsum('...rc,cd->...dr', values, weight, preferred_element_type=jnp....  5.61 us
    another operation x3, local copies, waits for them, and re-layouts, heads_of(): values.reshape(values.shape[:-1] + (HEADS, values.shape[-1] // HEADS))  5.49 us
    dot_general x1, matrix products, softmax_attend(): jnp.einsum(score_form, query, keys, preferred_element_type=jnp.float32)  4.2 us

profile of v3, /device:TPU:1, one launch (start us, length us, event | category | flops | bytes accessed | tf_op | source)
XLA Modules:
  0.0 163.1 jit_solution(16097130678405833239)
XLA Ops:
  0.0 33.1 %shard_map.109 = (bf16[16,2,64,256]{3,2,1,0:T(8,128)(2,1)}, bf16[16,64,256]{2,1,0:T(8,128)(2,1)}) custom-call(bf16[16,2,64,256]{3,2,1,0:T(8,128)(2,1)} %bitcast.81), custom_call_target="tpu_custom_call" | custom-call | tf_op jit(solution)/shard_map/pallas_call | solution.py:123
  33.1 1.4 copy.72
  34.6 0.4 multiply_reduce_fusion.2
  35.1 1.7 %fusion.16.kt_ref = bf16[2,256,1024]{2,1,0:T(8,128)(2,1)} fusion(bf16[2,1024,256]{2,1,0:T(8,128)(2,1)S(1)} %bitcast.74, f32[256]{0:T(256)S(1)} %copy-done.12, f32[2,1024]{1,0:T(2,128)S(1)} %rsqrt.39, bf16[256,256]{1,0:T(8,128)(2,1)S(1)} %copy-done), kind=kOutput, calls=%fused_computation.30 | convolution fusion | flops 271056896 | bytes 2237440 | tf_op jit(solution)/shard_map/...rc,cd->...dr/dot_general | solution.py:191
  36.8 1.6 %fusion.17.vt_ref = bf16[2,256,1024]{2,1,0:T(8,128)(2,1)} fusion(bf16[2,1024,256]{2,1,0:T(8,128)(2,1)S(1)} %bitcast.75, f32[256]{0:T(256)S(1)} %copy-done.12, f32[2,1024]{1,0:T(2,128)S(1)} %rsqrt.39, bf16[256,256]{1,0:T(8,128)(2,1)S(1)} %copy-done.7), kind=kOutput, calls=%fused_computation.31 | convolution fusion | flops 271056896 | bytes 2237440 | tf_op jit(solution)/shard_map/...rc,cd->...dr/dot_general | solution.py:191
  38.5 0.3 bitcast_convert_fusion
  39.0 0.3 fusion.10
  39.3 0.5 copy-done.6
  39.9 1.4 convolution_convert_fusion.3
  41.8 1.1 fusion.18.k0t_ref
  42.9 1.2 fusion.19.v0t_ref
  44.1 44.6 %shard_map.110 = bf16[2,1024,256]{2,1,0:T(8,128)(2,1)} custom-call(bf16[2,1024,256]{2,1,0:T(8,128)(2,1)} %bitcast.76, bf16[2,1024,256]{2,1,0:T(8,128)(2,1)} %bitcast.77, bf16[2,256,1024]{2,1,0:T(8,128)(2,1)} %fusion.16.kt_ref, bf16[2,256,1024]{2,1,0:T(8,128)(2,1)} %fusion.17.vt_ref, bf16[256,1024]{1,0:T(8,128)(2,1)} %fusion.18.k0t_ref, ...), custom_call_target="tpu_custom_call" | custom-call | tf_op jit(solution)/shard_map/pallas_call | solution.py:173
  88.7 2.3 %copy.79 = bf16[2,16,8,8,256]{4,3,0,1,2:T(8,128)(2,1)} copy(bf16[2,16,8,8,256]{4,3,2,1,0:T(8,128)(2,1)} %bitcast.78) | data formatting | bytes 2097152 | tf_op jit(solution)/shard_map/reshape | solution.py:260
  91.0 26.5 %shard_map.111 = bf16[128,2,8,256]{3,2,1,0:T(8,128)(2,1)} custom-call(bf16[128,2,8,256]{3,2,1,0:T(8,128)(2,1)} %bitcast.79), custom_call_target="tpu_custom_call" | custom-call | tf_op jit(solution)/shard_map/pallas_call | solution.py:46
  117.6 1.7 %multiply_reduce_fusion.1 = f32[128,2,8]{2,1,0:T(2,128)S(1)} fusion(bf16[128,2,8,256]{3,2,1,0:T(8,128)(2,1)} %shard_map.111), kind=kLoop, calls=%fused_computation.25 | loop fusion | flops 1570816 | bytes 1056768 | tf_op jit(solution)/shard_map/reduce_sum | solution.py:197
  119.6 0.3 fusion.8
  120.0 0.4 convolution_convert_fusion.1
  120.4 1.8 %reshape_reshape.10 = bf16[256,8,4,64]{3,2,1,0:T(4,128)(2,1)} reshape(bf16[2048,256]{1,0:T(8,128)(2,1)S(1)} %convolution_convert_fusion.1) | data formatting | bytes 2097152 | tf_op jit(solution)/shard_map/reshape;reshape | solution.py:208
  122.3 0.4 convolution_convert_fusion
  122.7 1.9 %reshape_reshape.11 = bf16[256,8,4,64]{3,2,1,0:T(4,128)(2,1)} reshape(bf16[2048,256]{1,0:T(8,128)(2,1)S(1)} %convolution_convert_fusion) | data formatting | bytes 2097152 | tf_op jit(solution)/shard_map/reshape;reshape | solution.py:208
  124.6 4.2 %multiply_reduce_fusion = (f32[8,4,256]{2,1,0:T(4,128)S(1)}, f32[8,4,256,256]{2,3,1,0:T(8,128)S(1)}) fusion(bf16[256,8,4,64]{3,2,1,0:T(4,128)(2,1)} %reshape_reshape.11, bf16[256,8,4,64]{3,2,1,0:T(4,128)(2,1)} %reshape_reshape.10), kind=kOutput, calls=%fused_computation.1 | convolution fusion | flops 272621568 | bytes 10518528 | tf_op jit(solution)/shard_map/fphd,kphd->phfk/dot_general | solution.py:213
  128.8 1.6 fusion
  130.4 1.6 copy-done.1
  132.0 0.4 convolution_convert_fusion.2
  132.4 1.8 %reshape_reshape.9 = bf16[256,8,4,64]{3,2,1,0:T(4,128)(2,1)} reshape(bf16[2048,256]{1,0:T(8,128)(2,1)S(1)} %convolution_convert_fusion.2) | data formatting | bytes 2097152 | tf_op jit(solution)/shard_map/reshape;reshape | solution.py:208
  134.2 5.9 %fusion.6 = bf16[256,8,4,64]{0,3,2,1:T(8,128)(2,1)S(1)} fusion(f32[256,8,4]{0,2,1:T(4,128)S(1)} %bitcast.83, f32[8,4,256,256]{2,3,1,0:T(8,128)} %copy-done.1, f32[8,4,256]{2,1,0:T(4,128)S(1)} %get-tuple-element.9, bf16[256,8,4,64]{3,2,1,0:T(4,128)(2,1)} %reshape_reshape.9), kind=kOutput, calls=%fused_computation.12 | convolution fusion | flops 275775488 | bytes 10551296 | tf_op jit(solution)/shard_map/phfk,kphd->fphd/dot_general | solution.py:216
  140.2 0.2 bitcast_convert_fusion.1
  140.4 0.7 copy-done.11
  141.1 0.9 fusion.11
  142.0 1.6 copy.86
  143.5 17.2 %shard_map.112 = bf16[8,32,8,256]{3,2,1,0:T(8,128)(2,1)} custom-call(bf16[8,32,8,256]{3,2,1,0:T(8,128)(2,1)} %bitcast.80), custom_call_target="tpu_custom_call" | custom-call | tf_op jit(solution)/shard_map/pallas_call | solution.py:46
  160.8 2.3 %copy_bitcast_fusion = bf16[32,64,256]{2,1,0:T(8,128)(2,1)} fusion(bf16[8,32,8,256]{3,2,1,0:T(8,128)(2,1)} %shard_map.112), kind=kLoop, calls=%fused_computation.39 | loop fusion | bytes 2097152 | tf_op jit(solution)/shard_map/reshape | solution.py:281
  (35 shorter events, 1.4 us)
Async XLA Ops:
  0.0 35.1 %copy-start = (bf16[256,256]{1,0:T(8,128)(2,1)S(1)}, bf16[256,256]{1,0:T(8,128)(2,1)}, u32[]{:S(2)}) copy-start(bf16[256,256]{1,0:T(8,128)(2,1)} %param.14) | copy-start | bytes 393220
  0.0 35.1 %copy-start.12 = (f32[256]{0:T(256)S(1)}, f32[256]{0:T(256)}, u32[]{:S(2)}) copy-start(f32[256]{0:T(256)} %param.12) | copy-start | bytes 3076
  33.1 1.5 copy-start.3
  34.5 4.0 %copy-start.4 = (bf16[2,16,64,256]{3,2,1,0:T(8,128)(2,1)}, bf16[2,16,64,256]{3,2,1,0:T(8,128)(2,1)S(1)}, u32[]{:S(2)}) copy-start(bf16[2,16,64,256]{3,2,1,0:T(8,128)(2,1)S(1)} %copy.72) | copy-start | bytes 3145732
  34.5 2.3 %copy-start.7 = (bf16[256,256]{1,0:T(8,128)(2,1)S(1)}, bf16[256,256]{1,0:T(8,128)(2,1)}, u32[]{:S(2)}) copy-start(bf16[256,256]{1,0:T(8,128)(2,1)} %param.15) | copy-start | bytes 393220
  39.0 0.9 copy-start.6
  39.0 2.3 %copy-start.5 = (bf16[16,64,256]{2,1,0:T(8,128)(2,1)S(1)}, bf16[16,64,256]{2,1,0:T(8,128)(2,1)}, u32[]{:S(2)}) copy-start(bf16[16,64,256]{2,1,0:T(8,128)(2,1)} %get-tuple-element.8) | copy-start | bytes 1572868
  91.0 28.6 %copy-start.13 = (f32[256]{0:T(256)S(1)}, f32[256]{0:T(256)}, u32[]{:S(2)}) copy-start(f32[256]{0:T(256)} %param.17) | copy-start | bytes 3076
  117.6 2.1 %copy-start.2 = (bf16[128,2,8,256]{3,2,1,0:T(8,128)(2,1)S(1)}, bf16[128,2,8,256]{3,2,1,0:T(8,128)(2,1)}, u32[]{:S(2)}) copy-start(bf16[128,2,8,256]{3,2,1,0:T(8,128)(2,1)} %shard_map.111) | copy-start | bytes 3145732
  117.6 2.4 %copy-start.8 = (bf16[256,256]{1,0:T(8,128)(2,1)S(1)}, bf16[256,256]{1,0:T(8,128)(2,1)}, u32[]{:S(2)}) copy-start(bf16[256,256]{1,0:T(8,128)(2,1)} %param.18) | copy-start | bytes 393220
  120.4 1.8 %copy-start.9 = (bf16[256,256]{1,0:T(8,128)(2,1)S(1)}, bf16[256,256]{1,0:T(8,128)(2,1)}, u32[]{:S(2)}) copy-start(bf16[256,256]{1,0:T(8,128)(2,1)} %param.19) | copy-start | bytes 393220
  128.8 3.2 %copy-start.1 = (f32[8,4,256,256]{2,3,1,0:T(8,128)}, f32[8,4,256,256]{2,3,1,0:T(8,128)S(1)}, u32[]{:S(2)}) copy-start(f32[8,4,256,256]{2,3,1,0:T(8,128)S(1)} %get-tuple-element.10) | copy-start | bytes 25165828
  128.8 3.2 %copy-start.10 = (bf16[256,256]{1,0:T(8,128)(2,1)S(1)}, bf16[256,256]{1,0:T(8,128)(2,1)}, u32[]{:S(2)}) copy-start(bf16[256,256]{1,0:T(8,128)(2,1)} %param.20) | copy-start | bytes 393220
  140.2 0.9 copy-start.11

commit v4 on v3

--- a/solution.py
+++ b/solution.py
@@ -141,12 +141,31 @@
     )(x)
 
 
-def spatial_attend(x, q, kt, vt, k0t, v0t, out_w, rows):
+def spatial_attend(x, q, kt, vt, k0t, v0t, out_w, rows, n_frame, n_pos, cid):
     frames, places, width = x.shape
     depth = width // HEADS
     scale = depth ** (-0.5)
-
-    def kernel(x_ref, q_ref, kt_ref, vt_ref, k0t_ref, v0t_ref, w_ref, o_ref):
+    n_dev = n_frame * n_pos
+    run = places // n_dev
+    chunks = rows // run
+
+    def kernel(x_ref, q_ref, kt_ref, vt_ref, k0t_ref, v0t_ref, w_ref, o_ref, made, got, send_sem, recv_sem):
+        f = pl.program_id(0)
+        t = pl.program_id(1)
+        fi = lax.axis_index("frame")
+        pi = lax.axis_index("pos")
+        me = fi * n_pos + pi
+
+        @pl.when((f == 0) & (t == 0))
+        def _():
+            barrier = pltpu.get_barrier_semaphore()
+            for k in range(1, n_dev):
+                peer = (me + k) % n_dev
+                pl.semaphore_signal(
+                    barrier, inc=1, device_id={"frame": peer // n_pos, "pos": peer % n_pos}, device_id_type=MESH
+                )
+            pl.semaphore_wait(barrier, n_dev - 1)
+
         acc = x_ref[0].astype(jnp.float32)
         for h in range(HEADS):
             part = pl.ds(h * depth, depth)
@@ -165,14 +184,42 @@
             )
             attended = (summed / totals).astype(jnp.bfloat16)
             acc = acc + jnp.dot(attended, w_ref[part, :], preferred_element_type=jnp.float32)
-        o_ref[0] = acc.astype(o_ref.dtype)
+        base = t * chunks
+        made[f, pl.ds(base, chunks)] = acc.reshape(chunks, run, width).astype(made.dtype)
+
+        for i in range(chunks):
+            gf = i % n_frame
+            gp = (base + i) // n_frame
+
+            @pl.when((gf == fi) & (gp == pi))
+            def _():
+                got[me, f] = made[f, base + i]
+
+            @pl.when((gf != fi) | (gp != pi))
+            def _():
+                pltpu.make_async_remote_copy(
+                    src_ref=made.at[f, base + i],
+                    dst_ref=got.at[me, f],
+                    send_sem=send_sem,
+                    recv_sem=recv_sem,
+                    device_id={"frame": gf, "pos": gp},
+                    device_id_type=MESH,
+                ).start()
+
+        @pl.when((f == frames - 1) & (t == places // rows - 1))
+        def _():
+            others = pltpu.make_async_copy(got.at[pl.ds(0, n_dev - 1)], got.at[pl.ds(1, n_dev - 1)], recv_sem)
+            others.wait()
+            sent = pltpu.make_async_copy(got.at[pl.ds(0, n_dev - 1)], got.at[pl.ds(1, n_dev - 1)], send_sem)
+            sent.wait()
+            o_ref[...] = got[...]
 
     tile = lambda f, t: (f, t, 0)
     whole = lambda f, t: (f, 0, 0)
     fixed = lambda f, t: (0, 0)
     return pl.pallas_call(
         kernel,
-        out_shape=jax.ShapeDtypeStruct(x.shape, x.dtype),
+        out_shape=jax.ShapeDtypeStruct((n_dev, frames, run, width), x.dtype),
         grid=(frames, places // rows),
         in_specs=[
             pl.BlockSpec((1, rows, width), tile),
@@ -183,7 +230,14 @@
             pl.BlockSpec((width, places), fixed),
             pl.BlockSpec((width, width), fixed),
         ],
-        out_specs=pl.BlockSpec((1, rows, width), tile),
+        out_specs=pl.BlockSpec(memory_space=pltpu.VMEM),
+        scratch_shapes=[
+            pltpu.VMEM((frames, n_dev, run, width), x.dtype),
+            pltpu.VMEM((n_dev, frames, run, width), x.dtype),
+            pltpu.SemaphoreType.DMA,
+            pltpu.SemaphoreType.DMA,
+        ],
+        compiler_params=pltpu.CompilerParams(collective_id=cid, has_side_effects=True),
     )(x, q, kt, vt, k0t, v0t, out_w)
 
 
@@ -243,7 +297,7 @@
     n_one = normed(xs, gain_one)
     q_one = project(n_one, query_one)
     n_zero = normed(x0, gain_one)
-    middle = spatial_attend(
+    got = spatial_attend(
         xs,
         q_one,
         transposed(n_one, key_one),
@@ -252,16 +306,12 @@
         transposed(n_zero, value_one),
         out_one,
         min(256, n_pos * places),
+        n_frame,
+        n_pos,
+        2,
     )
-
     all_places = n_pos * places
     run = all_places // (n_pos * n_frame)
-    sent = (
-        middle.reshape(per, n_pos, n_frame, run, width)
-        .transpose(2, 1, 0, 3, 4)
-        .reshape(n_frame * n_pos, per, run, width)
-    )
-    got = exchange(sent, ("frame", "pos"), (n_frame, n_pos), 2)
     mid_t = got.reshape(n_frame * n_pos * per, run, width)
 
     n_two = normed(mid_t, gain_two)

time: 166 us -> 155 us (0.934)
  Pallas kernels: 121 us -> 114 us
  local copies, waits for them, and re-layouts: 16.7 us -> 14.4 us
    pallas_call x2 -> x1, Pallas kernels: 43.8 us -> 23.8 us  [exchange(): pl.pallas_call(kernel, out_shape=jax.ShapeDtypeStruct(x.shape, x.dtype),...]
    pallas_call x1, Pallas kernels: 44.6 us -> 56.9 us  [spatial_attend(): pl.pallas_call(kernel, out_shape=jax.ShapeDtypeStruct((n_dev, frames, run...]
    reshape x1 -> x0, local copies, waits for them, and re-layouts: 2.29 us -> none  [shards(): middle.reshape(per, n_pos, n_frame, run, width).transpose(2, 1, 0, 3, 4)]
where the time goes in v4:
time: 155 us; the launch traced here: 153 us
  Pallas kernels  114 us (74%)
  matrix products  19.3 us (12%)
  local copies, waits for them, and re-layouts  14.4 us (9%)
  other arithmetic  5.4 us (3%)
    pallas_call x1, Pallas kernels, spatial_attend(): pl.pallas_call(kernel, out_shape=jax.ShapeDtypeStruct((n_dev, frames, run...  56.9 us
    pallas_call x1, Pallas kernels, spatial_exchange(): pl.pallas_call(kernel, out_shape=(jax.ShapeDtypeStruct(x.shape, x.dtype),...  33.1 us
    pallas_call x1, Pallas kernels, exchange(): pl.pallas_call(kernel, out_shape=jax.ShapeDtypeStruct(x.shape, x.dtype),...  23.8 us
    dot_general x1, matrix products, softmax_attend(): jnp.einsum(value_form, weights.astype(jnp.bfloat16), vals, preferred_elem...  5.93 us
    dot_general x4, matrix products, transposed(): jnp.einsum('...rc,cd->...dr', values, weight, preferred_element_type=jnp....  5.61 us
    another operation x3, local copies, waits for them, and re-layouts, heads_of(): values.reshape(values.shape[:-1] + (HEADS, values.shape[-1] // HEADS))  5.49 us
    dot_general x1, matrix products, softmax_attend(): jnp.einsum(score_form, query, keys, preferred_element_type=jnp.float32)  4.2 us

profile of v4, /device:TPU:1, one launch (start us, length us, event | category | flops | bytes accessed | tf_op | source)
XLA Modules:
  0.0 153.1 jit_solution(6229882556470671842)
XLA Ops:
  0.0 33.1 %shard_map.109 = (bf16[16,2,64,256]{3,2,1,0:T(8,128)(2,1)}, bf16[16,64,256]{2,1,0:T(8,128)(2,1)}) custom-call(bf16[16,2,64,256]{3,2,1,0:T(8,128)(2,1)} %bitcast.75), custom_call_target="tpu_custom_call" | custom-call | tf_op jit(solution)/shard_map/pallas_call | solution.py:123
  33.1 1.4 copy.68
  34.6 0.4 multiply_reduce_fusion.2
  35.1 1.7 %fusion.16.kt_ref = bf16[2,256,1024]{2,1,0:T(8,128)(2,1)} fusion(bf16[2,1024,256]{2,1,0:T(8,128)(2,1)S(1)} %bitcast.70, f32[256]{0:T(256)S(1)} %copy-done.12, f32[2,1024]{1,0:T(2,128)S(1)} %rsqrt.39, bf16[256,256]{1,0:T(8,128)(2,1)S(1)} %copy-done), kind=kOutput, calls=%fused_computation.30 | convolution fusion | flops 271056896 | bytes 2237440 | tf_op jit(solution)/shard_map/...rc,cd->...dr/dot_general | solution.py:245
  36.8 1.6 %fusion.17.vt_ref = bf16[2,256,1024]{2,1,0:T(8,128)(2,1)} fusion(bf16[2,1024,256]{2,1,0:T(8,128)(2,1)S(1)} %bitcast.71, f32[256]{0:T(256)S(1)} %copy-done.12, f32[2,1024]{1,0:T(2,128)S(1)} %rsqrt.39, bf16[256,256]{1,0:T(8,128)(2,1)S(1)} %copy-done.7), kind=kOutput, calls=%fused_computation.31 | convolution fusion | flops 271056896 | bytes 2237440 | tf_op jit(solution)/shard_map/...rc,cd->...dr/dot_general | solution.py:245
  38.5 0.3 bitcast_convert_fusion
  38.7 0.2 copy.69
  39.0 0.3 fusion.10
  39.3 0.5 copy-done.6
  39.9 1.4 convolution_convert_fusion.3
  41.6 0.2 fusion.21
  41.8 1.1 fusion.18.k0t_ref
  42.9 1.2 fusion.19.v0t_ref
  44.1 56.9 %shard_map.110 = bf16[128,2,8,256]{3,2,1,0:T(8,128)(2,1)} custom-call(bf16[2,1024,256]{2,1,0:T(8,128)(2,1)} %bitcast.72, bf16[2,1024,256]{2,1,0:T(8,128)(2,1)} %bitcast.73, bf16[2,256,1024]{2,1,0:T(8,128)(2,1)} %fusion.16.kt_ref, bf16[2,256,1024]{2,1,0:T(8,128)(2,1)} %fusion.17.vt_ref, bf16[256,1024]{1,0:T(8,128)(2,1)} %fusion.18.k0t_ref, ...), custom_call_target="tpu_custom_call" | custom-call | tf_op jit(solution)/shard_map/pallas_call | solution.py:220
  101.0 1.7 %multiply_reduce_fusion.1 = f32[128,2,8]{2,1,0:T(2,128)S(1)} fusion(bf16[128,2,8,256]{3,2,1,0:T(8,128)(2,1)} %shard_map.110), kind=kLoop, calls=%fused_computation.25 | loop fusion | flops 1570816 | bytes 1056768 | tf_op jit(solution)/shard_map/reduce_sum | solution.py:251
  103.1 0.3 fusion.8
  103.4 0.4 convolution_convert_fusion.1
  103.9 1.8 %reshape_reshape.10 = bf16[256,8,4,64]{3,2,1,0:T(4,128)(2,1)} reshape(bf16[2048,256]{1,0:T(8,128)(2,1)S(1)} %convolution_convert_fusion.1) | data formatting | bytes 2097152 | tf_op jit(solution)/shard_map/reshape;reshape | solution.py:262
  105.7 0.4 convolution_convert_fusion
  106.1 1.9 %reshape_reshape.11 = bf16[256,8,4,64]{3,2,1,0:T(4,128)(2,1)} reshape(bf16[2048,256]{1,0:T(8,128)(2,1)S(1)} %convolution_convert_fusion) | data formatting | bytes 2097152 | tf_op jit(solution)/shard_map/reshape;reshape | solution.py:262
  108.0 4.2 %multiply_reduce_fusion = (f32[8,4,256]{2,1,0:T(4,128)S(1)}, f32[8,4,256,256]{2,3,1,0:T(8,128)S(1)}) fusion(bf16[256,8,4,64]{3,2,1,0:T(4,128)(2,1)} %reshape_reshape.11, bf16[256,8,4,64]{3,2,1,0:T(4,128)(2,1)} %reshape_reshape.10), kind=kOutput, calls=%fused_computation.1 | convolution fusion | flops 272621568 | bytes 10518528 | tf_op jit(solution)/shard_map/fphd,kphd->phfk/dot_general | solution.py:267
  112.2 1.6 %fusion = f32[8,4,256]{2,1,0:T(4,128)S(1)} fusion(f32[8,4,256,256]{2,3,1,0:T(8,128)S(1)} %get-tuple-element.10, f32[8,4,256]{2,1,0:T(4,128)S(1)} %get-tuple-element.9), kind=kLoop, calls=%fused_computation.2 | loop fusion | flops 6283264 | bytes 8454144 | tf_op jit(solution)/shard_map/reduce_sum | solution.py:269
  113.8 1.6 %copy-done.1 = f32[8,4,256,256]{2,3,1,0:T(8,128)} copy-done((f32[8,4,256,256]{2,3,1,0:T(8,128)}, f32[8,4,256,256]{2,3,1,0:T(8,128)S(1)}, u32[]{:S(2)}) %copy-start.1) | copy-done | bytes 8388632
  115.4 0.4 convolution_convert_fusion.2
  115.9 1.8 %reshape_reshape.9 = bf16[256,8,4,64]{3,2,1,0:T(4,128)(2,1)} reshape(bf16[2048,256]{1,0:T(8,128)(2,1)S(1)} %convolution_convert_fusion.2) | data formatting | bytes 2097152 | tf_op jit(solution)/shard_map/reshape;reshape | solution.py:262
  117.7 5.9 %fusion.6 = bf16[256,8,4,64]{0,3,2,1:T(8,128)(2,1)S(1)} fusion(f32[256,8,4]{0,2,1:T(4,128)S(1)} %bitcast.77, f32[8,4,256,256]{2,3,1,0:T(8,128)} %copy-done.1, f32[8,4,256]{2,1,0:T(4,128)S(1)} %get-tuple-element.9, bf16[256,8,4,64]{3,2,1,0:T(4,128)(2,1)} %reshape_reshape.9), kind=kOutput, calls=%fused_computation.12 | convolution fusion | flops 275775488 | bytes 10551296 | tf_op jit(solution)/shard_map/phfk,kphd->fphd/dot_general | solution.py:270
  123.6 0.2 bitcast_convert_fusion.1
  123.9 0.7 copy-done.11
  124.5 0.9 fusion.11
  125.4 1.6 %copy.81 = bf16[256,8,256]{2,1,0:T(8,128)(2,1)} copy(bf16[256,8,256]{2,0,1:T(8,128)(2,1)S(1)} %fusion.11) | data formatting | bytes 2097152 | tf_op jit(solution)/shard_map/convert_element_type | solution.py:327
  127.0 23.8 %shard_map.111 = bf16[8,32,8,256]{3,2,1,0:T(8,128)(2,1)} custom-call(bf16[8,32,8,256]{3,2,1,0:T(8,128)(2,1)} %bitcast.74), custom_call_target="tpu_custom_call" | custom-call | tf_op jit(solution)/shard_map/pallas_call | solution.py:46
  150.8 2.3 %copy_bitcast_fusion = bf16[32,64,256]{2,1,0:T(8,128)(2,1)} fusion(bf16[8,32,8,256]{3,2,1,0:T(8,128)(2,1)} %shard_map.111), kind=kLoop, calls=%fused_computation.39 | loop fusion | bytes 2097152 | tf_op jit(solution)/shard_map/reshape | solution.py:331
  (33 shorter events, 0.9 us)
Async XLA Ops:
  0.0 35.1 %copy-start = (bf16[256,256]{1,0:T(8,128)(2,1)S(1)}, bf16[256,256]{1,0:T(8,128)(2,1)}, u32[]{:S(2)}) copy-start(bf16[256,256]{1,0:T(8,128)(2,1)} %param.14) | copy-start | bytes 393220
  0.0 35.1 %copy-start.12 = (f32[256]{0:T(256)S(1)}, f32[256]{0:T(256)}, u32[]{:S(2)}) copy-start(f32[256]{0:T(256)} %param.12) | copy-start | bytes 3076
  33.1 1.5 %copy-start.3 = (bf16[16,2,64,256]{3,2,1,0:T(8,128)(2,1)S(1)}, bf16[16,2,64,256]{3,2,1,0:T(8,128)(2,1)}, u32[]{:S(2)}) copy-start(bf16[16,2,64,256]{3,2,1,0:T(8,128)(2,1)} %get-tuple-element.7) | copy-start | bytes 3145732
  34.5 4.0 %copy-start.4 = (bf16[2,16,64,256]{3,2,1,0:T(8,128)(2,1)}, bf16[2,16,64,256]{3,2,1,0:T(8,128)(2,1)S(1)}, u32[]{:S(2)}) copy-start(bf16[2,16,64,256]{3,2,1,0:T(8,128)(2,1)S(1)} %copy.68) | copy-start | bytes 3145732
  34.5 2.3 %copy-start.7 = (bf16[256,256]{1,0:T(8,128)(2,1)S(1)}, bf16[256,256]{1,0:T(8,128)(2,1)}, u32[]{:S(2)}) copy-start(bf16[256,256]{1,0:T(8,128)(2,1)} %param.15) | copy-start | bytes 393220
  39.0 0.9 copy-start.6
  39.0 2.3 %copy-start.5 = (bf16[16,64,256]{2,1,0:T(8,128)(2,1)S(1)}, bf16[16,64,256]{2,1,0:T(8,128)(2,1)}, u32[]{:S(2)}) copy-start(bf16[16,64,256]{2,1,0:T(8,128)(2,1)} %get-tuple-element.8) | copy-start | bytes 1572868
  44.1 59.0 %copy-start.13 = (f32[256]{0:T(256)S(1)}, f32[256]{0:T(256)}, u32[]{:S(2)}) copy-start(f32[256]{0:T(256)} %param.17) | copy-start | bytes 3076
  101.0 2.1 %copy-start.2 = (bf16[128,2,8,256]{3,2,1,0:T(8,128)(2,1)S(1)}, bf16[128,2,8,256]{3,2,1,0:T(8,128)(2,1)}, u32[]{:S(2)}) copy-start(bf16[128,2,8,256]{3,2,1,0:T(8,128)(2,1)} %shard_map.110) | copy-start | bytes 3145732
  101.0 2.4 %copy-start.8 = (bf16[256,256]{1,0:T(8,128)(2,1)S(1)}, bf16[256,256]{1,0:T(8,128)(2,1)}, u32[]{:S(2)}) copy-start(bf16[256,256]{1,0:T(8,128)(2,1)} %param.18) | copy-start | bytes 393220
  103.9 1.8 %copy-start.9 = (bf16[256,256]{1,0:T(8,128)(2,1)S(1)}, bf16[256,256]{1,0:T(8,128)(2,1)}, u32[]{:S(2)}) copy-start(bf16[256,256]{1,0:T(8,128)(2,1)} %param.19) | copy-start | bytes 393220
  112.2 3.2 %copy-start.1 = (f32[8,4,256,256]{2,3,1,0:T(8,128)}, f32[8,4,256,256]{2,3,1,0:T(8,128)S(1)}, u32[]{:S(2)}) copy-start(f32[8,4,256,256]{2,3,1,0:T(8,128)S(1)} %get-tuple-element.10) | copy-start | bytes 25165828
  112.2 3.2 %copy-start.10 = (bf16[256,256]{1,0:T(8,128)(2,1)S(1)}, bf16[256,256]{1,0:T(8,128)(2,1)}, u32[]{:S(2)}) copy-start(bf16[256,256]{1,0:T(8,128)(2,1)} %param.20) | copy-start | bytes 393220
  123.6 0.9 copy-start.11

commit v5 on v4

--- a/solution.py
+++ b/solution.py
@@ -241,6 +241,90 @@
     )(x, q, kt, vt, k0t, v0t, out_w)
 
 
+def temporal_attend(x, gain, wq, wk, wv, out_w, n_frame, cid):
+    run, every, width = x.shape
+    depth = width // HEADS
+    scale = depth ** (-0.5)
+    frames = every // n_frame
+
+    def kernel(x_ref, g_ref, wq_ref, wk_ref, wv_ref, w_ref, o_ref, made, got, send_sem, recv_sem):
+        p = pl.program_id(0)
+        fi = lax.axis_index("frame")
+
+        @pl.when(p == 0)
+        def _():
+            barrier = pltpu.get_barrier_semaphore()
+            for k in range(1, n_frame):
+                pl.semaphore_signal(barrier, inc=1, device_id={"frame": (fi + k) % n_frame}, device_id_type=MESH)
+            pl.semaphore_wait(barrier, n_frame - 1)
+
+        wide = x_ref[0].astype(jnp.float32)
+        factor = lax.rsqrt(jnp.mean(wide * wide, axis=-1, keepdims=True) + 1e-06)
+        normed_two = (wide * factor * g_ref[...]).astype(jnp.bfloat16)
+        acc = wide
+        for h in range(HEADS):
+            qh = jnp.dot(normed_two, wq_ref[h], preferred_element_type=jnp.float32).astype(jnp.bfloat16)
+            kh = jnp.dot(normed_two, wk_ref[h], preferred_element_type=jnp.float32).astype(jnp.bfloat16)
+            vh = jnp.dot(normed_two, wv_ref[h], preferred_element_type=jnp.float32).astype(jnp.bfloat16)
+            contract = (((1,), (1,)), ((), ()))
+            scores = lax.dot_general(qh, kh, contract, preferred_element_type=jnp.float32) * scale
+            weights = jnp.exp(scores - jnp.max(scores, axis=-1, keepdims=True))
+            totals = jnp.sum(weights, axis=-1, keepdims=True)
+            summed = jnp.dot(weights.astype(jnp.bfloat16), vh, preferred_element_type=jnp.float32)
+            attended = (summed / totals).astype(jnp.bfloat16)
+            acc = acc + jnp.dot(attended, w_ref[pl.ds(h * depth, depth), :], preferred_element_type=jnp.float32)
+        made[p] = acc.astype(made.dtype)
+
+        for g in range(n_frame):
+            @pl.when(g == fi)
+            def _():
+                got[fi, p] = made[p, pl.ds(g * frames, frames)]
+
+            @pl.when(g != fi)
+            def _():
+                pltpu.make_async_remote_copy(
+                    src_ref=made.at[p, pl.ds(g * frames, frames)],
+                    dst_ref=got.at[fi, p],
+                    send_sem=send_sem,
+                    recv_sem=recv_sem,
+                    device_id={"frame": g},
+                    device_id_type=MESH,
+                ).start()
+
+        @pl.when(p == run - 1)
+        def _():
+            others = pltpu.make_async_copy(got.at[pl.ds(0, n_frame - 1)], got.at[pl.ds(1, n_frame - 1)], recv_sem)
+            others.wait()
+            sent = pltpu.make_async_copy(got.at[pl.ds(0, n_frame - 1)], got.at[pl.ds(1, n_frame - 1)], send_sem)
+            sent.wait()
+            o_ref[...] = got[...]
+
+    fixed = lambda p: (0, 0)
+    fixed3 = lambda p: (0, 0, 0)
+    split = lambda w: w.reshape(width, HEADS, depth).transpose(1, 0, 2)
+    return pl.pallas_call(
+        kernel,
+        out_shape=jax.ShapeDtypeStruct((n_frame, run, frames, width), x.dtype),
+        grid=(run,),
+        in_specs=[
+            pl.BlockSpec((1, every, width), lambda p: (p, 0, 0)),
+            pl.BlockSpec((1, width), fixed),
+            pl.BlockSpec((HEADS, width, depth), fixed3),
+            pl.BlockSpec((HEADS, width, depth), fixed3),
+            pl.BlockSpec((HEADS, width, depth), fixed3),
+            pl.BlockSpec((width, width), fixed),
+        ],
+        out_specs=pl.BlockSpec(memory_space=pltpu.VMEM),
+        scratch_shapes=[
+            pltpu.VMEM((run, every, width), x.dtype),
+            pltpu.VMEM((n_frame, run, frames, width), x.dtype),
+            pltpu.SemaphoreType.DMA,
+            pltpu.SemaphoreType.DMA,
+        ],
+        compiler_params=pltpu.CompilerParams(collective_id=cid, has_side_effects=True),
+    )(x, gain.reshape(1, width), split(wq), split(wk), split(wv), out_w)
+
+
 def transposed(values, weight):
     result = jnp.einsum("...rc,cd->...dr", values, weight, preferred_element_type=jnp.float32)
     return result.astype(jnp.bfloat16)
@@ -312,23 +396,9 @@
     )
     all_places = n_pos * places
     run = all_places // (n_pos * n_frame)
-    mid_t = got.reshape(n_frame * n_pos * per, run, width)
-
-    n_two = normed(mid_t, gain_two)
-    q_two = heads_of(project(n_two, query_two))
-    k_two = heads_of(project(n_two, key_two))
-    v_two = heads_of(project(n_two, value_two))
-    attended_two = softmax_attend(
-        q_two, k_two, v_two, "fphd,kphd->phfk", "phfk,kphd->fphd", "phf->fph"
-    ).reshape(mid_t.shape).astype(jnp.bfloat16)
-    mixed_two = jnp.dot(
-        attended_two.reshape(-1, width), out_two, preferred_element_type=jnp.float32
-    ).reshape(mid_t.shape)
-    decoded = (mid_t.astype(jnp.float32) + mixed_two).astype(jnp.bfloat16)
-
-    sent = decoded.reshape(n_frame, frames, run, width)
-    got = exchange(sent, ("frame",), (n_frame,), 3)
-    return got.transpose(1, 0, 2, 3).reshape(frames, places, width)
+    mid_t = got.reshape(n_frame * n_pos * per, run, width).transpose(1, 0, 2)
+    got = temporal_attend(mid_t, gain_two, query_two, key_two, value_two, out_two, n_frame, 3)
+    return got.transpose(2, 0, 1, 3).reshape(frames, places, width)
 
 
 def solution(mesh):

time: 155 us -> 145 us (0.935)
  matrix products: 19.3 us -> 7.03 us
  Pallas kernels: 114 us -> 124 us
  local copies, waits for them, and re-layouts: 14.4 us -> 10 us
  other arithmetic: 5.4 us -> 1.4 us
    dot_general x3 -> x0, matrix products: 11 us -> none  [the longest x1 5.93 us: softmax_attend(): jnp.einsum(value_form, weights.astype(jnp.bfloat16), vals, preferred_elem...]
    pallas_call x1, Pallas kernels: 23.8 us -> 34.5 us  [temporal_attend(): pl.pallas_call(kernel, out_shape=jax.ShapeDtypeStruct((n_frame, run, fram...]
    another operation x3 -> x0, local copies, waits for them, and re-layouts: 5.49 us -> none  [heads_of(): values.reshape(values.shape[:-1] + (HEADS, values.shape[-1] // HEADS))]
    reshape x1 -> x5, local copies, waits for them, and re-layouts: 2.32 us -> 7.74 us  [the longest x1 2.78 us: shards(): return got.transpose(2, 0, 1, 3).reshape(frames, places, width)]
    unnamed x28 -> x23, local copies, waits for them, and re-layouts: 2.99 us -> 0.57 us
    reduce_sum x3 -> x2, other arithmetic: 2.32 us -> 0.58 us  [normed(): factor = lax.rsqrt(jnp.mean(wide * wide, axis=-1, keepdims=True) + 1e-06)]
    reduce_sum x1 -> x0, other arithmetic: 1.59 us -> none  [softmax_attend(): totals = jnp.sum(weights, axis=-1)]
    convert_element_type x1 -> x0, local copies, waits for them, and re-layouts: 1.56 us -> none  [shards(): decoded = (mid_t.astype(jnp.float32) + mixed_two).astype(jnp.bfloat16)]
where the time goes in v5:
time: 145 us; the launch traced here: 143 us
  Pallas kernels  124 us (86%)
  local copies, waits for them, and re-layouts  10 us (7%)
  matrix products  7.03 us (5%)
    pallas_call x1, Pallas kernels, spatial_attend(): pl.pallas_call(kernel, out_shape=jax.ShapeDtypeStruct((n_dev, frames, run...  56.9 us
    pallas_call x1, Pallas kernels, temporal_attend(): pl.pallas_call(kernel, out_shape=jax.ShapeDtypeStruct((n_frame, run, fram...  34.5 us
    pallas_call x1, Pallas kernels, spatial_exchange(): pl.pallas_call(kernel, out_shape=(jax.ShapeDtypeStruct(x.shape, x.dtype),...  33.1 us
    dot_general x4, matrix products, transposed(): jnp.einsum('...rc,cd->...dr', values, weight, preferred_element_type=jnp....  5.62 us

profile of v5, /device:TPU:1, one launch (start us, length us, event | category | flops | bytes accessed | tf_op | source)
XLA Modules:
  0.0 143.1 jit_solution(15555836980848189714)
XLA Ops:
  0.0 33.1 %shard_map.109 = (bf16[16,2,64,256]{3,2,1,0:T(8,128)(2,1)}, bf16[16,64,256]{2,1,0:T(8,128)(2,1)}) custom-call(bf16[16,2,64,256]{3,2,1,0:T(8,128)(2,1)} %bitcast.60), custom_call_target="tpu_custom_call" | custom-call | tf_op jit(solution)/shard_map/pallas_call | solution.py:123
  33.1 1.4 copy.63
  34.5 0.1 copy-done.1
  34.6 0.3 bitcast_convert_fusion
  34.9 0.0 copy-start.9
  34.9 0.1 copy.64
  35.0 0.0 copy-start.4
  35.0 0.4 multiply_reduce_fusion
  35.4 0.1 rsqrt.27
  35.5 0.1 copy-done.9
  35.6 0.3 fusion.1
  35.9 0.0 copy-done.4
  35.9 1.4 convolution_convert_fusion
  37.4 0.1 rsqrt.28
  37.5 1.7 %fusion.2.kt_ref = bf16[2,256,1024]{2,1,0:T(8,128)(2,1)} fusion(bf16[2,1024,256]{2,1,0:T(8,128)(2,1)S(1)} %bitcast.53, f32[256]{0:T(256)S(1)} %copy-done.9, f32[2,1024]{1,0:T(2,128)S(1)} %rsqrt.28, bf16[256,256]{1,0:T(8,128)(2,1)S(1)} %copy-done), kind=kOutput, calls=%fused_computation.8 | convolution fusion | flops 271056896 | bytes 2237440 | tf_op jit(solution)/shard_map/...rc,cd->...dr/dot_general | solution.py:329
  39.1 1.6 %fusion.3.vt_ref = bf16[2,256,1024]{2,1,0:T(8,128)(2,1)} fusion(bf16[2,1024,256]{2,1,0:T(8,128)(2,1)S(1)} %bitcast.54, f32[256]{0:T(256)S(1)} %copy-done.9, f32[2,1024]{1,0:T(2,128)S(1)} %rsqrt.28, bf16[256,256]{1,0:T(8,128)(2,1)S(1)} %copy-done.5), kind=kOutput, calls=%fused_computation.9 | convolution fusion | flops 271056896 | bytes 2237440 | tf_op jit(solution)/shard_map/...rc,cd->...dr/dot_general | solution.py:329
  40.8 0.2 multiply_reduce_fusion.1
  41.0 0.1 rsqrt.30
  41.1 0.2 fusion.7
  41.3 1.2 fusion.4.k0t_ref
  42.4 1.2 fusion.5.v0t_ref
  43.6 56.9 %shard_map.110 = bf16[128,2,8,256]{3,2,1,0:T(8,128)(2,1)} custom-call(bf16[2,1024,256]{2,1,0:T(8,128)(2,1)} %bitcast.55, bf16[2,1024,256]{2,1,0:T(8,128)(2,1)} %bitcast.56, bf16[2,256,1024]{2,1,0:T(8,128)(2,1)} %fusion.2.kt_ref, bf16[2,256,1024]{2,1,0:T(8,128)(2,1)} %fusion.3.vt_ref, bf16[256,1024]{1,0:T(8,128)(2,1)} %fusion.4.k0t_ref, ...), custom_call_target="tpu_custom_call" | custom-call | tf_op jit(solution)/shard_map/pallas_call | solution.py:220
  100.5 0.0 copy-start.6
  100.5 2.5 %copy.89 = bf16[256,8,256]{2,0,1:T(8,128)(2,1)} copy(bf16[256,8,256]{2,1,0:T(8,128)(2,1)} %bitcast.57) | data formatting | bytes 2097152 | tf_op jit(solution)/shard_map/reshape | solution.py:399
  103.0 0.1 copy.71
  103.1 0.8 copy.72
  103.9 0.1 copy.73
  104.0 0.8 copy.74
  104.8 0.1 copy.75
  105.0 0.8 copy.76
  105.8 34.5 %shard_map.111 = bf16[8,8,32,256]{3,2,1,0:T(8,128)(2,1)} custom-call(bf16[8,256,256]{2,1,0:T(8,128)(2,1)} %bitcast.58, f32[1,256]{1,0:T(1,128)} %bitcast.67, bf16[4,256,64]{2,1,0:T(8,128)(2,1)} %bitcast.61, bf16[4,256,64]{2,1,0:T(8,128)(2,1)} %bitcast.62, bf16[4,256,64]{2,1,0:T(8,128)(2,1)} %bitcast.63, bf16[256,256]{1,0:T(8,128)(2,1)} %w_ref.3), custom_call_target="tpu_custom_call" | custom-call | tf_op jit(solution)/shard_map/pallas_call | solution.py:305
  140.3 2.8 %copy.77 = bf16[32,64,256]{2,1,0:T(8,128)(2,1)} copy(bf16[32,64,256]{2,0,1:T(8,128)(2,1)} %bitcast.59) | data formatting | bytes 2097152 | tf_op jit(solution)/shard_map/reshape | solution.py:401
  (16 shorter events, 0.1 us)
Async XLA Ops:
  0.0 37.4 %copy-start = (bf16[256,256]{1,0:T(8,128)(2,1)S(1)}, bf16[256,256]{1,0:T(8,128)(2,1)}, u32[]{:S(2)}) copy-start(bf16[256,256]{1,0:T(8,128)(2,1)} %param.14) | copy-start | bytes 393220
  33.1 1.5 %copy-start.1 = (bf16[16,2,64,256]{3,2,1,0:T(8,128)(2,1)S(1)}, bf16[16,2,64,256]{3,2,1,0:T(8,128)(2,1)}, u32[]{:S(2)}) copy-start(bf16[16,2,64,256]{3,2,1,0:T(8,128)(2,1)} %get-tuple-element.7) | copy-start | bytes 3145732
  34.5 4.7 %copy-start.2 = (bf16[2,16,64,256]{3,2,1,0:T(8,128)(2,1)}, bf16[2,16,64,256]{3,2,1,0:T(8,128)(2,1)S(1)}, u32[]{:S(2)}) copy-start(bf16[2,16,64,256]{3,2,1,0:T(8,128)(2,1)S(1)} %copy.63) | copy-start | bytes 3145732
  34.9 0.7 copy-start.9
  35.0 0.9 copy-start.4
  35.9 3.2 %copy-start.5 = (bf16[256,256]{1,0:T(8,128)(2,1)S(1)}, bf16[256,256]{1,0:T(8,128)(2,1)}, u32[]{:S(2)}) copy-start(bf16[256,256]{1,0:T(8,128)(2,1)} %param.15) | copy-start | bytes 393220
  37.4 3.3 %copy-start.3 = (bf16[16,64,256]{2,1,0:T(8,128)(2,1)S(1)}, bf16[16,64,256]{2,1,0:T(8,128)(2,1)}, u32[]{:S(2)}) copy-start(bf16[16,64,256]{2,1,0:T(8,128)(2,1)} %get-tuple-element.8) | copy-start | bytes 1572868
  100.5 2.5 %copy-start.6 = (bf16[256,256]{1,0:T(8,128)(2,1)S(1)}, bf16[256,256]{1,0:T(8,128)(2,1)}, u32[]{:S(2)}) copy-start(bf16[256,256]{1,0:T(8,128)(2,1)} %param.18) | copy-start | bytes 393220
  100.5 3.4 %copy-start.7 = (bf16[256,256]{1,0:T(8,128)(2,1)S(1)}, bf16[256,256]{1,0:T(8,128)(2,1)}, u32[]{:S(2)}) copy-start(bf16[256,256]{1,0:T(8,128)(2,1)} %param.19) | copy-start | bytes 393220
  100.5 4.4 %copy-start.8 = (bf16[256,256]{1,0:T(8,128)(2,1)S(1)}, bf16[256,256]{1,0:T(8,128)(2,1)}, u32[]{:S(2)}) copy-start(bf16[256,256]{1,0:T(8,128)(2,1)} %param.20) | copy-start | bytes 393220

commit v6 on v5

--- a/solution.py
+++ b/solution.py
@@ -150,42 +150,47 @@
     chunks = rows // run
 
     def kernel(x_ref, q_ref, kt_ref, vt_ref, k0t_ref, v0t_ref, w_ref, o_ref, made, got, send_sem, recv_sem):
-        f = pl.program_id(0)
-        t = pl.program_id(1)
+        t = pl.program_id(0)
         fi = lax.axis_index("frame")
         pi = lax.axis_index("pos")
         me = fi * n_pos + pi
-
-        @pl.when((f == 0) & (t == 0))
-        def _():
-            barrier = pltpu.get_barrier_semaphore()
+        barrier = pltpu.get_barrier_semaphore()
+
+        @pl.when(t == 0)
+        def _():
             for k in range(1, n_dev):
                 peer = (me + k) % n_dev
                 pl.semaphore_signal(
                     barrier, inc=1, device_id={"frame": peer // n_pos, "pos": peer % n_pos}, device_id_type=MESH
                 )
+
+        base = t * chunks
+        for f in range(frames):
+            acc = x_ref[f].astype(jnp.float32)
+            for h in range(HEADS):
+                part = pl.ds(h * depth, depth)
+                qh = q_ref[f, :, part]
+                own = jnp.dot(qh, kt_ref[f, part, :], preferred_element_type=jnp.float32) * scale
+                first = jnp.dot(qh, k0t_ref[part, :], preferred_element_type=jnp.float32) * scale
+                high = jnp.maximum(
+                    jnp.max(own, axis=-1, keepdims=True), jnp.max(first, axis=-1, keepdims=True)
+                )
+                own = jnp.exp(own - high)
+                first = jnp.exp(first - high)
+                totals = jnp.sum(own, axis=-1, keepdims=True) + jnp.sum(first, axis=-1, keepdims=True)
+                contract = (((1,), (1,)), ((), ()))
+                summed = lax.dot_general(
+                    own.astype(jnp.bfloat16), vt_ref[f, part, :], contract, preferred_element_type=jnp.float32
+                ) + lax.dot_general(
+                    first.astype(jnp.bfloat16), v0t_ref[part, :], contract, preferred_element_type=jnp.float32
+                )
+                attended = (summed / totals).astype(jnp.bfloat16)
+                acc = acc + jnp.dot(attended, w_ref[part, :], preferred_element_type=jnp.float32)
+            made[pl.ds(base, chunks), f] = acc.reshape(chunks, run, width).astype(made.dtype)
+
+        @pl.when(t == 0)
+        def _():
             pl.semaphore_wait(barrier, n_dev - 1)
-
-        acc = x_ref[0].astype(jnp.float32)
-        for h in range(HEADS):
-            part = pl.ds(h * depth, depth)
-            qh = q_ref[0, :, part]
-            own = jnp.dot(qh, kt_ref[0, part, :], preferred_element_type=jnp.float32) * scale
-            first = jnp.dot(qh, k0t_ref[part, :], preferred_element_type=jnp.float32) * scale
-            high = jnp.maximum(jnp.max(own, axis=-1, keepdims=True), jnp.max(first, axis=-1, keepdims=True))
-            own = jnp.exp(own - high)
-            first = jnp.exp(first - high)
-            totals = jnp.sum(own, axis=-1, keepdims=True) + jnp.sum(first, axis=-1, keepdims=True)
-            contract = (((1,), (1,)), ((), ()))
-            summed = lax.dot_general(
-                own.astype(jnp.bfloat16), vt_ref[0, part, :], contract, preferred_element_type=jnp.float32
-            ) + lax.dot_general(
-                first.astype(jnp.bfloat16), v0t_ref[part, :], contract, preferred_element_type=jnp.float32
-            )
-            attended = (summed / totals).astype(jnp.bfloat16)
-            acc = acc + jnp.dot(attended, w_ref[part, :], preferred_element_type=jnp.float32)
-        base = t * chunks
-        made[f, pl.ds(base, chunks)] = acc.reshape(chunks, run, width).astype(made.dtype)
 
         for i in range(chunks):
             gf = i % n_frame
@@ -193,20 +198,20 @@
 
             @pl.when((gf == fi) & (gp == pi))
             def _():
-                got[me, f] = made[f, base + i]
+                got[me] = made[base + i]
 
             @pl.when((gf != fi) | (gp != pi))
             def _():
                 pltpu.make_async_remote_copy(
-                    src_ref=made.at[f, base + i],
-                    dst_ref=got.at[me, f],
+                    src_ref=made.at[base + i],
+                    dst_ref=got.at[me],
                     send_sem=send_sem,
                     recv_sem=recv_sem,
                     device_id={"frame": gf, "pos": gp},
                     device_id_type=MESH,
                 ).start()
 
-        @pl.when((f == frames - 1) & (t == places // rows - 1))
+        @pl.when(t == places // rows - 1)
         def _():
             others = pltpu.make_async_copy(got.at[pl.ds(0, n_dev - 1)], got.at[pl.ds(1, n_dev - 1)], recv_sem)
             others.wait()
@@ -214,25 +219,25 @@
             sent.wait()
             o_ref[...] = got[...]
 
-    tile = lambda f, t: (f, t, 0)
-    whole = lambda f, t: (f, 0, 0)
-    fixed = lambda f, t: (0, 0)
+    tile = lambda t: (0, t, 0)
+    whole = lambda t: (0, 0, 0)
+    fixed = lambda t: (0, 0)
     return pl.pallas_call(
         kernel,
         out_shape=jax.ShapeDtypeStruct((n_dev, frames, run, width), x.dtype),
-        grid=(frames, places // rows),
+        grid=(places // rows,),
         in_specs=[
-            pl.BlockSpec((1, rows, width), tile),
-            pl.BlockSpec((1, rows, width), tile),
-            pl.BlockSpec((1, width, places), whole),
-            pl.BlockSpec((1, width, places), whole),
+            pl.BlockSpec((frames, rows, width), tile),
+            pl.BlockSpec((frames, rows, width), tile),
+            pl.BlockSpec((frames, width, places), whole),
+            pl.BlockSpec((frames, width, places), whole),
             pl.BlockSpec((width, places), fixed),
             pl.BlockSpec((width, places), fixed),
             pl.BlockSpec((width, width), fixed),
         ],
         out_specs=pl.BlockSpec(memory_space=pltpu.VMEM),
         scratch_shapes=[
-            pltpu.VMEM((frames, n_dev, run, width), x.dtype),
+            pltpu.VMEM((n_dev, frames, run, width), x.dtype),
             pltpu.VMEM((n_dev, frames, run, width), x.dtype),
             pltpu.SemaphoreType.DMA,
             pltpu.SemaphoreType.DMA,
@@ -251,12 +256,12 @@
         p = pl.program_id(0)
         fi = lax.axis_index("frame")
 
+        barrier = pltpu.get_barrier_semaphore()
+
         @pl.when(p == 0)
         def _():
-            barrier = pltpu.get_barrier_semaphore()
             for k in range(1, n_frame):
                 pl.semaphore_signal(barrier, inc=1, device_id={"frame": (fi + k) % n_frame}, device_id_type=MESH)
-            pl.semaphore_wait(barrier, n_frame - 1)
 
         wide = x_ref[0].astype(jnp.float32)
         factor = lax.rsqrt(jnp.mean(wide * wide, axis=-1, keepdims=True) + 1e-06)
@@ -274,6 +279,10 @@
             attended = (summed / totals).astype(jnp.bfloat16)
             acc = acc + jnp.dot(attended, w_ref[pl.ds(h * depth, depth), :], preferred_element_type=jnp.float32)
         made[p] = acc.astype(made.dtype)
+
+        @pl.when(p == 0)
+        def _():
+            pl.semaphore_wait(barrier, n_frame - 1)
 
         for g in range(n_frame):
             @pl.when(g == fi)

time: 145 us -> 136 us (0.938)
  Pallas kernels: 124 us -> 115 us
    pallas_call x1, Pallas kernels: 34.5 us -> 27.4 us  [temporal_attend(): pl.pallas_call(kernel, out_shape=jax.ShapeDtypeStruct((n_frame, run, fram...]
    pallas_call x1, Pallas kernels: 56.9 us -> 54.9 us  [spatial_attend(): pl.pallas_call(kernel, out_shape=jax.ShapeDtypeStruct((n_dev, frames, run...]
where the time goes in v6:
time: 136 us; the launch traced here: 134 us
  Pallas kernels  115 us (85%)
  local copies, waits for them, and re-layouts  10 us (7%)
  matrix products  7.03 us (5%)
  other arithmetic  1.4 us (1%)
    pallas_call x1, Pallas kernels, spatial_attend(): pl.pallas_call(kernel, out_shape=jax.ShapeDtypeStruct((n_dev, frames, run...  54.9 us
    pallas_call x1, Pallas kernels, spatial_exchange(): pl.pallas_call(kernel, out_shape=(jax.ShapeDtypeStruct(x.shape, x.dtype),...  33.1 us
    pallas_call x1, Pallas kernels, temporal_attend(): pl.pallas_call(kernel, out_shape=jax.ShapeDtypeStruct((n_frame, run, fram...  27.4 us
    dot_general x4, matrix products, transposed(): jnp.einsum('...rc,cd->...dr', values, weight, preferred_element_type=jnp....  5.62 us
    reshape x1, local copies, waits for them, and re-layouts, shards(): return got.transpose(2, 0, 1, 3).reshape(frames, places, width)  2.78 us

profile of v6, /device:TPU:1, one launch (start us, length us, event | category | flops | bytes accessed | tf_op | source)
XLA Modules:
  0.0 134.1 jit_solution(2657653372013165921)
XLA Ops:
  0.0 33.1 %shard_map.109 = (bf16[16,2,64,256]{3,2,1,0:T(8,128)(2,1)}, bf16[16,64,256]{2,1,0:T(8,128)(2,1)}) custom-call(bf16[16,2,64,256]{3,2,1,0:T(8,128)(2,1)} %bitcast.60), custom_call_target="tpu_custom_call" | custom-call | tf_op jit(solution)/shard_map/pallas_call | solution.py:123
  33.1 1.4 %copy.63 = bf16[2,16,64,256]{3,2,1,0:T(8,128)(2,1)S(1)} copy(bf16[2,16,64,256]{3,2,0,1:T(8,128)(2,1)} %bitcast.52) | data formatting | bytes 2097152 | tf_op jit(solution)/shard_map/transpose | solution.py:387
  34.5 0.1 copy-done.1
  34.6 0.3 bitcast_convert_fusion
  34.9 0.0 copy-start.9
  34.9 0.1 copy.64
  35.0 0.0 copy-start.4
  35.0 0.4 multiply_reduce_fusion
  35.4 0.1 rsqrt.27
  35.5 0.1 copy-done.9
  35.6 0.3 fusion.1
  35.9 0.0 copy-done.4
  35.9 1.4 %convolution_convert_fusion = bf16[2048,256]{1,0:T(8,128)(2,1)} fusion(bf16[2048,256]{1,0:T(8,128)(2,1)S(1)} %fusion.1, bf16[256,256]{1,0:T(8,128)(2,1)S(1)} %copy-done.4), kind=kOutput, calls=%fused_computation | convolution fusion | flops 268959744 | bytes 2228224 | tf_op jit(solution)/shard_map/dot_general | solution.py:350
  37.4 0.1 rsqrt.28
  37.5 1.7 %fusion.2.kt_ref = bf16[2,256,1024]{2,1,0:T(8,128)(2,1)} fusion(bf16[2,1024,256]{2,1,0:T(8,128)(2,1)S(1)} %bitcast.53, f32[256]{0:T(256)S(1)} %copy-done.9, f32[2,1024]{1,0:T(2,128)S(1)} %rsqrt.28, bf16[256,256]{1,0:T(8,128)(2,1)S(1)} %copy-done), kind=kOutput, calls=%fused_computation.8 | convolution fusion | flops 271056896 | bytes 2237440 | tf_op jit(solution)/shard_map/...rc,cd->...dr/dot_general | solution.py:338
  39.1 1.6 %fusion.3.vt_ref = bf16[2,256,1024]{2,1,0:T(8,128)(2,1)} fusion(bf16[2,1024,256]{2,1,0:T(8,128)(2,1)S(1)} %bitcast.54, f32[256]{0:T(256)S(1)} %copy-done.9, f32[2,1024]{1,0:T(2,128)S(1)} %rsqrt.28, bf16[256,256]{1,0:T(8,128)(2,1)S(1)} %copy-done.5), kind=kOutput, calls=%fused_computation.9 | convolution fusion | flops 271056896 | bytes 2237440 | tf_op jit(solution)/shard_map/...rc,cd->...dr/dot_general | solution.py:338
  40.8 0.2 multiply_reduce_fusion.1
  41.0 0.1 rsqrt.30
  41.1 0.2 fusion.7
  41.3 1.2 fusion.4.k0t_ref
  42.4 1.2 fusion.5.v0t_ref
  43.6 54.9 %shard_map.110 = bf16[128,2,8,256]{3,2,1,0:T(8,128)(2,1)} custom-call(bf16[2,1024,256]{2,1,0:T(8,128)(2,1)} %bitcast.55, bf16[2,1024,256]{2,1,0:T(8,128)(2,1)} %bitcast.56, bf16[2,256,1024]{2,1,0:T(8,128)(2,1)} %fusion.2.kt_ref, bf16[2,256,1024]{2,1,0:T(8,128)(2,1)} %fusion.3.vt_ref, bf16[256,1024]{1,0:T(8,128)(2,1)} %fusion.4.k0t_ref, ...), custom_call_target="tpu_custom_call" | custom-call | tf_op jit(solution)/shard_map/pallas_call | solution.py:225
  98.6 0.0 copy-start.8
  98.6 2.5 %copy.89 = bf16[256,8,256]{2,0,1:T(8,128)(2,1)} copy(bf16[256,8,256]{2,1,0:T(8,128)(2,1)} %bitcast.57) | data formatting | bytes 2097152 | tf_op jit(solution)/shard_map/reshape | solution.py:408
  101.0 0.1 copy.71
  101.1 0.8 copy.72
  102.0 0.1 copy.73
  102.1 0.8 copy.74
  102.9 0.1 copy.75
  103.0 0.8 copy.76
  103.9 27.4 %shard_map.111 = bf16[8,8,32,256]{3,2,1,0:T(8,128)(2,1)} custom-call(bf16[8,256,256]{2,1,0:T(8,128)(2,1)} %bitcast.58, f32[1,256]{1,0:T(1,128)} %bitcast.67, bf16[4,256,64]{2,1,0:T(8,128)(2,1)} %bitcast.61, bf16[4,256,64]{2,1,0:T(8,128)(2,1)} %bitcast.62, bf16[4,256,64]{2,1,0:T(8,128)(2,1)} %bitcast.63, bf16[256,256]{1,0:T(8,128)(2,1)} %w_ref.3), custom_call_target="tpu_custom_call" | custom-call | tf_op jit(solution)/shard_map/pallas_call | solution.py:314
  131.3 2.8 %copy.77 = bf16[32,64,256]{2,1,0:T(8,128)(2,1)} copy(bf16[32,64,256]{2,0,1:T(8,128)(2,1)} %bitcast.59) | data formatting | bytes 2097152 | tf_op jit(solution)/shard_map/reshape | solution.py:410
  (16 shorter events, 0.1 us)
Async XLA Ops:
  0.0 37.4 %copy-start = (bf16[256,256]{1,0:T(8,128)(2,1)S(1)}, bf16[256,256]{1,0:T(8,128)(2,1)}, u32[]{:S(2)}) copy-start(bf16[256,256]{1,0:T(8,128)(2,1)} %param.14) | copy-start | bytes 393220
  33.1 1.5 %copy-start.1 = (bf16[16,2,64,256]{3,2,1,0:T(8,128)(2,1)S(1)}, bf16[16,2,64,256]{3,2,1,0:T(8,128)(2,1)}, u32[]{:S(2)}) copy-start(bf16[16,2,64,256]{3,2,1,0:T(8,128)(2,1)} %get-tuple-element.7) | copy-start | bytes 3145732
  34.5 4.7 %copy-start.2 = (bf16[2,16,64,256]{3,2,1,0:T(8,128)(2,1)}, bf16[2,16,64,256]{3,2,1,0:T(8,128)(2,1)S(1)}, u32[]{:S(2)}) copy-start(bf16[2,16,64,256]{3,2,1,0:T(8,128)(2,1)S(1)} %copy.63) | copy-start | bytes 3145732
  34.9 0.7 copy-start.9
  35.0 0.9 copy-start.4
  35.9 3.2 %copy-start.5 = (bf16[256,256]{1,0:T(8,128)(2,1)S(1)}, bf16[256,256]{1,0:T(8,128)(2,1)}, u32[]{:S(2)}) copy-start(bf16[256,256]{1,0:T(8,128)(2,1)} %param.15) | copy-start | bytes 393220
  37.4 3.3 %copy-start.3 = (bf16[16,64,256]{2,1,0:T(8,128)(2,1)S(1)}, bf16[16,64,256]{2,1,0:T(8,128)(2,1)}, u32[]{:S(2)}) copy-start(bf16[16,64,256]{2,1,0:T(8,128)(2,1)} %get-tuple-element.8) | copy-start | bytes 1572868
  98.5 2.5 %copy-start.6 = (bf16[256,256]{1,0:T(8,128)(2,1)S(1)}, bf16[256,256]{1,0:T(8,128)(2,1)}, u32[]{:S(2)}) copy-start(bf16[256,256]{1,0:T(8,128)(2,1)} %param.18) | copy-start | bytes 393220
  98.5 3.4 %copy-start.7 = (bf16[256,256]{1,0:T(8,128)(2,1)S(1)}, bf16[256,256]{1,0:T(8,128)(2,1)}, u32[]{:S(2)}) copy-start(bf16[256,256]{1,0:T(8,128)(2,1)} %param.19) | copy-start | bytes 393220
  98.6 4.4 %copy-start.8 = (bf16[256,256]{1,0:T(8,128)(2,1)S(1)}, bf16[256,256]{1,0:T(8,128)(2,1)}, u32[]{:S(2)}) copy-start(bf16[256,256]{1,0:T(8,128)(2,1)} %param.20) | copy-start | bytes 393220

commit v7 on v6

--- a/solution.py
+++ b/solution.py
@@ -246,61 +246,63 @@
     )(x, q, kt, vt, k0t, v0t, out_w)
 
 
-def temporal_attend(x, gain, wq, wk, wv, out_w, n_frame, cid):
+def temporal_attend(x, gain, wq, wk, wv, out_w, n_frame, cid, per_step=2):
     run, every, width = x.shape
     depth = width // HEADS
     scale = depth ** (-0.5)
     frames = every // n_frame
 
     def kernel(x_ref, g_ref, wq_ref, wk_ref, wv_ref, w_ref, o_ref, made, got, send_sem, recv_sem):
-        p = pl.program_id(0)
+        step = pl.program_id(0)
         fi = lax.axis_index("frame")
-
         barrier = pltpu.get_barrier_semaphore()
 
-        @pl.when(p == 0)
+        @pl.when(step == 0)
         def _():
             for k in range(1, n_frame):
                 pl.semaphore_signal(barrier, inc=1, device_id={"frame": (fi + k) % n_frame}, device_id_type=MESH)
 
-        wide = x_ref[0].astype(jnp.float32)
-        factor = lax.rsqrt(jnp.mean(wide * wide, axis=-1, keepdims=True) + 1e-06)
-        normed_two = (wide * factor * g_ref[...]).astype(jnp.bfloat16)
-        acc = wide
-        for h in range(HEADS):
-            qh = jnp.dot(normed_two, wq_ref[h], preferred_element_type=jnp.float32).astype(jnp.bfloat16)
-            kh = jnp.dot(normed_two, wk_ref[h], preferred_element_type=jnp.float32).astype(jnp.bfloat16)
-            vh = jnp.dot(normed_two, wv_ref[h], preferred_element_type=jnp.float32).astype(jnp.bfloat16)
-            contract = (((1,), (1,)), ((), ()))
-            scores = lax.dot_general(qh, kh, contract, preferred_element_type=jnp.float32) * scale
-            weights = jnp.exp(scores - jnp.max(scores, axis=-1, keepdims=True))
-            totals = jnp.sum(weights, axis=-1, keepdims=True)
-            summed = jnp.dot(weights.astype(jnp.bfloat16), vh, preferred_element_type=jnp.float32)
-            attended = (summed / totals).astype(jnp.bfloat16)
-            acc = acc + jnp.dot(attended, w_ref[pl.ds(h * depth, depth), :], preferred_element_type=jnp.float32)
-        made[p] = acc.astype(made.dtype)
-
-        @pl.when(p == 0)
+        for s in range(per_step):
+            wide = x_ref[s].astype(jnp.float32)
+            factor = lax.rsqrt(jnp.mean(wide * wide, axis=-1, keepdims=True) + 1e-06)
+            normed_two = (wide * factor * g_ref[...]).astype(jnp.bfloat16)
+            q = jnp.dot(normed_two, wq_ref[...], preferred_element_type=jnp.float32).astype(jnp.bfloat16)
+            k = jnp.dot(normed_two, wk_ref[...], preferred_element_type=jnp.float32).astype(jnp.bfloat16)
+            v = jnp.dot(normed_two, wv_ref[...], preferred_element_type=jnp.float32).astype(jnp.bfloat16)
+            acc = wide
+            for h in range(HEADS):
+                part = slice(h * depth, (h + 1) * depth)
+                contract = (((1,), (1,)), ((), ()))
+                scores = lax.dot_general(q[:, part], k[:, part], contract, preferred_element_type=jnp.float32) * scale
+                weights = jnp.exp(scores - jnp.max(scores, axis=-1, keepdims=True))
+                totals = jnp.sum(weights, axis=-1, keepdims=True)
+                summed = jnp.dot(weights.astype(jnp.bfloat16), v[:, part], preferred_element_type=jnp.float32)
+                attended = (summed / totals).astype(jnp.bfloat16)
+                acc = acc + jnp.dot(attended, w_ref[part, :], preferred_element_type=jnp.float32)
+            made[step * per_step + s] = acc.astype(made.dtype)
+
+        @pl.when(step == 0)
         def _():
             pl.semaphore_wait(barrier, n_frame - 1)
 
+        these = pl.ds(step * per_step, per_step)
         for g in range(n_frame):
             @pl.when(g == fi)
             def _():
-                got[fi, p] = made[p, pl.ds(g * frames, frames)]
+                got[fi, these] = made[these, pl.ds(g * frames, frames)]
 
             @pl.when(g != fi)
             def _():
                 pltpu.make_async_remote_copy(
-                    src_ref=made.at[p, pl.ds(g * frames, frames)],
-                    dst_ref=got.at[fi, p],
+                    src_ref=made.at[these, pl.ds(g * frames, frames)],
+                    dst_ref=got.at[fi, these],
                     send_sem=send_sem,
                     recv_sem=recv_sem,
                     device_id={"frame": g},
                     device_id_type=MESH,
                 ).start()
 
-        @pl.when(p == run - 1)
+        @pl.when(step == run // per_step - 1)
         def _():
             others = pltpu.make_async_copy(got.at[pl.ds(0, n_frame - 1)], got.at[pl.ds(1, n_frame - 1)], recv_sem)
             others.wait()
@@ -309,18 +311,16 @@
             o_ref[...] = got[...]
 
     fixed = lambda p: (0, 0)
-    fixed3 = lambda p: (0, 0, 0)
-    split = lambda w: w.reshape(width, HEADS, depth).transpose(1, 0, 2)
     return pl.pallas_call(
         kernel,
         out_shape=jax.ShapeDtypeStruct((n_frame, run, frames, width), x.dtype),
-        grid=(run,),
+        grid=(run // per_step,),
         in_specs=[
-            pl.BlockSpec((1, every, width), lambda p: (p, 0, 0)),
+            pl.BlockSpec((per_step, every, width), lambda p: (p, 0, 0)),
             pl.BlockSpec((1, width), fixed),
-            pl.BlockSpec((HEADS, width, depth), fixed3),
-            pl.BlockSpec((HEADS, width, depth), fixed3),
-            pl.BlockSpec((HEADS, width, depth), fixed3),
+            pl.BlockSpec((width, width), fixed),
+            pl.BlockSpec((width, width), fixed),
+            pl.BlockSpec((width, width), fixed),
             pl.BlockSpec((width, width), fixed),
         ],
         out_specs=pl.BlockSpec(memory_space=pltpu.VMEM),
@@ -331,7 +331,7 @@
             pltpu.SemaphoreType.DMA,
         ],
         compiler_params=pltpu.CompilerParams(collective_id=cid, has_side_effects=True),
-    )(x, gain.reshape(1, width), split(wq), split(wk), split(wv), out_w)
+    )(x, gain.reshape(1, width), wq, wk, wv, out_w)
 
 
 def transposed(values, weight):

time: 136 us -> 124 us (0.912)
  the two profiles are of different devices: /device:TPU:1 before, /device:TPU:24 now
where the time goes in v7:
time: 124 us
  Pallas kernels  108 us (87%)
  local copies, waits for them, and re-layouts  7.18 us (6%)
  matrix products  7.03 us (6%)
  other arithmetic  1.4 us (1%)
    pallas_call x1, Pallas kernels, spatial_attend(): pl.pallas_call(kernel, out_shape=jax.ShapeDtypeStruct((n_dev, frames, run...  56.8 us
    pallas_call x1, Pallas kernels, spatial_exchange(): pl.pallas_call(kernel, out_shape=(jax.ShapeDtypeStruct(x.shape, x.dtype),...  30 us
    pallas_call x1, Pallas kernels, temporal_attend(): pl.pallas_call(kernel, out_shape=jax.ShapeDtypeStruct((n_frame, run, fram...  21.2 us
    dot_general x4, matrix products, transposed(): jnp.einsum('...rc,cd->...dr', values, weight, preferred_element_type=jnp....  5.63 us
    reshape x1, local copies, waits for them, and re-layouts, shards(): return got.transpose(2, 0, 1, 3).reshape(frames, places, width)  2.78 us

profile of v7, /device:TPU:24, one launch (start us, length us, event | category | flops | bytes accessed | tf_op | source)
XLA Modules:
  0.0 123.7 jit_solution(11155889872952043075)
XLA Ops:
  0.0 0.0 copy-start
  0.0 30.0 %shard_map.109 = (bf16[16,2,64,256]{3,2,1,0:T(8,128)(2,1)}, bf16[16,64,256]{2,1,0:T(8,128)(2,1)}) custom-call(bf16[16,2,64,256]{3,2,1,0:T(8,128)(2,1)} %bitcast.54), custom_call_target="tpu_custom_call" | custom-call | tf_op jit(solution)/shard_map/pallas_call | solution.py:123
  30.0 0.0 copy-start.1
  30.0 1.4 %copy.45 = bf16[2,16,64,256]{3,2,1,0:T(8,128)(2,1)S(1)} copy(bf16[2,16,64,256]{3,2,0,1:T(8,128)(2,1)} %bitcast.46) | data formatting | bytes 2097152 | tf_op jit(solution)/shard_map/transpose | solution.py:387
  31.4 0.0 copy-start.2
  31.4 0.1 copy-done.1
  31.5 0.3 bitcast_convert_fusion
  31.8 0.0 copy-start.6
  31.8 0.1 copy.46
  31.9 0.0 copy-start.4
  32.0 0.4 multiply_reduce_fusion
  32.3 0.1 rsqrt.27
  32.4 0.1 copy-done.6
  32.5 0.3 fusion.1
  32.8 0.0 copy-done.4
  32.9 1.4 %convolution_convert_fusion = bf16[2048,256]{1,0:T(8,128)(2,1)} fusion(bf16[2048,256]{1,0:T(8,128)(2,1)S(1)} %fusion.1, bf16[256,256]{1,0:T(8,128)(2,1)S(1)} %copy-done.4), kind=kOutput, calls=%fused_computation | convolution fusion | flops 268959744 | bytes 2228224 | tf_op jit(solution)/shard_map/dot_general | solution.py:350
  34.3 0.1 rsqrt.28
  34.3 0.0 copy-done
  34.3 0.0 copy-start.3
  34.4 1.7 %fusion.2.kt_ref = bf16[2,256,1024]{2,1,0:T(8,128)(2,1)} fusion(bf16[2,1024,256]{2,1,0:T(8,128)(2,1)S(1)} %bitcast.47, f32[256]{0:T(256)S(1)} %copy-done.6, f32[2,1024]{1,0:T(2,128)S(1)} %rsqrt.28, bf16[256,256]{1,0:T(8,128)(2,1)S(1)} %copy-done), kind=kOutput, calls=%fused_computation.8 | convolution fusion | flops 271056896 | bytes 2237440 | tf_op jit(solution)/shard_map/...rc,cd->...dr/dot_general | solution.py:338
  36.0 0.0 copy-done.2
  36.0 0.0 copy-done.5
  36.0 1.6 %fusion.3.vt_ref = bf16[2,256,1024]{2,1,0:T(8,128)(2,1)} fusion(bf16[2,1024,256]{2,1,0:T(8,128)(2,1)S(1)} %bitcast.48, f32[256]{0:T(256)S(1)} %copy-done.6, f32[2,1024]{1,0:T(2,128)S(1)} %rsqrt.28, bf16[256,256]{1,0:T(8,128)(2,1)S(1)} %copy-done.5), kind=kOutput, calls=%fused_computation.9 | convolution fusion | flops 271056896 | bytes 2237440 | tf_op jit(solution)/shard_map/...rc,cd->...dr/dot_general | solution.py:338
  37.7 0.2 multiply_reduce_fusion.1
  37.9 0.1 rsqrt.30
  38.0 0.2 fusion.7
  38.2 1.1 fusion.4.k0t_ref
  39.3 1.2 fusion.5.v0t_ref
  40.5 56.8 %shard_map.110 = bf16[128,2,8,256]{3,2,1,0:T(8,128)(2,1)} custom-call(bf16[2,1024,256]{2,1,0:T(8,128)(2,1)} %bitcast.49, bf16[2,1024,256]{2,1,0:T(8,128)(2,1)} %bitcast.50, bf16[2,256,1024]{2,1,0:T(8,128)(2,1)} %fusion.2.kt_ref, bf16[2,256,1024]{2,1,0:T(8,128)(2,1)} %fusion.3.vt_ref, bf16[256,1024]{1,0:T(8,128)(2,1)} %fusion.4.k0t_ref, ...), custom_call_target="tpu_custom_call" | custom-call | tf_op jit(solution)/shard_map/pallas_call | solution.py:225
  97.3 2.4 %copy.65 = bf16[256,8,256]{2,0,1:T(8,128)(2,1)} copy(bf16[256,8,256]{2,1,0:T(8,128)(2,1)} %bitcast.51) | data formatting | bytes 2097152 | tf_op jit(solution)/shard_map/reshape | solution.py:408
  99.7 21.2 %shard_map.111 = bf16[8,8,32,256]{3,2,1,0:T(8,128)(2,1)} custom-call(bf16[8,256,256]{2,1,0:T(8,128)(2,1)} %bitcast.52, f32[1,256]{1,0:T(1,128)} %bitcast.55, bf16[256,256]{1,0:T(8,128)(2,1)} %wq_ref.1, bf16[256,256]{1,0:T(8,128)(2,1)} %wk_ref.1, bf16[256,256]{1,0:T(8,128)(2,1)} %wv_ref.1, bf16[256,256]{1,0:T(8,128)(2,1)} %w_ref.3), custom_call_target="tpu_custom_call" | custom-call | tf_op jit(solution)/shard_map/pallas_call | solution.py:314
  120.9 2.8 %copy.53 = bf16[32,64,256]{2,1,0:T(8,128)(2,1)} copy(bf16[32,64,256]{2,0,1:T(8,128)(2,1)} %bitcast.53) | data formatting | bytes 2097152 | tf_op jit(solution)/shard_map/reshape | solution.py:410
  (4 shorter events, 0.0 us)
Async XLA Ops:
  0.0 34.3 %copy-start = (bf16[256,256]{1,0:T(8,128)(2,1)S(1)}, bf16[256,256]{1,0:T(8,128)(2,1)}, u32[]{:S(2)}) copy-start(bf16[256,256]{1,0:T(8,128)(2,1)} %param.14) | copy-start | bytes 393220
  30.0 1.5 %copy-start.1 = (bf16[16,2,64,256]{3,2,1,0:T(8,128)(2,1)S(1)}, bf16[16,2,64,256]{3,2,1,0:T(8,128)(2,1)}, u32[]{:S(2)}) copy-start(bf16[16,2,64,256]{3,2,1,0:T(8,128)(2,1)} %get-tuple-element.7) | copy-start | bytes 3145732
  31.4 4.6 %copy-start.2 = (bf16[2,16,64,256]{3,2,1,0:T(8,128)(2,1)}, bf16[2,16,64,256]{3,2,1,0:T(8,128)(2,1)S(1)}, u32[]{:S(2)}) copy-start(bf16[2,16,64,256]{3,2,1,0:T(8,128)(2,1)S(1)} %copy.45) | copy-start | bytes 3145732
  31.8 0.7 copy-start.6
  31.9 0.9 copy-start.4
  32.9 3.2 %copy-start.5 = (bf16[256,256]{1,0:T(8,128)(2,1)S(1)}, bf16[256,256]{1,0:T(8,128)(2,1)}, u32[]{:S(2)}) copy-start(bf16[256,256]{1,0:T(8,128)(2,1)} %param.15) | copy-start | bytes 393220
  34.3 3.3 %copy-start.3 = (bf16[16,64,256]{2,1,0:T(8,128)(2,1)S(1)}, bf16[16,64,256]{2,1,0:T(8,128)(2,1)}, u32[]{:S(2)}) copy-start(bf16[16,64,256]{2,1,0:T(8,128)(2,1)} %get-tuple-element.8) | copy-start | bytes 1572868

commit v8 on v7

--- a/solution.py
+++ b/solution.py
@@ -65,6 +65,21 @@
         for g in range(1, n_frame):
             pl.semaphore_signal(barrier, inc=1, device_id={"frame": (fi + g) % n_frame}, device_id_type=MESH)
         pl.semaphore_wait(barrier, n_pos - 1 + n_frame - 1)
+        def spread(g):
+            return pltpu.make_async_remote_copy(
+                src_ref=x_ref.at[0, 0],
+                dst_ref=z_ref.at[pi],
+                send_sem=fsend_sem.at[g],
+                recv_sem=frecv_sem,
+                device_id={"frame": g},
+                device_id_type=MESH,
+            )
+
+        @pl.when(fi == 0)
+        def _():
+            for g in range(1, n_frame):
+                spread(g).start()
+
         copies = []
         for k in range(1, n_pos):
             peer = (pi + k) % n_pos
@@ -78,28 +93,12 @@
             )
             copy.start()
             copies.append(copy)
-        o_ref[pi] = x_ref[pi]
-
-        def spread(g):
-            return pltpu.make_async_remote_copy(
-                src_ref=x_ref.at[0, 0],
-                dst_ref=z_ref.at[pi],
-                send_sem=fsend_sem.at[g],
-                recv_sem=frecv_sem,
-                device_id={"frame": g},
-                device_id_type=MESH,
-            )
 
         @pl.when(fi == 0)
         def _():
             local = pltpu.make_async_copy(x_ref.at[0, 0], z_ref.at[pi], local_sem)
             local.start()
-            sends = [spread(g) for g in range(1, n_frame)]
-            for send in sends:
-                send.start()
             local.wait()
-            for send in sends:
-                send.wait_send()
 
         @pl.when(fi != 0)
         def _():
@@ -117,8 +116,15 @@
             )
             copy.start()
             copies.append(copy)
+
+        @pl.when(fi == 0)
+        def _():
+            for g in range(1, n_frame):
+                spread(g).wait_send()
+
         for copy in copies:
             copy.wait()
+        o_ref[pi] = x_ref[pi]
 
     return pl.pallas_call(
         kernel,

time: 124 us -> 122 us (0.984)
  the two profiles are of different devices: /device:TPU:24 before, /device:TPU:1 now
where the time goes in v8:
time: 122 us; the launch traced here: 120 us
  Pallas kernels  105 us (86%)
  local copies, waits for them, and re-layouts  7.18 us (6%)
  matrix products  7.04 us (6%)
  other arithmetic  1.4 us (1%)
    pallas_call x1, Pallas kernels, spatial_attend(): pl.pallas_call(kernel, out_shape=jax.ShapeDtypeStruct((n_dev, frames, run...  53.9 us
    pallas_call x1, Pallas kernels, spatial_exchange(): pl.pallas_call(kernel, out_shape=(jax.ShapeDtypeStruct(x.shape, x.dtype),...  32.1 us
    pallas_call x1, Pallas kernels, temporal_attend(): pl.pallas_call(kernel, out_shape=jax.ShapeDtypeStruct((n_frame, run, fram...  18.7 us
    dot_general x4, matrix products, transposed(): jnp.einsum('...rc,cd->...dr', values, weight, preferred_element_type=jnp....  5.63 us
    reshape x1, local copies, waits for them, and re-layouts, shards(): return got.transpose(2, 0, 1, 3).reshape(frames, places, width)  2.78 us

profile of v8, /device:TPU:1, one launch (start us, length us, event | category | flops | bytes accessed | tf_op | source)
XLA Modules:
  0.0 120.4 jit_solution(13672280228885776167)
XLA Ops:
  0.0 0.0 copy-start
  0.0 32.1 %shard_map.109 = (bf16[16,2,64,256]{3,2,1,0:T(8,128)(2,1)}, bf16[16,64,256]{2,1,0:T(8,128)(2,1)}) custom-call(bf16[16,2,64,256]{3,2,1,0:T(8,128)(2,1)} %bitcast.54), custom_call_target="tpu_custom_call" | custom-call | tf_op jit(solution)/shard_map/pallas_call | solution.py:129
  32.1 0.0 copy-start.1
  32.1 1.4 %copy.45 = bf16[2,16,64,256]{3,2,1,0:T(8,128)(2,1)S(1)} copy(bf16[2,16,64,256]{3,2,0,1:T(8,128)(2,1)} %bitcast.46) | data formatting | bytes 2097152 | tf_op jit(solution)/shard_map/transpose | solution.py:393
  33.5 0.0 copy-start.2
  33.5 0.1 copy-done.1
  33.6 0.3 bitcast_convert_fusion
  33.9 0.0 copy-start.6
  33.9 0.1 copy.46
  34.1 0.0 copy-start.4
  34.1 0.4 multiply_reduce_fusion
  34.5 0.1 rsqrt.27
  34.5 0.1 copy-done.6
  34.6 0.3 fusion.1
  34.9 0.0 copy-done.4
  35.0 1.4 %convolution_convert_fusion = bf16[2048,256]{1,0:T(8,128)(2,1)} fusion(bf16[2048,256]{1,0:T(8,128)(2,1)S(1)} %fusion.1, bf16[256,256]{1,0:T(8,128)(2,1)S(1)} %copy-done.4), kind=kOutput, calls=%fused_computation | convolution fusion | flops 268959744 | bytes 2228224 | tf_op jit(solution)/shard_map/dot_general | solution.py:356
  36.4 0.1 rsqrt.28
  36.5 0.0 copy-done
  36.5 0.0 copy-start.3
  36.5 1.7 %fusion.2.kt_ref = bf16[2,256,1024]{2,1,0:T(8,128)(2,1)} fusion(bf16[2,1024,256]{2,1,0:T(8,128)(2,1)S(1)} %bitcast.47, f32[256]{0:T(256)S(1)} %copy-done.6, f32[2,1024]{1,0:T(2,128)S(1)} %rsqrt.28, bf16[256,256]{1,0:T(8,128)(2,1)S(1)} %copy-done), kind=kOutput, calls=%fused_computation.8 | convolution fusion | flops 271056896 | bytes 2237440 | tf_op jit(solution)/shard_map/...rc,cd->...dr/dot_general | solution.py:344
  38.1 0.0 copy-done.2
  38.1 0.0 copy-done.5
  38.2 1.6 %fusion.3.vt_ref = bf16[2,256,1024]{2,1,0:T(8,128)(2,1)} fusion(bf16[2,1024,256]{2,1,0:T(8,128)(2,1)S(1)} %bitcast.48, f32[256]{0:T(256)S(1)} %copy-done.6, f32[2,1024]{1,0:T(2,128)S(1)} %rsqrt.28, bf16[256,256]{1,0:T(8,128)(2,1)S(1)} %copy-done.5), kind=kOutput, calls=%fused_computation.9 | convolution fusion | flops 271056896 | bytes 2237440 | tf_op jit(solution)/shard_map/...rc,cd->...dr/dot_general | solution.py:344
  39.8 0.2 multiply_reduce_fusion.1
  40.0 0.1 rsqrt.30
  40.1 0.2 fusion.7
  40.3 1.1 fusion.4.k0t_ref
  41.5 1.2 fusion.5.v0t_ref
  42.6 53.9 %shard_map.110 = bf16[128,2,8,256]{3,2,1,0:T(8,128)(2,1)} custom-call(bf16[2,1024,256]{2,1,0:T(8,128)(2,1)} %bitcast.49, bf16[2,1024,256]{2,1,0:T(8,128)(2,1)} %bitcast.50, bf16[2,256,1024]{2,1,0:T(8,128)(2,1)} %fusion.2.kt_ref, bf16[2,256,1024]{2,1,0:T(8,128)(2,1)} %fusion.3.vt_ref, bf16[256,1024]{1,0:T(8,128)(2,1)} %fusion.4.k0t_ref, ...), custom_call_target="tpu_custom_call" | custom-call | tf_op jit(solution)/shard_map/pallas_call | solution.py:231
  96.5 2.4 %copy.65 = bf16[256,8,256]{2,0,1:T(8,128)(2,1)} copy(bf16[256,8,256]{2,1,0:T(8,128)(2,1)} %bitcast.51) | data formatting | bytes 2097152 | tf_op jit(solution)/shard_map/reshape | solution.py:414
  98.9 18.7 %shard_map.111 = bf16[8,8,32,256]{3,2,1,0:T(8,128)(2,1)} custom-call(bf16[8,256,256]{2,1,0:T(8,128)(2,1)} %bitcast.52, f32[1,256]{1,0:T(1,128)} %bitcast.55, bf16[256,256]{1,0:T(8,128)(2,1)} %wq_ref.1, bf16[256,256]{1,0:T(8,128)(2,1)} %wk_ref.1, bf16[256,256]{1,0:T(8,128)(2,1)} %wv_ref.1, bf16[256,256]{1,0:T(8,128)(2,1)} %w_ref.3), custom_call_target="tpu_custom_call" | custom-call | tf_op jit(solution)/shard_map/pallas_call | solution.py:320
  117.6 2.8 %copy.53 = bf16[32,64,256]{2,1,0:T(8,128)(2,1)} copy(bf16[32,64,256]{2,0,1:T(8,128)(2,1)} %bitcast.53) | data formatting | bytes 2097152 | tf_op jit(solution)/shard_map/reshape | solution.py:416
  (4 shorter events, 0.0 us)
Async XLA Ops:
  0.0 36.5 %copy-start = (bf16[256,256]{1,0:T(8,128)(2,1)S(1)}, bf16[256,256]{1,0:T(8,128)(2,1)}, u32[]{:S(2)}) copy-start(bf16[256,256]{1,0:T(8,128)(2,1)} %param.14) | copy-start | bytes 393220
  32.1 1.5 %copy-start.1 = (bf16[16,2,64,256]{3,2,1,0:T(8,128)(2,1)S(1)}, bf16[16,2,64,256]{3,2,1,0:T(8,128)(2,1)}, u32[]{:S(2)}) copy-start(bf16[16,2,64,256]{3,2,1,0:T(8,128)(2,1)} %get-tuple-element.7) | copy-start | bytes 3145732
  33.5 4.6 %copy-start.2 = (bf16[2,16,64,256]{3,2,1,0:T(8,128)(2,1)}, bf16[2,16,64,256]{3,2,1,0:T(8,128)(2,1)S(1)}, u32[]{:S(2)}) copy-start(bf16[2,16,64,256]{3,2,1,0:T(8,128)(2,1)S(1)} %copy.45) | copy-start | bytes 3145732
  33.9 0.7 copy-start.6
  34.1 0.9 copy-start.4
  35.0 3.2 %copy-start.5 = (bf16[256,256]{1,0:T(8,128)(2,1)S(1)}, bf16[256,256]{1,0:T(8,128)(2,1)}, u32[]{:S(2)}) copy-start(bf16[256,256]{1,0:T(8,128)(2,1)} %param.15) | copy-start | bytes 393220
  36.5 3.3 %copy-start.3 = (bf16[16,64,256]{2,1,0:T(8,128)(2,1)S(1)}, bf16[16,64,256]{2,1,0:T(8,128)(2,1)}, u32[]{:S(2)}) copy-start(bf16[16,64,256]{2,1,0:T(8,128)(2,1)} %get-tuple-element.8) | copy-start | bytes 1572868

commit v9 on v8

--- a/solution.py
+++ b/solution.py
@@ -154,6 +154,7 @@
     n_dev = n_frame * n_pos
     run = places // n_dev
     chunks = rows // run
+    n_tiles = places // rows
 
     def kernel(x_ref, q_ref, kt_ref, vt_ref, k0t_ref, v0t_ref, w_ref, o_ref, made, got, send_sem, recv_sem):
         t = pl.program_id(0)
@@ -170,12 +171,14 @@
                     barrier, inc=1, device_id={"frame": peer // n_pos, "pos": peer % n_pos}, device_id_type=MESH
                 )
 
-        base = t * chunks
+        tt = (t + fi + pi) % n_tiles
+        base = tt * chunks
+        these = pl.ds(pl.multiple_of(tt * rows, rows), rows)
         for f in range(frames):
-            acc = x_ref[f].astype(jnp.float32)
+            acc = x_ref[f, these, :].astype(jnp.float32)
             for h in range(HEADS):
                 part = pl.ds(h * depth, depth)
-                qh = q_ref[f, :, part]
+                qh = q_ref[f, these, part]
                 own = jnp.dot(qh, kt_ref[f, part, :], preferred_element_type=jnp.float32) * scale
                 first = jnp.dot(qh, k0t_ref[part, :], preferred_element_type=jnp.float32) * scale
                 high = jnp.maximum(
@@ -217,7 +220,7 @@
                     device_id_type=MESH,
                 ).start()
 
-        @pl.when(t == places // rows - 1)
+        @pl.when(t == n_tiles - 1)
         def _():
             others = pltpu.make_async_copy(got.at[pl.ds(0, n_dev - 1)], got.at[pl.ds(1, n_dev - 1)], recv_sem)
             others.wait()
@@ -225,16 +228,15 @@
             sent.wait()
             o_ref[...] = got[...]
 
-    tile = lambda t: (0, t, 0)
     whole = lambda t: (0, 0, 0)
     fixed = lambda t: (0, 0)
     return pl.pallas_call(
         kernel,
         out_shape=jax.ShapeDtypeStruct((n_dev, frames, run, width), x.dtype),
-        grid=(places // rows,),
+        grid=(n_tiles,),
         in_specs=[
-            pl.BlockSpec((frames, rows, width), tile),
-            pl.BlockSpec((frames, rows, width), tile),
+            pl.BlockSpec(memory_space=pltpu.VMEM),
+            pl.BlockSpec(memory_space=pltpu.VMEM),
             pl.BlockSpec((frames, width, places), whole),
             pl.BlockSpec((frames, width, places), whole),
             pl.BlockSpec((width, places), fixed),

time: 122 us -> 118 us (0.967)
  Pallas kernels: 105 us -> 101 us
    pallas_call x1, Pallas kernels: 53.9 us -> 49.7 us  [spatial_attend(): pl.pallas_call(kernel, out_shape=jax.ShapeDtypeStruct((n_dev, frames, run...]
where the time goes in v9:
time: 118 us; the launch traced here: 116 us
  Pallas kernels  101 us (86%)
  local copies, waits for them, and re-layouts  7.18 us (6%)
  matrix products  7.04 us (6%)
  other arithmetic  1.4 us (1%)
    pallas_call x1, Pallas kernels, spatial_attend(): pl.pallas_call(kernel, out_shape=jax.ShapeDtypeStruct((n_dev, frames, run...  49.7 us
    pallas_call x1, Pallas kernels, spatial_exchange(): pl.pallas_call(kernel, out_shape=(jax.ShapeDtypeStruct(x.shape, x.dtype),...  32.1 us
    pallas_call x1, Pallas kernels, temporal_attend(): pl.pallas_call(kernel, out_shape=jax.ShapeDtypeStruct((n_frame, run, fram...  18.9 us
    dot_general x4, matrix products, transposed(): jnp.einsum('...rc,cd->...dr', values, weight, preferred_element_type=jnp....  5.63 us
    reshape x1, local copies, waits for them, and re-layouts, shards(): return got.transpose(2, 0, 1, 3).reshape(frames, places, width)  2.78 us
    reshape x1, local copies, waits for them, and re-layouts, shards(): mid_t = got.reshape(n_frame * n_pos * per, run, width).transpose(1, 0, 2)  2.4 us

profile of v9, /device:TPU:1, one launch (start us, length us, event | category | flops | bytes accessed | tf_op | source)
XLA Modules:
  0.0 116.5 jit_solution(9770799164032581459)
XLA Ops:
  0.0 0.0 copy-start
  0.0 32.1 %shard_map.109 = (bf16[16,2,64,256]{3,2,1,0:T(8,128)(2,1)}, bf16[16,64,256]{2,1,0:T(8,128)(2,1)}) custom-call(bf16[16,2,64,256]{3,2,1,0:T(8,128)(2,1)} %bitcast.54), custom_call_target="tpu_custom_call" | custom-call | tf_op jit(solution)/shard_map/pallas_call | solution.py:129
  32.1 0.0 copy-start.1
  32.1 1.4 %copy.45 = bf16[2,16,64,256]{3,2,1,0:T(8,128)(2,1)S(1)} copy(bf16[2,16,64,256]{3,2,0,1:T(8,128)(2,1)} %bitcast.46) | data formatting | bytes 2097152 | tf_op jit(solution)/shard_map/transpose | solution.py:395
  33.5 0.0 copy-start.2
  33.5 0.1 copy-done.1
  33.6 0.3 bitcast_convert_fusion
  33.9 0.0 copy-start.6
  33.9 0.1 copy.46
  34.1 0.0 copy-start.4
  34.1 0.4 multiply_reduce_fusion
  34.5 0.1 rsqrt.27
  34.5 0.1 copy-done.6
  34.6 0.3 fusion.1
  34.9 0.0 copy-done.4
  35.0 1.4 %convolution_convert_fusion = bf16[2048,256]{1,0:T(8,128)(2,1)} fusion(bf16[2048,256]{1,0:T(8,128)(2,1)S(1)} %fusion.1, bf16[256,256]{1,0:T(8,128)(2,1)S(1)} %copy-done.4), kind=kOutput, calls=%fused_computation | convolution fusion | flops 268959744 | bytes 2228224 | tf_op jit(solution)/shard_map/dot_general | solution.py:358
  36.4 0.1 rsqrt.28
  36.5 0.0 copy-done
  36.5 0.0 copy-start.3
  36.5 1.7 %fusion.2.kt_ref = bf16[2,256,1024]{2,1,0:T(8,128)(2,1)} fusion(bf16[2,1024,256]{2,1,0:T(8,128)(2,1)S(1)} %bitcast.47, f32[256]{0:T(256)S(1)} %copy-done.6, f32[2,1024]{1,0:T(2,128)S(1)} %rsqrt.28, bf16[256,256]{1,0:T(8,128)(2,1)S(1)} %copy-done), kind=kOutput, calls=%fused_computation.8 | convolution fusion | flops 271056896 | bytes 2237440 | tf_op jit(solution)/shard_map/...rc,cd->...dr/dot_general | solution.py:346
  38.1 0.0 copy-done.2
  38.1 0.0 copy-done.5
  38.2 1.6 %fusion.3.vt_ref = bf16[2,256,1024]{2,1,0:T(8,128)(2,1)} fusion(bf16[2,1024,256]{2,1,0:T(8,128)(2,1)S(1)} %bitcast.48, f32[256]{0:T(256)S(1)} %copy-done.6, f32[2,1024]{1,0:T(2,128)S(1)} %rsqrt.28, bf16[256,256]{1,0:T(8,128)(2,1)S(1)} %copy-done.5), kind=kOutput, calls=%fused_computation.9 | convolution fusion | flops 271056896 | bytes 2237440 | tf_op jit(solution)/shard_map/...rc,cd->...dr/dot_general | solution.py:346
  39.8 0.2 multiply_reduce_fusion.1
  40.0 0.1 rsqrt.30
  40.1 0.2 fusion.7
  40.3 1.1 fusion.4.k0t_ref
  41.5 1.2 %fusion.5.v0t_ref = bf16[256,1024]{1,0:T(8,128)(2,1)} fusion(bf16[1024,256]{1,0:T(8,128)(2,1)S(1)} %fusion.7, bf16[256,256]{1,0:T(8,128)(2,1)S(1)} %copy-done.5), kind=kOutput, calls=%fused_computation.13 | convolution fusion | flops 134479872 | bytes 1179648 | tf_op jit(solution)/shard_map/...rc,cd->...dr/dot_general | solution.py:346
  42.6 49.7 %shard_map.110 = bf16[128,2,8,256]{3,2,1,0:T(8,128)(2,1)} custom-call(bf16[2,1024,256]{2,1,0:T(8,128)(2,1)} %bitcast.49, bf16[2,1024,256]{2,1,0:T(8,128)(2,1)} %bitcast.50, bf16[2,256,1024]{2,1,0:T(8,128)(2,1)} %fusion.2.kt_ref, bf16[2,256,1024]{2,1,0:T(8,128)(2,1)} %fusion.3.vt_ref, bf16[256,1024]{1,0:T(8,128)(2,1)} %fusion.4.k0t_ref, ...), custom_call_target="tpu_custom_call" | custom-call | tf_op jit(solution)/shard_map/pallas_call | solution.py:233
  92.3 2.4 %copy.65 = bf16[256,8,256]{2,0,1:T(8,128)(2,1)} copy(bf16[256,8,256]{2,1,0:T(8,128)(2,1)} %bitcast.51) | data formatting | bytes 2097152 | tf_op jit(solution)/shard_map/reshape | solution.py:416
  94.7 18.9 %shard_map.111 = bf16[8,8,32,256]{3,2,1,0:T(8,128)(2,1)} custom-call(bf16[8,256,256]{2,1,0:T(8,128)(2,1)} %bitcast.52, f32[1,256]{1,0:T(1,128)} %bitcast.55, bf16[256,256]{1,0:T(8,128)(2,1)} %wq_ref.1, bf16[256,256]{1,0:T(8,128)(2,1)} %wk_ref.1, bf16[256,256]{1,0:T(8,128)(2,1)} %wv_ref.1, bf16[256,256]{1,0:T(8,128)(2,1)} %w_ref.3), custom_call_target="tpu_custom_call" | custom-call | tf_op jit(solution)/shard_map/pallas_call | solution.py:322
  113.7 2.8 %copy.53 = bf16[32,64,256]{2,1,0:T(8,128)(2,1)} copy(bf16[32,64,256]{2,0,1:T(8,128)(2,1)} %bitcast.53) | data formatting | bytes 2097152 | tf_op jit(solution)/shard_map/reshape | solution.py:418
  (4 shorter events, 0.0 us)
Async XLA Ops:
  0.0 36.5 %copy-start = (bf16[256,256]{1,0:T(8,128)(2,1)S(1)}, bf16[256,256]{1,0:T(8,128)(2,1)}, u32[]{:S(2)}) copy-start(bf16[256,256]{1,0:T(8,128)(2,1)} %param.14) | copy-start | bytes 393220
  32.1 1.5 %copy-start.1 = (bf16[16,2,64,256]{3,2,1,0:T(8,128)(2,1)S(1)}, bf16[16,2,64,256]{3,2,1,0:T(8,128)(2,1)}, u32[]{:S(2)}) copy-start(bf16[16,2,64,256]{3,2,1,0:T(8,128)(2,1)} %get-tuple-element.7) | copy-start | bytes 3145732
  33.5 4.6 %copy-start.2 = (bf16[2,16,64,256]{3,2,1,0:T(8,128)(2,1)}, bf16[2,16,64,256]{3,2,1,0:T(8,128)(2,1)S(1)}, u32[]{:S(2)}) copy-start(bf16[2,16,64,256]{3,2,1,0:T(8,128)(2,1)S(1)} %copy.45) | copy-start | bytes 3145732
  33.9 0.7 copy-start.6
  34.1 0.9 copy-start.4
  35.0 3.2 %copy-start.5 = (bf16[256,256]{1,0:T(8,128)(2,1)S(1)}, bf16[256,256]{1,0:T(8,128)(2,1)}, u32[]{:S(2)}) copy-start(bf16[256,256]{1,0:T(8,128)(2,1)} %param.15) | copy-start | bytes 393220
  36.5 3.3 %copy-start.3 = (bf16[16,64,256]{2,1,0:T(8,128)(2,1)S(1)}, bf16[16,64,256]{2,1,0:T(8,128)(2,1)}, u32[]{:S(2)}) copy-start(bf16[16,64,256]{2,1,0:T(8,128)(2,1)} %get-tuple-element.8) | copy-start | bytes 1572868

commit v10 on v9

--- a/solution.py
+++ b/solution.py
@@ -147,21 +147,33 @@
     )(x)
 
 
-def spatial_attend(x, q, kt, vt, k0t, v0t, out_w, rows, n_frame, n_pos, cid):
-    frames, places, width = x.shape
+def spatial_attend(got_in, zero, gain, wq, wk, wv, out_w, rows, n_frame, n_pos, cid):
+    _, frames, slab, width = got_in.shape
+    places = n_pos * slab
     depth = width // HEADS
     scale = depth ** (-0.5)
     n_dev = n_frame * n_pos
     run = places // n_dev
     chunks = rows // run
     n_tiles = places // rows
-
-    def kernel(x_ref, q_ref, kt_ref, vt_ref, k0t_ref, v0t_ref, w_ref, o_ref, made, got, send_sem, recv_sem):
+    per_tile = rows // slab
+
+    def kernel(x_ref, z_ref, g_ref, wq_ref, wkt_ref, wvt_ref, w_ref, o_ref,
+               q_ref, kt_ref, vt_ref, k0t_ref, v0t_ref, made, got, send_sem, recv_sem):
         t = pl.program_id(0)
         fi = lax.axis_index("frame")
         pi = lax.axis_index("pos")
         me = fi * n_pos + pi
         barrier = pltpu.get_barrier_semaphore()
+        contract = (((1,), (1,)), ((), ()))
+
+        def normed_rows(values):
+            wide = values.reshape(places, width).astype(jnp.float32)
+            factor = lax.rsqrt(jnp.mean(wide * wide, axis=-1, keepdims=True) + 1e-06)
+            return (wide * factor * g_ref[...]).astype(jnp.bfloat16)
+
+        def channels_first(weight_t, values):
+            return lax.dot_general(weight_t, values, contract, preferred_element_type=jnp.float32).astype(jnp.bfloat16)
 
         @pl.when(t == 0)
         def _():
@@ -170,12 +182,20 @@
                 pl.semaphore_signal(
                     barrier, inc=1, device_id={"frame": peer // n_pos, "pos": peer % n_pos}, device_id_type=MESH
                 )
+            for f in range(frames):
+                normed_one = normed_rows(x_ref[:, f])
+                q_ref[f] = jnp.dot(normed_one, wq_ref[...], preferred_element_type=jnp.float32).astype(jnp.bfloat16)
+                kt_ref[f] = channels_first(wkt_ref[...], normed_one)
+                vt_ref[f] = channels_first(wvt_ref[...], normed_one)
+            normed_zero = normed_rows(z_ref[...])
+            k0t_ref[...] = channels_first(wkt_ref[...], normed_zero)
+            v0t_ref[...] = channels_first(wvt_ref[...], normed_zero)
 
         tt = (t + fi + pi) % n_tiles
         base = tt * chunks
         these = pl.ds(pl.multiple_of(tt * rows, rows), rows)
         for f in range(frames):
-            acc = x_ref[f, these, :].astype(jnp.float32)
+            acc = x_ref[pl.ds(tt * per_tile, per_tile), f].reshape(rows, width).astype(jnp.float32)
             for h in range(HEADS):
                 part = pl.ds(h * depth, depth)
                 qh = q_ref[f, these, part]
@@ -187,7 +207,6 @@
                 own = jnp.exp(own - high)
                 first = jnp.exp(first - high)
                 totals = jnp.sum(own, axis=-1, keepdims=True) + jnp.sum(first, axis=-1, keepdims=True)
-                contract = (((1,), (1,)), ((), ()))
                 summed = lax.dot_general(
                     own.astype(jnp.bfloat16), vt_ref[f, part, :], contract, preferred_element_type=jnp.float32
                 ) + lax.dot_general(
@@ -228,30 +247,35 @@
             sent.wait()
             o_ref[...] = got[...]
 
-    whole = lambda t: (0, 0, 0)
     fixed = lambda t: (0, 0)
+    dtype = got_in.dtype
     return pl.pallas_call(
         kernel,
-        out_shape=jax.ShapeDtypeStruct((n_dev, frames, run, width), x.dtype),
+        out_shape=jax.ShapeDtypeStruct((n_dev, frames, run, width), dtype),
         grid=(n_tiles,),
         in_specs=[
             pl.BlockSpec(memory_space=pltpu.VMEM),
             pl.BlockSpec(memory_space=pltpu.VMEM),
-            pl.BlockSpec((frames, width, places), whole),
-            pl.BlockSpec((frames, width, places), whole),
-            pl.BlockSpec((width, places), fixed),
-            pl.BlockSpec((width, places), fixed),
+            pl.BlockSpec((1, width), fixed),
+            pl.BlockSpec((width, width), fixed),
+            pl.BlockSpec((width, width), fixed),
+            pl.BlockSpec((width, width), fixed),
             pl.BlockSpec((width, width), fixed),
         ],
         out_specs=pl.BlockSpec(memory_space=pltpu.VMEM),
         scratch_shapes=[
-            pltpu.VMEM((n_dev, frames, run, width), x.dtype),
-            pltpu.VMEM((n_dev, frames, run, width), x.dtype),
+            pltpu.VMEM((frames, places, width), dtype),
+            pltpu.VMEM((frames, width, places), dtype),
+            pltpu.VMEM((frames, width, places), dtype),
+            pltpu.VMEM((width, places), dtype),
+            pltpu.VMEM((width, places), dtype),
+            pltpu.VMEM((n_dev, frames, run, width), dtype),
+            pltpu.VMEM((n_dev, frames, run, width), dtype),
             pltpu.SemaphoreType.DMA,
             pltpu.SemaphoreType.DMA,
         ],
         compiler_params=pltpu.CompilerParams(collective_id=cid, has_side_effects=True),
-    )(x, q, kt, vt, k0t, v0t, out_w)
+    )(got_in, zero, gain.reshape(1, width), wq, wk.T, wv.T, out_w)
 
 
 def temporal_attend(x, gain, wq, wk, wv, out_w, n_frame, cid, per_step=2):
@@ -392,24 +416,9 @@
     n_frame = lax.axis_size("frame")
     per = frames // n_pos
     got, zero = spatial_exchange(latents.reshape(n_pos, per, places, width), n_pos, n_frame, 1)
-    xs = got.transpose(1, 0, 2, 3).reshape(per, n_pos * places, width)
-    x0 = zero.reshape(n_pos * places, width)
-
-    n_one = normed(xs, gain_one)
-    q_one = project(n_one, query_one)
-    n_zero = normed(x0, gain_one)
     got = spatial_attend(
-        xs,
-        q_one,
-        transposed(n_one, key_one),
-        transposed(n_one, value_one),
-        transposed(n_zero, key_one),
-        transposed(n_zero, value_one),
-        out_one,
-        min(256, n_pos * places),
-        n_frame,
-        n_pos,
-        2,
+        got, zero, gain_one, query_one, key_one, value_one, out_one,
+        min(256, n_pos * places), n_frame, n_pos, 2,
     )
     all_places = n_pos * places
     run = all_places // (n_pos * n_frame)

time: 118 us -> 110 us (0.932)
  matrix products: 7.04 us -> 0 us
  other arithmetic: 1.4 us -> 0 us
    dot_general x5 -> x0, matrix products: 7.04 us -> none  [the longest x4 5.63 us: transposed(): jnp.einsum('...rc,cd->...dr', values, weight, preferred_element_type=jnp....]
    unnamed x14 -> x4, local copies, waits for them, and re-layouts: 0.25 us -> 2.45 us
    transpose x1 -> x0, local copies, waits for them, and re-layouts: 1.38 us -> none  [shards(): xs = got.transpose(1, 0, 2, 3).reshape(per, n_pos * places, width)]
where the time goes in v10:
time: 110 us; the launch traced here: 109 us
  Pallas kernels  101 us (92%)
  local copies, waits for them, and re-layouts  7.63 us (7%)
    pallas_call x1, Pallas kernels, spatial_attend(): pl.pallas_call(kernel, out_shape=jax.ShapeDtypeStruct((n_dev, frames, run...  50.4 us
    pallas_call x1, Pallas kernels, spatial_exchange(): pl.pallas_call(kernel, out_shape=(jax.ShapeDtypeStruct(x.shape, x.dtype),...  32 us
    pallas_call x1, Pallas kernels, temporal_attend(): pl.pallas_call(kernel, out_shape=jax.ShapeDtypeStruct((n_frame, run, fram...  18.9 us
    reshape x1, local copies, waits for them, and re-layouts, shards(): return got.transpose(2, 0, 1, 3).reshape(frames, places, width)  2.78 us
    unnamed x4, local copies, waits for them, and re-layouts  2.45 us
    reshape x1, local copies, waits for them, and re-layouts, shards(): mid_t = got.reshape(n_frame * n_pos * per, run, width).transpose(1, 0, 2)  2.4 us

profile of v10, /device:TPU:1, one launch (start us, length us, event | category | flops | bytes accessed | tf_op | source)
XLA Modules:
  0.0 109.0 jit_solution(15799282276702951031)
XLA Ops:
  0.0 0.0 copy-start
  0.0 1.7 %copy.12 = bf16[256,256]{0,1:T(8,128)(2,1)} copy(bf16[256,256]{1,0:T(8,128)(2,1)} %param.14) | data formatting | bytes 262144 | tf_op args[3]
  1.7 0.0 copy-done
  1.7 0.7 copy.13
  2.5 32.0 %shard_map.109 = (bf16[16,2,64,256]{3,2,1,0:T(8,128)(2,1)}, bf16[16,64,256]{2,1,0:T(8,128)(2,1)}) custom-call(bf16[16,2,64,256]{3,2,1,0:T(8,128)(2,1)} %bitcast.15), custom_call_target="tpu_custom_call" | custom-call | tf_op jit(solution)/shard_map/pallas_call | solution.py:129
  34.5 50.4 %shard_map.110 = bf16[128,2,8,256]{3,2,1,0:T(8,128)(2,1)} custom-call(bf16[16,2,64,256]{3,2,1,0:T(8,128)(2,1)} %get-tuple-element.7.x_ref, bf16[16,64,256]{2,1,0:T(8,128)(2,1)} %get-tuple-element.8.z_ref, f32[1,256]{1,0:T(1,128)} %bitcast.18, bf16[256,256]{1,0:T(8,128)(2,1)} %wq_ref.2, bf16[256,256]{1,0:T(8,128)(2,1)} %bitcast.16, ...), custom_call_target="tpu_custom_call" | custom-call | tf_op jit(solution)/shard_map/pallas_call | solution.py:252
  84.9 2.4 %copy.18 = bf16[256,8,256]{2,0,1:T(8,128)(2,1)} copy(bf16[256,8,256]{2,1,0:T(8,128)(2,1)} %bitcast.14) | data formatting | bytes 2097152 | tf_op jit(solution)/shard_map/reshape | solution.py:425
  87.3 18.9 %shard_map.111 = bf16[8,8,32,256]{3,2,1,0:T(8,128)(2,1)} custom-call(bf16[8,256,256]{2,1,0:T(8,128)(2,1)} %bitcast.12, f32[1,256]{1,0:T(1,128)} %bitcast.19, bf16[256,256]{1,0:T(8,128)(2,1)} %wq_ref.3, bf16[256,256]{1,0:T(8,128)(2,1)} %wk_ref.1, bf16[256,256]{1,0:T(8,128)(2,1)} %wv_ref.1, bf16[256,256]{1,0:T(8,128)(2,1)} %w_ref.3), custom_call_target="tpu_custom_call" | custom-call | tf_op jit(solution)/shard_map/pallas_call | solution.py:346
  106.2 2.8 %copy.15 = bf16[32,64,256]{2,1,0:T(8,128)(2,1)} copy(bf16[32,64,256]{2,0,1:T(8,128)(2,1)} %bitcast.13) | data formatting | bytes 2097152 | tf_op jit(solution)/shard_map/reshape | solution.py:427
Async XLA Ops:
  0.0 1.7 %copy-start = (bf16[256,256]{1,0:T(8,128)(2,1)S(1)}, bf16[256,256]{1,0:T(8,128)(2,1)}, u32[]{:S(2)}) copy-start(bf16[256,256]{1,0:T(8,128)(2,1)} %param.15) | copy-start | bytes 393220

commit v11 on v10

--- a/solution.py
+++ b/solution.py
@@ -182,14 +182,16 @@
                 pl.semaphore_signal(
                     barrier, inc=1, device_id={"frame": peer // n_pos, "pos": peer % n_pos}, device_id_type=MESH
                 )
+            wkt = wkt_ref[...].T
+            wvt = wvt_ref[...].T
             for f in range(frames):
                 normed_one = normed_rows(x_ref[:, f])
                 q_ref[f] = jnp.dot(normed_one, wq_ref[...], preferred_element_type=jnp.float32).astype(jnp.bfloat16)
-                kt_ref[f] = channels_first(wkt_ref[...], normed_one)
-                vt_ref[f] = channels_first(wvt_ref[...], normed_one)
+                kt_ref[f] = channels_first(wkt, normed_one)
+                vt_ref[f] = channels_first(wvt, normed_one)
             normed_zero = normed_rows(z_ref[...])
-            k0t_ref[...] = channels_first(wkt_ref[...], normed_zero)
-            v0t_ref[...] = channels_first(wvt_ref[...], normed_zero)
+            k0t_ref[...] = channels_first(wkt, normed_zero)
+            v0t_ref[...] = channels_first(wvt, normed_zero)
 
         tt = (t + fi + pi) % n_tiles
         base = tt * chunks
@@ -275,7 +277,7 @@
             pltpu.SemaphoreType.DMA,
         ],
         compiler_params=pltpu.CompilerParams(collective_id=cid, has_side_effects=True),
-    )(got_in, zero, gain.reshape(1, width), wq, wk.T, wv.T, out_w)
+    )(got_in, zero, gain.reshape(1, width), wq, wk, wv, out_w)
 
 
 def temporal_attend(x, gain, wq, wk, wv, out_w, n_frame, cid, per_step=2):

time: 110 us -> 108 us (0.982)
  local copies, waits for them, and re-layouts: 7.63 us -> 5.18 us
    unnamed x4 -> x0, local copies, waits for them, and re-layouts: 2.45 us -> none
where the time goes in v11:
time: 108 us; the launch traced here: 107 us
  Pallas kernels  101 us (94%)
  local copies, waits for them, and re-layouts  5.18 us (5%)
    pallas_call x1, Pallas kernels, spatial_attend(): pl.pallas_call(kernel, out_shape=jax.ShapeDtypeStruct((n_dev, frames, run...  50.4 us
    pallas_call x1, Pallas kernels, spatial_exchange(): pl.pallas_call(kernel, out_shape=(jax.ShapeDtypeStruct(x.shape, x.dtype),...  32.1 us
    pallas_call x1, Pallas kernels, temporal_attend(): pl.pallas_call(kernel, out_shape=jax.ShapeDtypeStruct((n_frame, run, fram...  19 us
    reshape x1, local copies, waits for them, and re-layouts, shards(): return got.transpose(2, 0, 1, 3).reshape(frames, places, width)  2.78 us
    reshape x1, local copies, waits for them, and re-layouts, shards(): mid_t = got.reshape(n_frame * n_pos * per, run, width).transpose(1, 0, 2)  2.4 us

profile of v11, /device:TPU:1, one launch (start us, length us, event | category | flops | bytes accessed | tf_op | source)
XLA Modules:
  0.0 106.6 jit_solution(11079327091827551675)
XLA Ops:
  0.0 32.1 %shard_map.109 = (bf16[16,2,64,256]{3,2,1,0:T(8,128)(2,1)}, bf16[16,64,256]{2,1,0:T(8,128)(2,1)}) custom-call(bf16[16,2,64,256]{3,2,1,0:T(8,128)(2,1)} %bitcast.13), custom_call_target="tpu_custom_call" | custom-call | tf_op jit(solution)/shard_map/pallas_call | solution.py:129
  32.1 50.4 %shard_map.110 = bf16[128,2,8,256]{3,2,1,0:T(8,128)(2,1)} custom-call(bf16[16,2,64,256]{3,2,1,0:T(8,128)(2,1)} %get-tuple-element.7.x_ref, bf16[16,64,256]{2,1,0:T(8,128)(2,1)} %get-tuple-element.8.z_ref, f32[1,256]{1,0:T(1,128)} %bitcast.14, bf16[256,256]{1,0:T(8,128)(2,1)} %wq_ref.2, bf16[256,256]{1,0:T(8,128)(2,1)} %wkt_ref.1, bf16[256,256]{1,0:T(8,128)(2,1)} %wvt_ref.1, ...), custom_call_target="tpu_custom_call" | custom-call | tf_op jit(solution)/shard_map/pallas_call | solution.py:254
  82.5 2.4 %copy.16 = bf16[256,8,256]{2,0,1:T(8,128)(2,1)} copy(bf16[256,8,256]{2,1,0:T(8,128)(2,1)} %bitcast.12) | data formatting | bytes 2097152 | tf_op jit(solution)/shard_map/reshape | solution.py:427
  84.9 19.0 %shard_map.111 = bf16[8,8,32,256]{3,2,1,0:T(8,128)(2,1)} custom-call(bf16[8,256,256]{2,1,0:T(8,128)(2,1)} %bitcast.10, f32[1,256]{1,0:T(1,128)} %bitcast.15, bf16[256,256]{1,0:T(8,128)(2,1)} %wq_ref.3, bf16[256,256]{1,0:T(8,128)(2,1)} %wk_ref.1, bf16[256,256]{1,0:T(8,128)(2,1)} %wv_ref.1, bf16[256,256]{1,0:T(8,128)(2,1)} %w_ref.3), custom_call_target="tpu_custom_call" | custom-call | tf_op jit(solution)/shard_map/pallas_call | solution.py:348
  103.9 2.8 %copy.13 = bf16[32,64,256]{2,1,0:T(8,128)(2,1)} copy(bf16[32,64,256]{2,0,1:T(8,128)(2,1)} %bitcast.11) | data formatting | bytes 2097152 | tf_op jit(solution)/shard_map/reshape | solution.py:429

commit v12 on v11

--- a/solution.py
+++ b/solution.py
@@ -280,30 +280,41 @@
     )(got_in, zero, gain.reshape(1, width), wq, wk, wv, out_w)
 
 
-def temporal_attend(x, gain, wq, wk, wv, out_w, n_frame, cid, per_step=2):
-    run, every, width = x.shape
+def temporal_attend(x, gain, wq, wk, wv, out_w, n_frame, cid):
+    every, run, width = x.shape
     depth = width // HEADS
     scale = depth ** (-0.5)
     frames = every // n_frame
-
-    def kernel(x_ref, g_ref, wq_ref, wk_ref, wv_ref, w_ref, o_ref, made, got, send_sem, recv_sem):
-        step = pl.program_id(0)
+    rows = every * run
+    lanes = width // 128
+
+    def kernel(x_ref, g_ref, wq_ref, wk_ref, wv_ref, w_ref, o_ref, xs, qs, ks, vs, made, got, send_sem, recv_sem):
         fi = lax.axis_index("frame")
         barrier = pltpu.get_barrier_semaphore()
-
-        @pl.when(step == 0)
-        def _():
-            for k in range(1, n_frame):
-                pl.semaphore_signal(barrier, inc=1, device_id={"frame": (fi + k) % n_frame}, device_id_type=MESH)
-
-        for s in range(per_step):
-            wide = x_ref[s].astype(jnp.float32)
-            factor = lax.rsqrt(jnp.mean(wide * wide, axis=-1, keepdims=True) + 1e-06)
-            normed_two = (wide * factor * g_ref[...]).astype(jnp.bfloat16)
-            q = jnp.dot(normed_two, wq_ref[...], preferred_element_type=jnp.float32).astype(jnp.bfloat16)
-            k = jnp.dot(normed_two, wk_ref[...], preferred_element_type=jnp.float32).astype(jnp.bfloat16)
-            v = jnp.dot(normed_two, wv_ref[...], preferred_element_type=jnp.float32).astype(jnp.bfloat16)
-            acc = wide
+        for k in range(1, n_frame):
+            pl.semaphore_signal(barrier, inc=1, device_id={"frame": (fi + k) % n_frame}, device_id_type=MESH)
+
+        wide = x_ref[...].astype(jnp.float32).reshape(rows, width)
+        factor = lax.rsqrt(jnp.mean(wide * wide, axis=-1, keepdims=True) + 1e-06)
+        normed_two = (wide * factor * g_ref[...]).astype(jnp.bfloat16)
+        def keep(ref, values):
+            for c in range(lanes):
+                ref[c] = values[:, c * 128 : (c + 1) * 128]
+
+        def gather(ref, p):
+            place = pl.ds(p, every, stride=run)
+            return jnp.concatenate([ref[c, place, :] for c in range(lanes)], axis=-1)
+
+        keep(xs, wide)
+        for ref, weight in ((qs, wq_ref), (ks, wk_ref), (vs, wv_ref)):
+            projected = jnp.dot(normed_two, weight[...], preferred_element_type=jnp.float32)
+            keep(ref, projected.astype(jnp.bfloat16).astype(jnp.float32))
+
+        for p in range(run):
+            q = gather(qs, p).astype(jnp.bfloat16)
+            k = gather(ks, p).astype(jnp.bfloat16)
+            v = gather(vs, p).astype(jnp.bfloat16)
+            acc = gather(xs, p)
             for h in range(HEADS):
                 part = slice(h * depth, (h + 1) * depth)
                 contract = (((1,), (1,)), ((), ()))
@@ -313,52 +324,42 @@
                 summed = jnp.dot(weights.astype(jnp.bfloat16), v[:, part], preferred_element_type=jnp.float32)
                 attended = (summed / totals).astype(jnp.bfloat16)
                 acc = acc + jnp.dot(attended, w_ref[part, :], preferred_element_type=jnp.float32)
-            made[step * per_step + s] = acc.astype(made.dtype)
-
-        @pl.when(step == 0)
-        def _():
-            pl.semaphore_wait(barrier, n_frame - 1)
-
-        these = pl.ds(step * per_step, per_step)
-        for g in range(n_frame):
-            @pl.when(g == fi)
-            def _():
-                got[fi, these] = made[these, pl.ds(g * frames, frames)]
-
-            @pl.when(g != fi)
-            def _():
-                pltpu.make_async_remote_copy(
-                    src_ref=made.at[these, pl.ds(g * frames, frames)],
-                    dst_ref=got.at[fi, these],
-                    send_sem=send_sem,
-                    recv_sem=recv_sem,
-                    device_id={"frame": g},
-                    device_id_type=MESH,
-                ).start()
-
-        @pl.when(step == run // per_step - 1)
-        def _():
-            others = pltpu.make_async_copy(got.at[pl.ds(0, n_frame - 1)], got.at[pl.ds(1, n_frame - 1)], recv_sem)
-            others.wait()
-            sent = pltpu.make_async_copy(got.at[pl.ds(0, n_frame - 1)], got.at[pl.ds(1, n_frame - 1)], send_sem)
-            sent.wait()
-            o_ref[...] = got[...]
-
-    fixed = lambda p: (0, 0)
+            made[p] = acc.astype(made.dtype)
+            if p == 0:
+                pl.semaphore_wait(barrier, n_frame - 1)
+            for g in range(n_frame):
+                @pl.when(g == fi)
+                def _():
+                    got[fi, p] = made[p, pl.ds(g * frames, frames)]
+
+                @pl.when(g != fi)
+                def _():
+                    pltpu.make_async_remote_copy(
+                        src_ref=made.at[p, pl.ds(g * frames, frames)],
+                        dst_ref=got.at[fi, p],
+                        send_sem=send_sem,
+                        recv_sem=recv_sem,
+                        device_id={"frame": g},
+                        device_id_type=MESH,
+                    ).start()
+
+        others = pltpu.make_async_copy(got.at[pl.ds(0, n_frame - 1)], got.at[pl.ds(1, n_frame - 1)], recv_sem)
+        others.wait()
+        sent = pltpu.make_async_copy(got.at[pl.ds(0, n_frame - 1)], got.at[pl.ds(1, n_frame - 1)], send_sem)
+        sent.wait()
+        o_ref[...] = got[...]
+
+    vmem = pl.BlockSpec(memory_space=pltpu.VMEM)
     return pl.pallas_call(
         kernel,
         out_shape=jax.ShapeDtypeStruct((n_frame, run, frames, width), x.dtype),
-        grid=(run // per_step,),
-        in_specs=[
-            pl.BlockSpec((per_step, every, width), lambda p: (p, 0, 0)),
-            pl.BlockSpec((1, width), fixed),
-            pl.BlockSpec((width, width), fixed),
-            pl.BlockSpec((width, width), fixed),
-            pl.BlockSpec((width, width), fixed),
-            pl.BlockSpec((width, width), fixed),
-        ],
-        out_specs=pl.BlockSpec(memory_space=pltpu.VMEM),
+        in_specs=[vmem] * 6,
+        out_specs=vmem,
         scratch_shapes=[
+            pltpu.VMEM((lanes, rows, 128), jnp.float32),
+            pltpu.VMEM((lanes, rows, 128), jnp.float32),
+            pltpu.VMEM((lanes, rows, 128), jnp.float32),
+            pltpu.VMEM((lanes, rows, 128), jnp.float32),
             pltpu.VMEM((run, every, width), x.dtype),
             pltpu.VMEM((n_frame, run, frames, width), x.dtype),
             pltpu.SemaphoreType.DMA,
@@ -424,7 +425,7 @@
     )
     all_places = n_pos * places
     run = all_places // (n_pos * n_frame)
-    mid_t = got.reshape(n_frame * n_pos * per, run, width).transpose(1, 0, 2)
+    mid_t = got.reshape(n_frame * n_pos * per, run, width)
     got = temporal_attend(mid_t, gain_two, query_two, key_two, value_two, out_two, n_frame, 3)
     return got.transpose(2, 0, 1, 3).reshape(frames, places, width)
 

time: 108 us -> 106 us (0.981)
  local copies, waits for them, and re-layouts: 5.18 us -> 2.78 us
    reshape x1 -> x0, local copies, waits for them, and re-layouts: 2.4 us -> none  [shards(): mid_t = got.reshape(n_frame * n_pos * per, run, width).transpose(1, 0, 2)]
where the time goes in v12:
time: 106 us; the launch traced here: 105 us
  Pallas kernels  102 us (96%)
  local copies, waits for them, and re-layouts  2.78 us (3%)
    pallas_call x1, Pallas kernels, spatial_attend(): pl.pallas_call(kernel, out_shape=jax.ShapeDtypeStruct((n_dev, frames, run...  50.4 us
    pallas_call x1, Pallas kernels, spatial_exchange(): pl.pallas_call(kernel, out_shape=(jax.ShapeDtypeStruct(x.shape, x.dtype),...  32.1 us
    pallas_call x1, Pallas kernels, temporal_attend(): pl.pallas_call(kernel, out_shape=jax.ShapeDtypeStruct((n_frame, run, fram...  19.5 us
    reshape x1, local copies, waits for them, and re-layouts, shards(): return got.transpose(2, 0, 1, 3).reshape(frames, places, width)  2.78 us

profile of v12, /device:TPU:1, one launch (start us, length us, event | category | flops | bytes accessed | tf_op | source)
XLA Modules:
  0.0 104.8 jit_solution(9878371165741313323)
XLA Ops:
  0.0 32.1 %shard_map.109 = (bf16[16,2,64,256]{3,2,1,0:T(8,128)(2,1)}, bf16[16,64,256]{2,1,0:T(8,128)(2,1)}) custom-call(bf16[16,2,64,256]{3,2,1,0:T(8,128)(2,1)} %bitcast.9), custom_call_target="tpu_custom_call" | custom-call | tf_op jit(solution)/shard_map/pallas_call | solution.py:129
  32.1 50.4 %shard_map.110 = bf16[128,2,8,256]{3,2,1,0:T(8,128)(2,1)} custom-call(bf16[16,2,64,256]{3,2,1,0:T(8,128)(2,1)} %get-tuple-element.7.x_ref, bf16[16,64,256]{2,1,0:T(8,128)(2,1)} %get-tuple-element.8.z_ref, f32[1,256]{1,0:T(1,128)} %bitcast.10, bf16[256,256]{1,0:T(8,128)(2,1)} %wq_ref.2, bf16[256,256]{1,0:T(8,128)(2,1)} %wkt_ref.1, bf16[256,256]{1,0:T(8,128)(2,1)} %wvt_ref.1, ...), custom_call_target="tpu_custom_call" | custom-call | tf_op jit(solution)/shard_map/pallas_call | solution.py:254
  82.5 19.5 %shard_map.111 = bf16[8,8,32,256]{3,2,1,0:T(8,128)(2,1)} custom-call(bf16[256,8,256]{2,1,0:T(8,128)(2,1)} %bitcast.7, f32[1,256]{1,0:T(1,128)} %bitcast.11, bf16[256,256]{1,0:T(8,128)(2,1)} %wq_ref.3, bf16[256,256]{1,0:T(8,128)(2,1)} %wk_ref.1, bf16[256,256]{1,0:T(8,128)(2,1)} %wv_ref.1, bf16[256,256]{1,0:T(8,128)(2,1)} %w_ref.3), custom_call_target="tpu_custom_call" | custom-call | tf_op jit(solution)/shard_map/pallas_call | solution.py:353
  102.0 2.8 %copy.12 = bf16[32,64,256]{2,1,0:T(8,128)(2,1)} copy(bf16[32,64,256]{2,0,1:T(8,128)(2,1)} %bitcast.8) | data formatting | bytes 2097152 | tf_op jit(solution)/shard_map/reshape | solution.py:430

commit v13 on v12

--- a/solution.py
+++ b/solution.py
@@ -347,12 +347,18 @@
         others.wait()
         sent = pltpu.make_async_copy(got.at[pl.ds(0, n_frame - 1)], got.at[pl.ds(1, n_frame - 1)], send_sem)
         sent.wait()
-        o_ref[...] = got[...]
+        for g in range(n_frame):
+            for p in range(run):
+                block = got[g, p].astype(jnp.float32)
+                for c in range(lanes):
+                    xs[c, pl.ds(g * run + p, frames, stride=n_frame * run), :] = block[:, c * 128 : (c + 1) * 128]
+        whole = jnp.concatenate([xs[c, pl.ds(0, frames * n_frame * run), :] for c in range(lanes)], axis=-1)
+        o_ref[...] = whole.astype(o_ref.dtype).reshape(frames, n_frame * run, width)
 
     vmem = pl.BlockSpec(memory_space=pltpu.VMEM)
     return pl.pallas_call(
         kernel,
-        out_shape=jax.ShapeDtypeStruct((n_frame, run, frames, width), x.dtype),
+        out_shape=jax.ShapeDtypeStruct((frames, n_frame * run, width), x.dtype),
         in_specs=[vmem] * 6,
         out_specs=vmem,
         scratch_shapes=[
@@ -426,8 +432,7 @@
     all_places = n_pos * places
     run = all_places // (n_pos * n_frame)
     mid_t = got.reshape(n_frame * n_pos * per, run, width)
-    got = temporal_attend(mid_t, gain_two, query_two, key_two, value_two, out_two, n_frame, 3)
-    return got.transpose(2, 0, 1, 3).reshape(frames, places, width)
+    return temporal_attend(mid_t, gain_two, query_two, key_two, value_two, out_two, n_frame, 3)
 
 
 def solution(mesh):

time: 106 us -> 108 us (1.019)
  Pallas kernels: 102 us -> 104 us
    reshape x1 -> x0, local copies, waits for them, and re-layouts: 2.78 us -> none  [shards(): return got.transpose(2, 0, 1, 3).reshape(frames, places, width)]
    unnamed x0 -> x1, local copies, waits for them, and re-layouts: none -> 2.3 us
    pallas_call x1, Pallas kernels: 19.5 us -> 21.6 us  [temporal_attend(): pl.pallas_call(kernel, out_shape=jax.ShapeDtypeStruct((frames, n_frame *...]
where the time goes in v13:
time: 108 us; the launch traced here: 106 us
  Pallas kernels  104 us (96%)
  local copies, waits for them, and re-layouts  2.3 us (2%)
    pallas_call x1, Pallas kernels, spatial_attend(): pl.pallas_call(kernel, out_shape=jax.ShapeDtypeStruct((n_dev, frames, run...  50.4 us
    pallas_call x1, Pallas kernels, spatial_exchange(): pl.pallas_call(kernel, out_shape=(jax.ShapeDtypeStruct(x.shape, x.dtype),...  32.1 us
    pallas_call x1, Pallas kernels, temporal_attend(): pl.pallas_call(kernel, out_shape=jax.ShapeDtypeStruct((frames, n_frame *...  21.6 us
    unnamed x1, local copies, waits for them, and re-layouts  2.3 us

profile of v13, /device:TPU:1, one launch (start us, length us, event | category | flops | bytes accessed | tf_op | source)
XLA Modules:
  0.0 106.4 jit_solution(1080712879823668920)
XLA Ops:
  0.0 32.1 %shard_map.109 = (bf16[16,2,64,256]{3,2,1,0:T(8,128)(2,1)}, bf16[16,64,256]{2,1,0:T(8,128)(2,1)}) custom-call(bf16[16,2,64,256]{3,2,1,0:T(8,128)(2,1)} %bitcast.5), custom_call_target="tpu_custom_call" | custom-call | tf_op jit(solution)/shard_map/pallas_call | solution.py:129
  32.1 50.4 %shard_map.110 = bf16[128,2,8,256]{3,2,1,0:T(8,128)(2,1)} custom-call(bf16[16,2,64,256]{3,2,1,0:T(8,128)(2,1)} %get-tuple-element.7.x_ref, bf16[16,64,256]{2,1,0:T(8,128)(2,1)} %get-tuple-element.8.z_ref, f32[1,256]{1,0:T(1,128)} %bitcast.6, bf16[256,256]{1,0:T(8,128)(2,1)} %wq_ref.2, bf16[256,256]{1,0:T(8,128)(2,1)} %wkt_ref.1, bf16[256,256]{1,0:T(8,128)(2,1)} %wvt_ref.1, ...), custom_call_target="tpu_custom_call" | custom-call | tf_op jit(solution)/shard_map/pallas_call | solution.py:254
  82.5 21.6 %shard_map.111 = bf16[32,64,256]{2,1,0:T(8,128)(2,1)} custom-call(bf16[256,8,256]{2,1,0:T(8,128)(2,1)} %bitcast.4, f32[1,256]{1,0:T(1,128)} %bitcast.7, bf16[256,256]{1,0:T(8,128)(2,1)} %wq_ref.3, bf16[256,256]{1,0:T(8,128)(2,1)} %wk_ref.1, bf16[256,256]{1,0:T(8,128)(2,1)} %wv_ref.1, bf16[256,256]{1,0:T(8,128)(2,1)} %w_ref.3), custom_call_target="tpu_custom_call" | custom-call | tf_op jit(solution)/shard_map/pallas_call | solution.py:359
  104.1 2.3 %copy.13 = bf16[32,64,256]{2,1,0:T(8,128)(2,1)} copy(bf16[32,64,256]{2,1,0:T(8,128)(2,1)} %shard_map.111) | data formatting | bytes 2097152

commit v14 on v12

--- a/solution.py
+++ b/solution.py
@@ -421,7 +421,7 @@
     got, zero = spatial_exchange(latents.reshape(n_pos, per, places, width), n_pos, n_frame, 1)
     got = spatial_attend(
         got, zero, gain_one, query_one, key_one, value_one, out_one,
-        min(256, n_pos * places), n_frame, n_pos, 2,
+        min(512, n_pos * places), n_frame, n_pos, 2,
     )
     all_places = n_pos * places
     run = all_places // (n_pos * n_frame)

time: 106 us -> 105 us (level)
    pallas_call x1, Pallas kernels: 50.4 us -> 48 us  [spatial_attend(): pl.pallas_call(kernel, out_shape=jax.ShapeDtypeStruct((n_dev, frames, run...]
    pallas_call x1, Pallas kernels: 19.5 us -> 21.2 us  [temporal_attend(): pl.pallas_call(kernel, out_shape=jax.ShapeDtypeStruct((n_frame, run, fram...]
where the time goes in v14:
time: 105 us; the launch traced here: 104 us
  Pallas kernels  101 us (96%)
  local copies, waits for them, and re-layouts  2.78 us (3%)
    pallas_call x1, Pallas kernels, spatial_attend(): pl.pallas_call(kernel, out_shape=jax.ShapeDtypeStruct((n_dev, frames, run...  48 us
    pallas_call x1, Pallas kernels, spatial_exchange(): pl.pallas_call(kernel, out_shape=(jax.ShapeDtypeStruct(x.shape, x.dtype),...  32.1 us
    pallas_call x1, Pallas kernels, temporal_attend(): pl.pallas_call(kernel, out_shape=jax.ShapeDtypeStruct((n_frame, run, fram...  21.2 us
    reshape x1, local copies, waits for them, and re-layouts, shards(): return got.transpose(2, 0, 1, 3).reshape(frames, places, width)  2.78 us

profile of v14, /device:TPU:1, one launch (start us, length us, event | category | flops | bytes accessed | tf_op | source)
XLA Modules:
  0.0 104.1 jit_solution(14047183235303503123)
XLA Ops:
  0.0 32.1 %shard_map.109 = (bf16[16,2,64,256]{3,2,1,0:T(8,128)(2,1)}, bf16[16,64,256]{2,1,0:T(8,128)(2,1)}) custom-call(bf16[16,2,64,256]{3,2,1,0:T(8,128)(2,1)} %bitcast.9), custom_call_target="tpu_custom_call" | custom-call | tf_op jit(solution)/shard_map/pallas_call | solution.py:129
  32.1 48.0 %shard_map.110 = bf16[128,2,8,256]{3,2,1,0:T(8,128)(2,1)} custom-call(bf16[16,2,64,256]{3,2,1,0:T(8,128)(2,1)} %get-tuple-element.7.x_ref, bf16[16,64,256]{2,1,0:T(8,128)(2,1)} %get-tuple-element.8.z_ref, f32[1,256]{1,0:T(1,128)} %bitcast.10, bf16[256,256]{1,0:T(8,128)(2,1)} %wq_ref.2, bf16[256,256]{1,0:T(8,128)(2,1)} %wkt_ref.1, bf16[256,256]{1,0:T(8,128)(2,1)} %wvt_ref.1, ...), custom_call_target="tpu_custom_call" | custom-call | tf_op jit(solution)/shard_map/pallas_call | solution.py:254
  80.1 21.2 %shard_map.111 = bf16[8,8,32,256]{3,2,1,0:T(8,128)(2,1)} custom-call(bf16[256,8,256]{2,1,0:T(8,128)(2,1)} %bitcast.7, f32[1,256]{1,0:T(1,128)} %bitcast.11, bf16[256,256]{1,0:T(8,128)(2,1)} %wq_ref.3, bf16[256,256]{1,0:T(8,128)(2,1)} %wk_ref.1, bf16[256,256]{1,0:T(8,128)(2,1)} %wv_ref.1, bf16[256,256]{1,0:T(8,128)(2,1)} %w_ref.3), custom_call_target="tpu_custom_call" | custom-call | tf_op jit(solution)/shard_map/pallas_call | solution.py:353
  101.3 2.8 %copy.12 = bf16[32,64,256]{2,1,0:T(8,128)(2,1)} copy(bf16[32,64,256]{2,0,1:T(8,128)(2,1)} %bitcast.8) | data formatting | bytes 2097152 | tf_op jit(solution)/shard_map/reshape | solution.py:430

commit v15 on v14

--- a/solution.py
+++ b/solution.py
@@ -327,21 +327,17 @@
             made[p] = acc.astype(made.dtype)
             if p == 0:
                 pl.semaphore_wait(barrier, n_frame - 1)
-            for g in range(n_frame):
-                @pl.when(g == fi)
-                def _():
-                    got[fi, p] = made[p, pl.ds(g * frames, frames)]
-
-                @pl.when(g != fi)
-                def _():
-                    pltpu.make_async_remote_copy(
-                        src_ref=made.at[p, pl.ds(g * frames, frames)],
-                        dst_ref=got.at[fi, p],
-                        send_sem=send_sem,
-                        recv_sem=recv_sem,
-                        device_id={"frame": g},
-                        device_id_type=MESH,
-                    ).start()
+            for k in range(1, n_frame):
+                g = (fi + k) % n_frame
+                pltpu.make_async_remote_copy(
+                    src_ref=made.at[p, pl.ds(pl.multiple_of(g * frames, frames), frames)],
+                    dst_ref=got.at[fi, p],
+                    send_sem=send_sem,
+                    recv_sem=recv_sem,
+                    device_id={"frame": g},
+                    device_id_type=MESH,
+                ).start()
+            got[fi, p] = made[p, pl.ds(pl.multiple_of(fi * frames, frames), frames)]
 
         others = pltpu.make_async_copy(got.at[pl.ds(0, n_frame - 1)], got.at[pl.ds(1, n_frame - 1)], recv_sem)
         others.wait()

time: 105 us -> 105 us (level)
  no operation moved by 1% of the time
where the time goes in v15:
time: 105 us; the launch traced here: 104 us
  Pallas kernels  101 us (96%)
  local copies, waits for them, and re-layouts  2.78 us (3%)
    pallas_call x1, Pallas kernels, spatial_attend(): pl.pallas_call(kernel, out_shape=jax.ShapeDtypeStruct((n_dev, frames, run...  48 us
    pallas_call x1, Pallas kernels, spatial_exchange(): pl.pallas_call(kernel, out_shape=(jax.ShapeDtypeStruct(x.shape, x.dtype),...  32.1 us
    pallas_call x1, Pallas kernels, temporal_attend(): pl.pallas_call(kernel, out_shape=jax.ShapeDtypeStruct((n_frame, run, fram...  21.4 us
    reshape x1, local copies, waits for them, and re-layouts, shards(): return got.transpose(2, 0, 1, 3).reshape(frames, places, width)  2.78 us

profile of v15, /device:TPU:1, one launch (start us, length us, event | category | flops | bytes accessed | tf_op | source)
XLA Modules:
  0.0 104.2 jit_solution(2119539987869920240)
XLA Ops:
  0.0 32.1 %shard_map.109 = (bf16[16,2,64,256]{3,2,1,0:T(8,128)(2,1)}, bf16[16,64,256]{2,1,0:T(8,128)(2,1)}) custom-call(bf16[16,2,64,256]{3,2,1,0:T(8,128)(2,1)} %bitcast.9), custom_call_target="tpu_custom_call" | custom-call | tf_op jit(solution)/shard_map/pallas_call | solution.py:129
  32.1 48.0 %shard_map.110 = bf16[128,2,8,256]{3,2,1,0:T(8,128)(2,1)} custom-call(bf16[16,2,64,256]{3,2,1,0:T(8,128)(2,1)} %get-tuple-element.7.x_ref, bf16[16,64,256]{2,1,0:T(8,128)(2,1)} %get-tuple-element.8.z_ref, f32[1,256]{1,0:T(1,128)} %bitcast.10, bf16[256,256]{1,0:T(8,128)(2,1)} %wq_ref.2, bf16[256,256]{1,0:T(8,128)(2,1)} %wkt_ref.1, bf16[256,256]{1,0:T(8,128)(2,1)} %wvt_ref.1, ...), custom_call_target="tpu_custom_call" | custom-call | tf_op jit(solution)/shard_map/pallas_call | solution.py:254
  80.1 21.4 %shard_map.111 = bf16[8,8,32,256]{3,2,1,0:T(8,128)(2,1)} custom-call(bf16[256,8,256]{2,1,0:T(8,128)(2,1)} %bitcast.7, f32[1,256]{1,0:T(1,128)} %bitcast.11, bf16[256,256]{1,0:T(8,128)(2,1)} %wq_ref.3, bf16[256,256]{1,0:T(8,128)(2,1)} %wk_ref.1, bf16[256,256]{1,0:T(8,128)(2,1)} %wv_ref.1, bf16[256,256]{1,0:T(8,128)(2,1)} %w_ref.3), custom_call_target="tpu_custom_call" | custom-call | tf_op jit(solution)/shard_map/pallas_call | solution.py:349
  101.5 2.8 %copy.12 = bf16[32,64,256]{2,1,0:T(8,128)(2,1)} copy(bf16[32,64,256]{2,0,1:T(8,128)(2,1)} %bitcast.8) | data formatting | bytes 2097152 | tf_op jit(solution)/shard_map/reshape | solution.py:426

commit v16 on v14

--- a/solution.py
+++ b/solution.py
@@ -159,7 +159,7 @@
     per_tile = rows // slab
 
     def kernel(x_ref, z_ref, g_ref, wq_ref, wkt_ref, wvt_ref, w_ref, o_ref,
-               q_ref, kt_ref, vt_ref, k0t_ref, v0t_ref, made, got, send_sem, recv_sem):
+               q_ref, kt_ref, vt_ref, made, got, send_sem, recv_sem):
         t = pl.program_id(0)
         fi = lax.axis_index("frame")
         pi = lax.axis_index("pos")
@@ -184,14 +184,16 @@
                 )
             wkt = wkt_ref[...].T
             wvt = wvt_ref[...].T
+            normed_zero = normed_rows(z_ref[...])
+            k_zero = channels_first(wkt, normed_zero)
+            v_zero = channels_first(wvt, normed_zero)
             for f in range(frames):
                 normed_one = normed_rows(x_ref[:, f])
                 q_ref[f] = jnp.dot(normed_one, wq_ref[...], preferred_element_type=jnp.float32).astype(jnp.bfloat16)
-                kt_ref[f] = channels_first(wkt, normed_one)
-                vt_ref[f] = channels_first(wvt, normed_one)
-            normed_zero = normed_rows(z_ref[...])
-            k0t_ref[...] = channels_first(wkt, normed_zero)
-            v0t_ref[...] = channels_first(wvt, normed_zero)
+                kt_ref[f, :, pl.ds(0, places)] = channels_first(wkt, normed_one)
+                vt_ref[f, :, pl.ds(0, places)] = channels_first(wvt, normed_one)
+                kt_ref[f, :, pl.ds(places, places)] = k_zero
+                vt_ref[f, :, pl.ds(places, places)] = v_zero
 
         tt = (t + fi + pi) % n_tiles
         base = tt * chunks
@@ -201,18 +203,11 @@
             for h in range(HEADS):
                 part = pl.ds(h * depth, depth)
                 qh = q_ref[f, these, part]
-                own = jnp.dot(qh, kt_ref[f, part, :], preferred_element_type=jnp.float32) * scale
-                first = jnp.dot(qh, k0t_ref[part, :], preferred_element_type=jnp.float32) * scale
-                high = jnp.maximum(
-                    jnp.max(own, axis=-1, keepdims=True), jnp.max(first, axis=-1, keepdims=True)
-                )
-                own = jnp.exp(own - high)
-                first = jnp.exp(first - high)
-                totals = jnp.sum(own, axis=-1, keepdims=True) + jnp.sum(first, axis=-1, keepdims=True)
+                scores = jnp.dot(qh, kt_ref[f, part, :], preferred_element_type=jnp.float32) * scale
+                weights = jnp.exp(scores - jnp.max(scores, axis=-1, keepdims=True))
+                totals = jnp.sum(weights, axis=-1, keepdims=True)
                 summed = lax.dot_general(
-                    own.astype(jnp.bfloat16), vt_ref[f, part, :], contract, preferred_element_type=jnp.float32
-                ) + lax.dot_general(
-                    first.astype(jnp.bfloat16), v0t_ref[part, :], contract, preferred_element_type=jnp.float32
+                    weights.astype(jnp.bfloat16), vt_ref[f, part, :], contract, preferred_element_type=jnp.float32
                 )
                 attended = (summed / totals).astype(jnp.bfloat16)
                 acc = acc + jnp.dot(attended, w_ref[part, :], preferred_element_type=jnp.float32)
@@ -267,10 +262,8 @@
         out_specs=pl.BlockSpec(memory_space=pltpu.VMEM),
         scratch_shapes=[
             pltpu.VMEM((frames, places, width), dtype),
-            pltpu.VMEM((frames, width, places), dtype),
-            pltpu.VMEM((frames, width, places), dtype),
-            pltpu.VMEM((width, places), dtype),
-            pltpu.VMEM((width, places), dtype),
+            pltpu.VMEM((frames, width, 2 * places), dtype),
+            pltpu.VMEM((frames, width, 2 * places), dtype),
             pltpu.VMEM((n_dev, frames, run, width), dtype),
             pltpu.VMEM((n_dev, frames, run, width), dtype),
             pltpu.SemaphoreType.DMA,

time: 105 us -> 105 us (level)
  no operation moved by 1% of the time
where the time goes in v16:
time: 105 us; the launch traced here: 103 us
  Pallas kernels  101 us (96%)
  local copies, waits for them, and re-layouts  2.78 us (3%)
    pallas_call x1, Pallas kernels, spatial_attend(): pl.pallas_call(kernel, out_shape=jax.ShapeDtypeStruct((n_dev, frames, run...  47.2 us
    pallas_call x1, Pallas kernels, spatial_exchange(): pl.pallas_call(kernel, out_shape=(jax.ShapeDtypeStruct(x.shape, x.dtype),...  32.1 us
    pallas_call x1, Pallas kernels, temporal_attend(): pl.pallas_call(kernel, out_shape=jax.ShapeDtypeStruct((n_frame, run, fram...  21.2 us
    reshape x1, local copies, waits for them, and re-layouts, shards(): return got.transpose(2, 0, 1, 3).reshape(frames, places, width)  2.78 us

profile of v16, /device:TPU:1, one launch (start us, length us, event | category | flops | bytes accessed | tf_op | source)
XLA Modules:
  0.0 103.3 jit_solution(439653053861435235)
XLA Ops:
  0.0 32.1 %shard_map.109 = (bf16[16,2,64,256]{3,2,1,0:T(8,128)(2,1)}, bf16[16,64,256]{2,1,0:T(8,128)(2,1)}) custom-call(bf16[16,2,64,256]{3,2,1,0:T(8,128)(2,1)} %bitcast.9), custom_call_target="tpu_custom_call" | custom-call | tf_op jit(solution)/shard_map/pallas_call | solution.py:129
  32.1 47.2 %shard_map.110 = bf16[128,2,8,256]{3,2,1,0:T(8,128)(2,1)} custom-call(bf16[16,2,64,256]{3,2,1,0:T(8,128)(2,1)} %get-tuple-element.7.x_ref, bf16[16,64,256]{2,1,0:T(8,128)(2,1)} %get-tuple-element.8.z_ref, f32[1,256]{1,0:T(1,128)} %bitcast.10, bf16[256,256]{1,0:T(8,128)(2,1)} %wq_ref.2, bf16[256,256]{1,0:T(8,128)(2,1)} %wkt_ref.1, bf16[256,256]{1,0:T(8,128)(2,1)} %wvt_ref.1, ...), custom_call_target="tpu_custom_call" | custom-call | tf_op jit(solution)/shard_map/pallas_call | solution.py:249
  79.3 21.2 %shard_map.111 = bf16[8,8,32,256]{3,2,1,0:T(8,128)(2,1)} custom-call(bf16[256,8,256]{2,1,0:T(8,128)(2,1)} %bitcast.7, f32[1,256]{1,0:T(1,128)} %bitcast.11, bf16[256,256]{1,0:T(8,128)(2,1)} %wq_ref.3, bf16[256,256]{1,0:T(8,128)(2,1)} %wk_ref.1, bf16[256,256]{1,0:T(8,128)(2,1)} %wv_ref.1, bf16[256,256]{1,0:T(8,128)(2,1)} %w_ref.3), custom_call_target="tpu_custom_call" | custom-call | tf_op jit(solution)/shard_map/pallas_call | solution.py:346
  100.6 2.8 %copy.12 = bf16[32,64,256]{2,1,0:T(8,128)(2,1)} copy(bf16[32,64,256]{2,0,1:T(8,128)(2,1)} %bitcast.8) | data formatting | bytes 2097152 | tf_op jit(solution)/shard_map/reshape | solution.py:423

commit v17 on v16

--- a/solution.py
+++ b/solution.py
@@ -75,10 +75,25 @@
                 device_id_type=MESH,
             )
 
+        def forward(k):
+            return pltpu.make_async_remote_copy(
+                src_ref=z_ref.at[pi],
+                dst_ref=z_ref.at[pi],
+                send_sem=zsend_sem.at[k],
+                recv_sem=zrecv_sem.at[k],
+                device_id={"pos": (pi + k) % n_pos},
+                device_id_type=MESH,
+            )
+
         @pl.when(fi == 0)
         def _():
             for g in range(1, n_frame):
                 spread(g).start()
+            local = pltpu.make_async_copy(x_ref.at[0, 0], z_ref.at[pi], local_sem)
+            local.start()
+            local.wait()
+            for k in range(1, n_pos):
+                forward(k).start()
 
         copies = []
         for k in range(1, n_pos):
@@ -94,28 +109,13 @@
             copy.start()
             copies.append(copy)
 
-        @pl.when(fi == 0)
-        def _():
-            local = pltpu.make_async_copy(x_ref.at[0, 0], z_ref.at[pi], local_sem)
-            local.start()
-            local.wait()
-
         @pl.when(fi != 0)
         def _():
             spread(1).wait_recv()
-
-        for k in range(1, n_pos):
-            peer = (pi + k) % n_pos
-            copy = pltpu.make_async_remote_copy(
-                src_ref=z_ref.at[pi],
-                dst_ref=z_ref.at[pi],
-                send_sem=zsend_sem.at[k],
-                recv_sem=zrecv_sem.at[k],
-                device_id={"pos": peer},
-                device_id_type=MESH,
-            )
-            copy.start()
-            copies.append(copy)
+            for k in range(1, n_pos):
+                forward(k).start()
+
+        copies += [forward(k) for k in range(1, n_pos)]
 
         @pl.when(fi == 0)
         def _():

time: 105 us -> 104 us (level)
  no operation moved by 1% of the time
where the time goes in v17:
time: 104 us; the launch traced here: 103 us
  Pallas kernels  101 us (97%)
  local copies, waits for them, and re-layouts  2.78 us (3%)
    pallas_call x1, Pallas kernels, spatial_attend(): pl.pallas_call(kernel, out_shape=jax.ShapeDtypeStruct((n_dev, frames, run...  48.2 us
    pallas_call x1, Pallas kernels, spatial_exchange(): pl.pallas_call(kernel, out_shape=(jax.ShapeDtypeStruct(x.shape, x.dtype),...  31.2 us
    pallas_call x1, Pallas kernels, temporal_attend(): pl.pallas_call(kernel, out_shape=jax.ShapeDtypeStruct((n_frame, run, fram...  21.2 us
    reshape x1, local copies, waits for them, and re-layouts, shards(): return got.transpose(2, 0, 1, 3).reshape(frames, places, width)  2.78 us

profile of v17, /device:TPU:1, one launch (start us, length us, event | category | flops | bytes accessed | tf_op | source)
XLA Modules:
  0.0 103.3 jit_solution(17318960477903914031)
XLA Ops:
  0.0 31.2 %shard_map.109 = (bf16[16,2,64,256]{3,2,1,0:T(8,128)(2,1)}, bf16[16,64,256]{2,1,0:T(8,128)(2,1)}) custom-call(bf16[16,2,64,256]{3,2,1,0:T(8,128)(2,1)} %bitcast.9), custom_call_target="tpu_custom_call" | custom-call | tf_op jit(solution)/shard_map/pallas_call | solution.py:129
  31.2 48.2 %shard_map.110 = bf16[128,2,8,256]{3,2,1,0:T(8,128)(2,1)} custom-call(bf16[16,2,64,256]{3,2,1,0:T(8,128)(2,1)} %get-tuple-element.7.x_ref, bf16[16,64,256]{2,1,0:T(8,128)(2,1)} %get-tuple-element.8.z_ref, f32[1,256]{1,0:T(1,128)} %bitcast.10, bf16[256,256]{1,0:T(8,128)(2,1)} %wq_ref.2, bf16[256,256]{1,0:T(8,128)(2,1)} %wkt_ref.1, bf16[256,256]{1,0:T(8,128)(2,1)} %wvt_ref.1, ...), custom_call_target="tpu_custom_call" | custom-call | tf_op jit(solution)/shard_map/pallas_call | solution.py:249
  79.3 21.2 %shard_map.111 = bf16[8,8,32,256]{3,2,1,0:T(8,128)(2,1)} custom-call(bf16[256,8,256]{2,1,0:T(8,128)(2,1)} %bitcast.7, f32[1,256]{1,0:T(1,128)} %bitcast.11, bf16[256,256]{1,0:T(8,128)(2,1)} %wq_ref.3, bf16[256,256]{1,0:T(8,128)(2,1)} %wk_ref.1, bf16[256,256]{1,0:T(8,128)(2,1)} %wv_ref.1, bf16[256,256]{1,0:T(8,128)(2,1)} %w_ref.3), custom_call_target="tpu_custom_call" | custom-call | tf_op jit(solution)/shard_map/pallas_call | solution.py:346
  100.6 2.8 %copy.12 = bf16[32,64,256]{2,1,0:T(8,128)(2,1)} copy(bf16[32,64,256]{2,0,1:T(8,128)(2,1)} %bitcast.8) | data formatting | bytes 2097152 | tf_op jit(solution)/shard_map/reshape | solution.py:423

commit v18 on v16

--- a/solution.py
+++ b/solution.py
@@ -414,7 +414,7 @@
     got, zero = spatial_exchange(latents.reshape(n_pos, per, places, width), n_pos, n_frame, 1)
     got = spatial_attend(
         got, zero, gain_one, query_one, key_one, value_one, out_one,
-        min(512, n_pos * places), n_frame, n_pos, 2,
+        min(256, n_pos * places), n_frame, n_pos, 2,
     )
     all_places = n_pos * places
     run = all_places // (n_pos * n_frame)

time: 105 us -> 105 us (level)
    pallas_call x1, Pallas kernels: 47.2 us -> 49.7 us  [spatial_attend(): pl.pallas_call(kernel, out_shape=jax.ShapeDtypeStruct((n_dev, frames, run...]
    pallas_call x1, Pallas kernels: 21.2 us -> 19.5 us  [temporal_attend(): pl.pallas_call(kernel, out_shape=jax.ShapeDtypeStruct((n_frame, run, fram...]
where the time goes in v18:
time: 105 us; the launch traced here: 104 us
  Pallas kernels  101 us (96%)
  local copies, waits for them, and re-layouts  2.78 us (3%)
    pallas_call x1, Pallas kernels, spatial_attend(): pl.pallas_call(kernel, out_shape=jax.ShapeDtypeStruct((n_dev, frames, run...  49.7 us
    pallas_call x1, Pallas kernels, spatial_exchange(): pl.pallas_call(kernel, out_shape=(jax.ShapeDtypeStruct(x.shape, x.dtype),...  32.1 us
    pallas_call x1, Pallas kernels, temporal_attend(): pl.pallas_call(kernel, out_shape=jax.ShapeDtypeStruct((n_frame, run, fram...  19.5 us
    reshape x1, local copies, waits for them, and re-layouts, shards(): return got.transpose(2, 0, 1, 3).reshape(frames, places, width)  2.78 us

profile of v18, /device:TPU:1, one launch (start us, length us, event | category | flops | bytes accessed | tf_op | source)
XLA Modules:
  0.0 104.2 jit_solution(204550404492339547)
XLA Ops:
  0.0 32.1 %shard_map.109 = (bf16[16,2,64,256]{3,2,1,0:T(8,128)(2,1)}, bf16[16,64,256]{2,1,0:T(8,128)(2,1)}) custom-call(bf16[16,2,64,256]{3,2,1,0:T(8,128)(2,1)} %bitcast.9), custom_call_target="tpu_custom_call" | custom-call | tf_op jit(solution)/shard_map/pallas_call | solution.py:129
  32.1 49.7 %shard_map.110 = bf16[128,2,8,256]{3,2,1,0:T(8,128)(2,1)} custom-call(bf16[16,2,64,256]{3,2,1,0:T(8,128)(2,1)} %get-tuple-element.7.x_ref, bf16[16,64,256]{2,1,0:T(8,128)(2,1)} %get-tuple-element.8.z_ref, f32[1,256]{1,0:T(1,128)} %bitcast.10, bf16[256,256]{1,0:T(8,128)(2,1)} %wq_ref.2, bf16[256,256]{1,0:T(8,128)(2,1)} %wkt_ref.1, bf16[256,256]{1,0:T(8,128)(2,1)} %wvt_ref.1, ...), custom_call_target="tpu_custom_call" | custom-call | tf_op jit(solution)/shard_map/pallas_call | solution.py:249
  81.9 19.5 %shard_map.111 = bf16[8,8,32,256]{3,2,1,0:T(8,128)(2,1)} custom-call(bf16[256,8,256]{2,1,0:T(8,128)(2,1)} %bitcast.7, f32[1,256]{1,0:T(1,128)} %bitcast.11, bf16[256,256]{1,0:T(8,128)(2,1)} %wq_ref.3, bf16[256,256]{1,0:T(8,128)(2,1)} %wk_ref.1, bf16[256,256]{1,0:T(8,128)(2,1)} %wv_ref.1, bf16[256,256]{1,0:T(8,128)(2,1)} %w_ref.3), custom_call_target="tpu_custom_call" | custom-call | tf_op jit(solution)/shard_map/pallas_call | solution.py:346
  101.4 2.8 %copy.12 = bf16[32,64,256]{2,1,0:T(8,128)(2,1)} copy(bf16[32,64,256]{2,0,1:T(8,128)(2,1)} %bitcast.8) | data formatting | bytes 2097152 | tf_op jit(solution)/shard_map/reshape | solution.py:423
